TPU v7x, 1024 devices: a whole 4x4x32 slice. The times are simulated.
1024 devices in a mesh: sfc: 128 (over y, z), sub: 8 (over x, core).
Axes of the slice: x: 4, y: 4, z: 32, core: 2. Of those that a mesh axis runs over, the one named last changes fastest.
Arguments:
- right_side: float32 [8, 8, 8, 128, 16, 128], P(None, None, None, 'sfc', 'sub'), may hold values from -7 to 7
- coefficient: float32 [128, 16, 128], P('sfc', 'sub'), may hold values from 0.3 to 3
- stiffness: float32 [8, 8], replicated, may hold values from -0.3 to 3.5, as said below
Outputs:
- solution: float32 [8, 8, 8, 128, 16, 128], P(None, None, None, 'sfc', 'sub')
Inputs may be any that keep to these rules, and one draw needn't show every extreme that they name: `stiffness`: symmetric.
All inputs are finite; a program needn't handle non-finite values.
Results may differ from a plain program's by a relative error of at most 0.0002.
Values sent between devices are 32-bit elements; how exact they have to be, the bound alone decides.
No kernel may reach another device: no remote copies, remote signals or barrier semaphores. Data moves between devices by JAX's collectives and lax.ppermute only.
A program may use at most 32 MiB of HBM per device.

v0:
```python
import jax
import jax.numpy as jnp
from jax import lax
from jax.sharding import PartitionSpec as P

penalty = 4.0
shift_mass = 0.02
cheb_centre = 1.25
cheb_half = 0.95
exact = lax.Precision.HIGHEST


def with_halo(block, sides, width, periodic):
    for axis, dim in sides:
        count = lax.axis_size(axis)
        forward = [(i, i + 1) for i in range(count - 1)]
        if periodic:
            forward.append((count - 1, 0))
        backward = [(target, source) for source, target in forward]
        low = lax.ppermute(
            lax.slice_in_dim(block, block.shape[dim] - width, None, axis=dim), axis, forward
        )
        high = lax.ppermute(lax.slice_in_dim(block, 0, width, axis=dim), axis, backward)
        block = jnp.concatenate([low, block, high], axis=dim)
    return block


def entering(value, axis, join, neutral, backward):
    count, mine = (lax.axis_size(axis), lax.axis_index(axis))
    pieces = jax.tree.map(lambda part: lax.all_gather(part, axis), value)
    if backward:
        pieces = jax.tree.map(lambda part: part[::-1], pieces)
        mine = count - 1 - mine
    running = jax.tree.map(
        lambda part, zero: jnp.full_like(part, 0) + jnp.asarray(zero, part.dtype), value, neutral
    )

    def lap(position, running):
        longer = join(running, jax.tree.map(lambda part: part[position], pieces))
        return jax.tree.map(lambda new, old: jnp.where(position < mine, new, old), longer, running)

    return lax.fori_loop(0, count - 1, lap, running)


def stiff_part(nodal_field, stiffness, coefficient):
    along_first = jnp.einsum("ia,abcpqr->ibcpqr", stiffness, nodal_field, precision=exact)
    along_second = jnp.einsum("jb,abcpqr->ajcpqr", stiffness, nodal_field, precision=exact)
    along_third = jnp.einsum("kc,abcpqr->abkpqr", stiffness, nodal_field, precision=exact)
    return coefficient * (along_first + along_second + along_third)


def face_terms(lower_face, upper_face, coefficient, prev_upper, prev_coef, next_lower, next_coef):
    upper_term = penalty * 0.5 * (coefficient + next_coef) * (upper_face - next_lower)
    lower_term = penalty * 0.5 * (coefficient + prev_coef) * (lower_face - prev_upper)
    return (lower_term, upper_term)


def add_faces(result, lower_term, upper_term, node_axis):
    leading = (slice(None),) * node_axis
    return result.at[leading + (0,)].add(lower_term).at[leading + (-1,)].add(upper_term)


def apply_with_edges(nodal_field, stiffness, coefficient):
    nodes = nodal_field.shape[0]
    side = nodes * nodes
    span_z, span_y, span_x = coefficient.shape
    result = stiff_part(nodal_field, stiffness, coefficient)
    lower_face = nodal_field[:, :, 0]
    upper_face = nodal_field[:, :, -1]
    terms = face_terms(
        lower_face,
        upper_face,
        coefficient,
        jnp.roll(upper_face, 1, 4),
        jnp.roll(coefficient, 1, 2),
        jnp.roll(lower_face, -1, 4),
        jnp.roll(coefficient, -1, 2),
    )
    result = add_faces(result, terms[0], terms[1], 2)
    lower_face = nodal_field[0]
    upper_face = nodal_field[-1]
    first_row = jnp.concatenate(
        [lower_face[:, :, 0].reshape(side, span_y, span_x), coefficient[0][None]], 0
    )
    last_row = jnp.concatenate(
        [upper_face[:, :, -1].reshape(side, span_y, span_x), coefficient[-1][None]], 0
    )
    padded = with_halo(jnp.stack([first_row, last_row], 1), (("sfc", 1),), 1, False)
    beneath = padded[:, 0]
    overhead = padded[:, 3]
    below_coef = beneath[side]
    above_coef = overhead[side]
    prev_upper = jnp.concatenate(
        [beneath[:side].reshape(nodes, nodes, span_y, span_x)[:, :, None], upper_face[:, :, :-1]], 2
    )
    prev_coef = jnp.concatenate([below_coef[None], coefficient[:-1]], 0)
    next_lower = jnp.concatenate(
        [lower_face[:, :, 1:], overhead[:side].reshape(nodes, nodes, span_y, span_x)[:, :, None]], 2
    )
    next_coef = jnp.concatenate([coefficient[1:], above_coef[None]], 0)
    terms = face_terms(
        lower_face, upper_face, coefficient, prev_upper, prev_coef, next_lower, next_coef
    )
    result = add_faces(result, terms[0], terms[1], 0)
    lower_face = nodal_field[:, 0]
    upper_face = nodal_field[:, -1]
    first_row = jnp.concatenate(
        [lower_face[:, :, :, 0].reshape(side, span_z, span_x), coefficient[:, 0][None]], 0
    )
    last_row = jnp.concatenate(
        [upper_face[:, :, :, -1].reshape(side, span_z, span_x), coefficient[:, -1][None]], 0
    )
    padded = with_halo(jnp.stack([first_row, last_row], 1), (("sub", 1),), 1, True)
    beneath = padded[:, 0]
    overhead = padded[:, 3]
    prev_upper = jnp.concatenate(
        [
            beneath[:side].reshape(nodes, nodes, span_z, span_x)[:, :, :, None],
            upper_face[:, :, :, :-1],
        ],
        3,
    )
    prev_coef = jnp.concatenate([beneath[side][:, None], coefficient[:, :-1]], 1)
    next_lower = jnp.concatenate(
        [
            lower_face[:, :, :, 1:],
            overhead[:side].reshape(nodes, nodes, span_z, span_x)[:, :, :, None],
        ],
        3,
    )
    next_coef = jnp.concatenate([coefficient[:, 1:], overhead[side][:, None]], 1)
    terms = face_terms(
        lower_face, upper_face, coefficient, prev_upper, prev_coef, next_lower, next_coef
    )
    return (add_faces(result, terms[0], terms[1], 1), below_coef, above_coef)


def apply_operator(nodal_field, stiffness, coefficient):
    return apply_with_edges(nodal_field, stiffness, coefficient)[0]


def inverse_diagonal(stiffness, coefficient):
    count = stiffness.shape[0]
    ladder = jnp.arange(count)
    edges = ((ladder == 0) | (ladder == count - 1)).astype(stiffness.dtype)
    main = jnp.diagonal(stiffness) + penalty * 0.5 * edges
    total = main[:, None, None] + main[None, :, None] + main[None, None, :]
    return 1.0 / (total[:, :, :, None, None, None] * coefficient)


def second_step(right_side, iterate, previous_step, inverse, stiffness, coefficient):
    residual = right_side - apply_operator(iterate, stiffness, coefficient)
    rho_first = cheb_half / cheb_centre
    rho_second = 1.0 / (2.0 * cheb_centre / cheb_half - rho_first)
    update = rho_second * rho_first * previous_step + 2.0 * rho_second / cheb_half * (
        residual * inverse
    )
    return iterate + update


def combine_maps(earlier, later):
    product = jnp.einsum("...ij,...jk->...ik", later, earlier, precision=exact)
    return product / jnp.max(jnp.abs(product), axis=(-2, -1), keepdims=True)


def compose_back(higher, lower):
    return (lower[0] + lower[1] * higher[0], lower[1] * higher[1])


def elimination_matrix(gain, diag_term, upper_term, mean_term):
    zeros = jnp.zeros_like(gain)
    ones = jnp.ones_like(gain)
    first_line = jnp.stack(
        [penalty * gain, zeros, upper_term * upper_term - penalty * gain * diag_term], -1
    )
    second_line = jnp.stack([zeros, -upper_term, upper_term * mean_term], -1)
    third_line = jnp.stack([-ones, zeros, diag_term], -1)
    return jnp.stack([first_line, second_line, third_line], -2)


def per_device(right_side, coefficient, stiffness):
    inverse = inverse_diagonal(stiffness, coefficient)
    first_step = right_side * inverse / cheb_centre
    iterate = second_step(right_side, first_step, first_step, inverse, stiffness, coefficient)
    image, below_coef, above_coef = apply_with_edges(iterate, stiffness, coefficient)
    residual = right_side - image
    nodes = right_side.shape[0]
    local_rows, local_span, stream_count = coefficient.shape
    residual_sums, coef_sums = lax.psum(
        (jnp.sum(residual, axis=(0, 1, 2, 4, 5)), jnp.sum(coefficient, axis=(1, 2))), "sub"
    )
    plane_count = local_span * lax.axis_size("sub") * stream_count
    plane_mean = residual_sums / (plane_count * nodes * nodes * nodes)
    plane_coef = coef_sums / plane_count
    position = lax.axis_index("sfc")
    identity = jnp.eye(3, dtype=jnp.float32)
    is_bottom = (position == 0).astype(jnp.float32)
    not_top = (position < lax.axis_size("sfc") - 1).astype(jnp.float32)
    device_map = identity
    row = 0
    gain = plane_coef[row]
    diag_term = (penalty + shift_mass) * gain
    diag_term = diag_term + penalty * gain * is_bottom
    upper_term = -penalty * gain
    upper_term = upper_term * not_top
    diag_terms = [diag_term]
    upper_terms = [upper_term]
    device_map = combine_maps(
        device_map, elimination_matrix(gain, diag_term, upper_term, plane_mean[row])
    )
    below_map = entering(device_map, "sfc", combine_maps, identity, False)
    state = below_map[:, 2]
    carried_rho = state[0] / state[2]
    carried_delta = state[1] / state[2]
    row = 0
    denom = diag_terms[row] - carried_rho
    slope = upper_terms[row] / denom
    offset = (plane_mean[row] - carried_delta) / denom
    slopes = [slope]
    offsets = [offset]
    alpha_part = jnp.float32(0.0)
    beta_part = jnp.float32(1.0)
    for row in reversed(range(local_rows)):
        alpha_part, beta_part = (offsets[row] - slopes[row] * alpha_part, -slopes[row] * beta_part)
    above_map = entering(
        (alpha_part, beta_part), "sfc", compose_back, (jnp.float32(0.0), jnp.float32(1.0)), True
    )
    next_value = above_map[0]
    values = [None] * local_rows
    for row in reversed(range(local_rows)):
        next_value = offsets[row] - slopes[row] * next_value
        values[row] = next_value
    correction = jnp.stack(values)
    iterate = iterate + correction[None, None, None, :, None, None]
    residual = right_side - apply_operator(iterate, stiffness, coefficient)
    post_step = residual * inverse / cheb_centre
    iterate = iterate + post_step
    return second_step(right_side, iterate, post_step, inverse, stiffness, coefficient)


def solution(mesh):
    in_specs = (P(None, None, None, "sfc", "sub", None), P("sfc", "sub", None), P())
    out_specs = P(None, None, None, "sfc", "sub", None)
    return jax.shard_map(
        per_device, mesh=mesh, in_specs=in_specs, out_specs=out_specs, check_vma=False
    )
```

profile of v0, /device:TPU:1, one launch (start us, length us, event | category | flops | bytes accessed | tf_op | source)
XLA Modules:
  0.0 1114.8 jit_solution(2883489745261337937)
XLA Ops:
  2.6 4.4 collective-permute-start
  7.1 2.1 collective-permute-start.2
  9.2 9.1 collective-permute-start.3
  19.0 0.9 fusion.30
  20.1 1.4 fusion.6
  23.0 1.3 dynamic-slice.192
  24.8 1.3 collective-permute-start.1
  26.1 1.3 scatter-add.84
  27.4 2.4 collective-permute-done.1
  30.0 1.3 scatter-add.85
  32.5 0.9 fusion.26
  34.4 1.7 collective-permute-start.4
  36.1 1.1 fusion.9
  37.4 3.4 collective-permute-done.6
  41.0 1.3 collective-permute-start.5
  42.4 1.3 scatter-add.94
  43.7 2.4 collective-permute-done.5
  46.2 1.3 scatter-add.95
  47.6 5.0 collective-permute-start.7
  52.7 0.9 collective-permute-done.7
  53.6 1.0 subtract_reduce_fusion
  54.6 13.4 %all-reduce.3 = (f32[1]{0:T(128)}, f32[1]{0:T(128)}) all-reduce(f32[1]{0:T(128)} %bitcast.108, f32[1]{0:T(128)} %bitcast.110), channel_id=1, replica_groups=mesh['sfc'=128,'sub'=8] {'sub'}, use_global_device_ids=true, to_apply=%region_1.2 | all-reduce | flops 2 | bytes 16 | tf_op jit(solution)/shard_map/psum | solution.py:189
  72.0 153.0 %all-gather.1 = f32[128,3,3]{2,1,0:T(4,128)S(1)} all-gather(f32[1,3,3]{2,1,0:T(4,128)S(1)} %divide_bitcast_fusion), channel_id=2, replica_groups=mesh['sfc'=128,'sub'=8] {'sfc'}, dimensions={0}, use_global_device_ids=true | all-gather | bytes 4644 | tf_op jit(solution)/shard_map/all_gather | solution.py:30
  225.0 190.4 %while.50 = (s32[]{:T(128)}, f32[3,3]{1,0:T(4,128)S(1)}, s32[]{:T(128)}, f32[128,3,3]{2,1,0:T(4,128)S(1)}, s32[]{:T(128)}) while((s32[]{:T(128)}, f32[3,3]{1,0:T(4,128)S(1)}, s32[]{:T(128)}, f32[128,3,3]{2,1,0:T(4,128)S(1)}, s32[]{:T(128)}) %tuple.189), condition=%wide.region_7.8_spmd, body=%wide.region_5.7_spmd.sunk | while | flops 362 | bytes 4323 | solution.py:42
  225.0 0.8 abs_reduce_fusion.3
  228.0 0.8 abs_reduce_fusion.3
  232.5 0.8 abs_reduce_fusion.3
  237.0 0.8 abs_reduce_fusion.3
  241.5 0.8 abs_reduce_fusion.3
  246.0 0.8 abs_reduce_fusion.3
  252.0 0.8 abs_reduce_fusion.3
  256.5 0.8 abs_reduce_fusion.3
  261.0 0.8 abs_reduce_fusion.3
  265.5 0.8 abs_reduce_fusion.3
  270.0 0.8 abs_reduce_fusion.3
  274.5 0.8 abs_reduce_fusion.3
  280.5 0.8 abs_reduce_fusion.3
  285.0 0.8 abs_reduce_fusion.3
  289.5 0.8 abs_reduce_fusion.3
  294.0 0.8 abs_reduce_fusion.3
  298.5 0.8 abs_reduce_fusion.3
  420.3 221.8 %all-reduce.2 = (f32[128]{0:T(128)S(1)}, f32[128]{0:T(128)S(1)}) all-reduce(f32[128]{0:T(128)S(1)} %dynamic-update-slice.72, f32[128]{0:T(128)S(1)} %dynamic-update-slice.73), channel_id=1, replica_groups=mesh['sfc'=128,'sub'=8] {'sfc'}, use_global_device_ids=true, to_apply=%add | all-reduce | flops 256 | bytes 2048
  642.3 320.3 %while.51 = (s32[]{:T(128)}, f32[]{:T(128)}, s32[]{:T(128)}, f32[128]{0:T(128)S(1)}, f32[128]{0:T(128)S(1)}, /*index=5*/s32[]{:T(128)}) while((s32[]{:T(128)}, f32[]{:T(128)}, s32[]{:T(128)}, f32[128]{0:T(128)S(1)}, f32[128]{0:T(128)S(1)}, /*index=5*/s32[]{:T(128)}) %tuple.192), condition=%wide.region_9.10_spmd, body=%wide.region_8.9_spmd.sunk | while | flops 6 | bytes 139 | solution.py:42
  963.4 0.9 fusion.22
  965.3 1.3 collective-permute-start.8
  966.7 110.9 %collective-permute-start.10 = (f32[65,1,1,128]{3,0,2,1:T(8,128)S(1)}, f32[65,1,1,128]{3,0,2,1:T(8,128)S(1)}, u32[]{:S(2)}, u32[]{:S(2)}) collective-permute-start(f32[65,1,1,128]{3,0,2,1:T(8,128)S(1)} %fusion.84), channel_id=1, source_target_pairs={{0,1},{1,2},{2,3},{3,4},{4,5},{5,6},{6,7},{7,0},{8,9},{9,10},{10,1... | collective-permute-start | bytes 99848 | tf_op jit(solution)/shard_map/ppermute | solution.py:20
  1077.6 1.1 fusion.12
  1080.4 1.3 collective-permute-start.9
  1081.7 1.3 scatter-add.104
  1083.0 2.4 collective-permute-done.9
  1085.6 1.3 scatter-add.105
  1087.0 5.0 collective-permute-start.11
  1092.0 0.9 collective-permute-done.11
  1094.0 0.9 fusion.18
  1095.4 1.1 fusion.15
  1097.1 1.6 collective-permute-start.12
  1099.5 1.0 collective-permute-done.14
  1100.8 1.3 collective-permute-start.13
  1102.1 1.3 scatter-add.114
  1103.4 2.4 collective-permute-done.13
  1105.9 1.3 scatter-add.115
  1107.3 5.0 collective-permute-start.15
  1112.4 0.9 collective-permute-done.15
  1113.7 1.1 copy.321
  (705 shorter events, 349.3 us)
Async XLA Ops:
  0.0 0.7 copy-start
  0.0 1.5 copy-start.1
  1.5 0.7 copy-start.2
  2.6 21.7 %collective-permute-start = (f32[65,1,2,128]{3,2,1,0:T(2,128)S(1)}, f32[65,1,2,128]{3,2,1,0:T(2,128)S(1)}, u32[]{:S(2)}, u32[]{:S(2)}) collective-permute-start(f32[65,1,2,128]{3,2,1,0:T(2,128)S(1)} %fusion.33), channel_id=1, source_target_pairs={{0,8},{8,16},{16,24},{24,32},{32,40},{40,48},{48,56},{56,64},{64,7... | collective-permute-start | bytes 199688 | tf_op jit(solution)/shard_map/ppermute | solution.py:20
  7.1 17.2 %collective-permute-start.2 = (f32[65,1,1,128]{3,0,2,1:T(8,128)S(1)}, f32[65,1,1,128]{3,0,2,1:T(8,128)S(1)}, u32[]{:S(2)}, u32[]{:S(2)}) collective-permute-start(f32[65,1,1,128]{3,0,2,1:T(8,128)S(1)} %fusion.82), channel_id=1, source_target_pairs={{0,1},{1,2},{2,3},{3,4},{4,5},{5,6},{6,7},{7,0},{8,9},{9,10},{10,1... | collective-permute-start | bytes 99848 | tf_op jit(solution)/shard_map/ppermute | solution.py:20
  9.2 15.1 %collective-permute-start.3 = (f32[65,1,1,128]{3,0,2,1:T(8,128)S(1)}, f32[65,1,1,128]{3,0,2,1:T(8,128)S(1)}, u32[]{:S(2)}, u32[]{:S(2)}) collective-permute-start(f32[65,1,1,128]{3,0,2,1:T(8,128)S(1)} %fusion.78), channel_id=1, source_target_pairs={{1,0},{2,1},{3,2},{4,3},{5,4},{6,5},{7,6},{0,7},{9,8},{10,9},{11,1... | collective-permute-start | bytes 99848 | tf_op jit(solution)/shard_map/ppermute | solution.py:23
  24.4 12.8 %copy-start.6 = (f32[1,2,128]{2,0,1:T(1,128)}, f32[1,2,128]{2,0,1:T(1,128)S(1)}, u32[]{:S(2)}) copy-start(f32[1,2,128]{2,0,1:T(1,128)S(1)} %get-tuple-element.557) | copy-start | bytes 3076
  24.4 12.9 %copy-start.3 = (f32[1,2,128]{2,0,1:T(1,128)}, f32[1,2,128]{2,0,1:T(1,128)S(1)}, u32[]{:S(2)}) copy-start(f32[1,2,128]{2,0,1:T(1,128)S(1)} %get-tuple-element.556) | copy-start | bytes 3076
  24.8 5.0 collective-permute-start.1
  34.4 6.4 collective-permute-start.4
  36.1 4.7 collective-permute-start.6
  41.0 5.0 collective-permute-start.5
  47.6 5.9 collective-permute-start.7
  965.3 114.9 %collective-permute-start.8 = (f32[65,1,2,128]{3,2,1,0:T(2,128)S(1)}, f32[65,1,2,128]{3,2,1,0:T(2,128)S(1)}, u32[]{:S(2)}, u32[]{:S(2)}) collective-permute-start(f32[65,1,2,128]{3,2,1,0:T(2,128)S(1)} %fusion.37), channel_id=1, source_target_pairs={{0,8},{8,16},{16,24},{24,32},{32,40},{40,48},{48,56},{56,64},{64,7... | collective-permute-start | bytes 199688 | tf_op jit(solution)/shard_map/ppermute | solution.py:20
  966.7 112.0 %copy-start.7 = (f32[1,2,128]{2,0,1:T(1,128)S(1)}, f32[1,2,128]{2,0,1:T(1,128)}, u32[]{:S(2)}) copy-start(f32[1,2,128]{2,0,1:T(1,128)} %copy-done.6) | copy-start | bytes 3076
  966.7 113.5 %collective-permute-start.10 = (f32[65,1,1,128]{3,0,2,1:T(8,128)S(1)}, f32[65,1,1,128]{3,0,2,1:T(8,128)S(1)}, u32[]{:S(2)}, u32[]{:S(2)}) collective-permute-start(f32[65,1,1,128]{3,0,2,1:T(8,128)S(1)} %fusion.84), channel_id=1, source_target_pairs={{0,1},{1,2},{2,3},{3,4},{4,5},{5,6},{6,7},{7,0},{8,9},{9,10},{10,1... | collective-permute-start | bytes 99848 | tf_op jit(solution)/shard_map/ppermute | solution.py:20
  1078.7 0.7 copy-start.4
  1080.4 5.0 collective-permute-start.9
  1087.0 5.9 collective-permute-start.11
  1095.4 1.1 copy-start.8
  1097.1 3.5 collective-permute-start.12
  1098.8 0.7 copy-start.5
  1098.8 1.8 collective-permute-start.14
  1100.8 5.0 collective-permute-start.13
  1107.3 5.9 collective-permute-start.15
where the time goes:
time: 1120 us; the launch traced here: 1110 us
  blocking collectives  388 us (35%)
  local copies, waits for them, and re-layouts  178 us (16%)
  loops' own time  168 us (15%)
  starting transfers between devices  151 us (13%)
  matrix products  113 us (10%)
  other arithmetic  93.1 us (8%)
  waiting for transfers between devices  17.2 us (2%)
    unnamed x1, blocking collectives  222 us
    another operation x2, loops' own time, entering(): return lax.fori_loop(0, count - 1, lap, running)  168 us
    dynamic_slice x254, local copies, waits for them, and re-layouts, lap(): longer = join(running, jax.tree.map(lambda part: part[position], pieces))  155 us
    all_gather x1, blocking collectives, entering(): pieces = jax.tree.map(lambda part: lax.all_gather(part, axis), value)  153 us
    ppermute x8, starting transfers between devices, with_halo(): lax.ppermute(lax.slice_in_dim(block, block.shape[dim] - width, None, axis...  122 us
    dot_general x128, matrix products, combine_maps(): product = jnp.einsum('...ij,...jk->...ik', later, earlier, precision=exact)  102 us
    select_n x127, other arithmetic, lap(): jnp.where(position < mine, new, old)  86.5 us
    ppermute x8, starting transfers between devices, with_halo(): lax.ppermute(lax.slice_in_dim(block, 0, width, axis=dim), axis, backward)  29.4 us
  transfers between devices with their start and end apart: 16, of which 10 were waited for; matrix products, arithmetic and copies ran while one was open for 1% of the time, Pallas kernels for 0%

commit v1 on v0

v1 whole, which is shorter than its diff:
```python
import jax
import jax.numpy as jnp
from jax import lax
from jax.experimental import pallas as pl
from jax.experimental.pallas import tpu as pltpu
from jax.sharding import Mesh
from jax.sharding import PartitionSpec as P


N = 8
TILES = 2 * N * N
ROWS = TILES * N
penalty = 4.0
shift_mass = 0.02
centre = 1.25
half = 0.95
rho1 = half / centre
rho2 = 1.0 / (2.0 * centre / half - rho1)
keep = rho2 * rho1
gain2 = 2.0 * rho2 / half
exact = lax.Precision.HIGHEST
f32 = jnp.float32
bf16 = jnp.bfloat16
SFC = ("y", "z")
SUB = ("x", "c")


def tile(ref, t):
    return ref[pl.ds(t * N, N), :]


def put(ref, t, value):
    ref[pl.ds(t * N, N), :] = value


def at(q, a, b):
    return (q * N + a) * N + b


def node_scalars(st):
    diag = [st[i, i] + (2.0 if i in (0, N - 1) else 0.0) for i in range(N)]
    sums = []
    for i in range(N):
        total = st[i, 0]
        for j in range(1, N):
            total = total + st[i, j]
        sums.append(total)
    return diag, sums


def spread(values, index):
    out = jnp.where(index == 0, values[0], 0.0)
    for k in range(1, N):
        out = jnp.where(index == k, values[k], out)
    return out


def pair_index():
    row = lax.broadcasted_iota(jnp.int32, (N * N, 128), 0)
    return row // N, row % N


def raw(ref, q, a, b):
    return ref[pl.ds(at(0, a, b) * 2 * N + q, N, stride=2), :]


def pack_first(rs, coef, st, to_n, to_s, to_e, to_w):
    diag, _ = node_scalars(st)
    sub = lax.broadcasted_iota(jnp.int32, (N, 128), 0)
    mc = spread(diag, sub)
    c = [coef[pl.ds(q, 1), :] for q in range(2)]
    scale = [1.0 / (centre * c[q]) for q in range(2)]

    def value(q, a, b):
        return raw(rs, q, a, b) * scale[q] / ((diag[a] + diag[b]) + mc)

    zero = jnp.zeros((N, 128), f32)
    both = jnp.where(sub == 0, c[0], jnp.where(sub == 1, c[1], zero))
    for q in range(2):
        for b in range(N):
            put(to_n, q * N + b, value(q, N - 1, b))
            put(to_s, q * N + b, value(q, 0, b))
    put(to_n, 2 * N, both)
    put(to_s, 2 * N, both)
    for a in range(N):
        put(to_e, a, value(1, a, N - 1))
        put(to_w, a, value(0, a, 0))
    put(to_e, N, zero + c[1])
    put(to_w, N, zero + c[0])


def stiff(u, kk, st, acc):
    for a in range(N):
        lo = u[pl.ds(at(0, a, 0) * N, N * N), :]
        hi = u[pl.ds(at(1, a, 0) * N, N * N), :]
        x = jnp.concatenate([lo, hi], axis=1)
        xh = x.astype(bf16)
        xl = (x - xh.astype(f32)).astype(bf16)
        main = jnp.dot(kk[...], xh, preferred_element_type=f32)
        rest = jnp.dot(kk[pl.ds(0, N * N), :], xl, preferred_element_type=f32)
        y = main[: N * N] + (main[N * N :] + rest)
        acc[pl.ds(at(0, a, 0) * N, N * N), :] = y[:, :128]
        acc[pl.ds(at(1, a, 0) * N, N * N), :] = y[:, 128:]
    for q in range(2):
        for b in range(N):
            us = [tile(u, at(q, j, b)) for j in range(N)]
            for i in range(N):
                t = tile(acc, at(q, i, b))
                for j in range(N):
                    t = t + st[i, j] * us[j]
                put(acc, at(q, i, b), t)


def inner_faces(u, coef, acc):
    c = [coef[pl.ds(q, 1), :] for q in range(2)]
    for q in range(2):
        rc = 2.0 / c[q]
        up = 2.0 + pltpu.roll(c[q], 127, 1) * rc
        down = 2.0 + pltpu.roll(c[q], 1, 1) * rc
        for a in range(N):
            base = at(q, a, 0) * N
            first = pl.ds(base, N, stride=N)
            last = pl.ds(base + N - 1, N, stride=N)
            lower, upper = u[first, :], u[last, :]
            acc[last, :] += up * (upper - pltpu.roll(lower, 127, 1))
            acc[first, :] += down * (lower - pltpu.roll(upper, 1, 1))
    w0 = 2.0 + 2.0 * c[1] / c[0]
    w1 = 2.0 + 2.0 * c[0] / c[1]
    for a in range(N):
        d = tile(u, at(0, a, N - 1)) - tile(u, at(1, a, 0))
        put(acc, at(0, a, N - 1), tile(acc, at(0, a, N - 1)) + w0 * d)
        put(acc, at(1, a, 0), tile(acc, at(1, a, 0)) - w1 * d)


def block(ref, q, a):
    return ref[pl.ds(at(q, a, 0) * N, N * N), :]


def set_block(ref, q, a, value):
    ref[pl.ds(at(q, a, 0) * N, N * N), :] = value


def start(rs, coef, st, sv, g, rt, rb, kk, first, part):
    diag, sums = node_scalars(st)
    bi, ci = pair_index()
    mbc = spread(diag, bi) + spread(diag, ci)
    rb[...] = spread(sums, bi) + spread(sums, ci)
    row = lax.broadcasted_iota(jnp.int32, (N * N, N), 0)
    col = lax.broadcasted_iota(jnp.int32, (N * N, N), 1)
    pb = (row // N == col).astype(f32)
    pc = (row % N == col).astype(f32)
    wide = (((1,), (1,)), ((), ()))

    def outer(p):
        ps = jnp.dot(p, sv[...], precision=exact, preferred_element_type=f32)
        return lax.dot_general(ps, p, wide, precision=exact, preferred_element_type=f32)

    i = lax.broadcasted_iota(jnp.int32, (N * N, N * N), 0)
    j = lax.broadcasted_iota(jnp.int32, (N * N, N * N), 1)
    k = jnp.where(i % N == j % N, outer(pb), 0.0) + jnp.where(i // N == j // N, outer(pc), 0.0)
    kh = k.astype(bf16)
    kk[pl.ds(0, N * N), :] = kh
    kk[pl.ds(N * N, N * N), :] = (k - kh.astype(f32)).astype(bf16)
    rc = [1.0 / coef[pl.ds(q, 1), :] for q in range(2)]
    for a in range(N):
        r = 1.0 / (diag[a] + mbc)
        rt[pl.ds(a * N * N, N * N), :] = r
        for q in range(2):
            for b in range(N):
                t = raw(rs, q, a, b) * rc[q]
                put(g, at(q, a, b), t)
                put(first, at(q, a, b), t * r[b * N : (b + 1) * N] * (1.0 / centre))
    stiff(first, kk, st, part)
    inner_faces(first, coef, part)
    for q in range(2):
        for a in range(N):
            r = rt[pl.ds(a * N * N, N * N), :]
            v = (1.0 + keep) * block(first, q, a) + gain2 * r * (block(g, q, a) - block(part, q, a))
            set_block(part, q, a, v)


def middle(where, coef, st, g, rt, rb, kk, first, part, from_n, from_s, from_e, from_w, it, post, sums_out, to_e, to_w):
    c = [coef[pl.ds(q, 1), :] for q in range(2)]
    it[...] = part[...]
    wn = [2.0 + 2.0 * from_n[pl.ds(2 * N * N + q, 1), :] / c[q] for q in range(2)]
    ws = [2.0 + 2.0 * from_s[pl.ds(2 * N * N + q, 1), :] / c[q] for q in range(2)]
    we = 2.0 + 2.0 * from_e[pl.ds(N * N, 1), :] / c[1]
    ww = 2.0 + 2.0 * from_w[pl.ds(N * N, 1), :] / c[0]

    def add(q, a, b, w, other):
        k = at(q, a, b)
        put(it, k, tile(it, k) - gain2 * tile(rt, a * N + b) * (w * (tile(first, k) - other)))

    for q in range(2):
        for b in range(N):
            add(q, N - 1, b, wn[q], tile(from_n, q * N + b))
            add(q, 0, b, ws[q], tile(from_s, q * N + b))
    for a in range(N):
        add(1, a, N - 1, we, tile(from_e, a))
        add(0, a, 0, ww, tile(from_w, a))
    own = jnp.zeros((N, 128), f32)
    above = jnp.zeros((N, 128), f32)
    below = jnp.zeros((N, 128), f32)
    _, sums = node_scalars(st)
    for q in range(2):
        z = jnp.zeros((N * N, 128), f32)
        for a in range(N):
            z = z + (block(g, q, a) - (sums[a] + rb[...]) * block(it, q, a))
        t = z[:N]
        up = tile(it, at(q, N - 1, 0))
        dn = tile(it, at(q, 0, 0))
        for b in range(1, N):
            t = t + z[b * N : (b + 1) * N]
            up = up + tile(it, at(q, N - 1, b))
            dn = dn + tile(it, at(q, 0, b))
        up = (c[q] * wn[q]) * up
        dn = (c[q] * ws[q]) * dn
        own = own + (c[q] * t - (up + dn))
        above = above + up
        below = below + dn
    sub = lax.broadcasted_iota(jnp.int32, (N, 128), 0)
    lane = lax.broadcasted_iota(jnp.int32, (1, 128), 1)

    def total(x):
        return jnp.sum(x, axis=0, keepdims=True)

    stack = jnp.where(sub == 0, total(own), 0.0)
    stack = jnp.where(sub == 1, total(above), stack)
    stack = jnp.where(sub == 2, total(below), stack)
    stack = jnp.where(sub == 3, c[0] + c[1], stack)
    s = jnp.sum(stack, axis=1, keepdims=True)
    p = where[0]
    means = jnp.where(lane == p, s[0:1], 0.0)
    means = means + jnp.where(lane == p + 1, s[1:2], 0.0) + jnp.where(lane == p - 1, s[2:3], 0.0)
    sums_out[pl.ds(0, 1), :] = means
    sums_out[pl.ds(1, 1), :] = jnp.where(lane == p, s[3:4], 0.0)
    stiff(it, kk, st, post)
    inner_faces(it, coef, post)
    for q in range(2):
        for a in range(N):
            r = rt[pl.ds(a * N * N, N * N), :] * (1.0 / centre)
            set_block(post, q, a, block(it, q, a) + r * (block(g, q, a) - block(post, q, a)))
    for a in range(N):
        put(to_e, a, tile(it, at(1, a, N - 1)))
        put(to_e, N + a, tile(post, at(1, a, N - 1)))
        put(to_w, a, tile(it, at(0, a, 0)))
        put(to_w, N + a, tile(post, at(0, a, 0)))


def side(coef, rt, it, post_in, from_e, from_w, got_e, got_w, post, to_n, to_s):
    c = [coef[pl.ds(q, 1), :] for q in range(2)]
    ce = from_e[pl.ds(N * N, 1), :]
    cw = from_w[pl.ds(N * N, 1), :]
    we = 2.0 + 2.0 * ce / c[1]
    ww = 2.0 + 2.0 * cw / c[0]
    post[...] = post_in[...]
    for a in range(N):
        for q, b, w, got in ((1, N - 1, we, got_e), (0, 0, ww, got_w)):
            k = at(q, a, b)
            r = tile(rt, a * N + b) * (1.0 / centre)
            put(post, k, tile(post, k) - r * (w * (tile(it, k) - tile(got, a))))
    sub = lax.broadcasted_iota(jnp.int32, (N, 128), 0)
    outer = jnp.where(sub == 0, ce, jnp.where(sub == 1, cw, 0.0))
    for a, to in ((N - 1, to_n), (0, to_s)):
        for q in range(2):
            for b in range(N):
                put(to, q * N + b, tile(it, at(q, a, b)))
                put(to, 2 * N + q * N + b, tile(post, at(q, a, b)))
        put(to, 4 * N, tile(got_e, a))
        put(to, 4 * N + 1, tile(got_w, a))
        put(to, 4 * N + 2, outer)


def coarse(planes, gains, means):
    lane = lax.broadcasted_iota(jnp.int32, (1, 128), 1)
    before = jnp.where(lane == 0, gains, pltpu.roll(gains, 1, 1))
    diag = penalty * before + (penalty + shift_mass) * gains
    upper = jnp.where(lane < planes - 1, -penalty * gains, 0.0)
    diag = jnp.where(lane < planes, diag, 1.0)
    lower = jnp.where(lane == 0, 0.0, pltpu.roll(upper, 1, 1))
    right = jnp.where(lane < planes, means, 0.0)
    step = 1
    while step < planes:
        inv = 1.0 / diag
        lo = -lower * pltpu.roll(inv, step, 1)
        hi = -upper * pltpu.roll(inv, 128 - step, 1)
        right = right + lo * pltpu.roll(right, step, 1) + hi * pltpu.roll(right, 128 - step, 1)
        diag = diag + lo * pltpu.roll(upper, step, 1) + hi * pltpu.roll(lower, 128 - step, 1)
        lower = lo * pltpu.roll(lower, step, 1)
        upper = hi * pltpu.roll(upper, 128 - step, 1)
        step *= 2
    return right / diag


def finish(planes, per_plane, where, coef, st, g, rt, rb, kk, it, post, ring, from_n, from_s, from_e, from_w, got_e, got_w, got_n, got_s, out, acc, v):
    scaled = ring[0]
    for k in range(1, ring.shape[0]):
        scaled = scaled + ring[k]
    corr = coarse(planes, scaled[1:2] * (1.0 / per_plane), scaled[0:1] * (1.0 / (per_plane * N * N * N)))
    p = where[0]
    lane = lax.broadcasted_iota(jnp.int32, (1, 128), 1)

    def pick(k):
        return jnp.sum(jnp.where(lane == k, corr, 0.0), axis=1, keepdims=True) + jnp.zeros((1, 128), f32)

    mid, high, low = pick(p), pick(p + 1), pick(p - 1)
    has_n = (where[0] < planes - 1).astype(f32)
    has_s = (where[0] > 0).astype(f32)
    _, sums = node_scalars(st)
    inner = 1.0 / centre
    c = [coef[pl.ds(q, 1), :] for q in range(2)]
    cn = [from_n[pl.ds(2 * N * N + q, 1), :] for q in range(2)]
    cs = [from_s[pl.ds(2 * N * N + q, 1), :] for q in range(2)]
    ce = from_e[pl.ds(N * N, 1), :]
    cw = from_w[pl.ds(N * N, 1), :]
    wn = [2.0 + 2.0 * cn[q] / c[q] for q in range(2)]
    ws = [2.0 + 2.0 * cs[q] / c[q] for q in range(2)]
    we = 2.0 + 2.0 * ce / c[1]
    ww = 2.0 + 2.0 * cw / c[0]

    def r_at(a, b):
        return tile(rt, a * N + b)

    def weight(a, b):
        return 1.0 - inner * r_at(a, b) * (sums[a] + rb[pl.ds(b * N, N), :])

    for q in range(2):
        for a in range(N):
            r = rt[pl.ds(a * N * N, N * N), :]
            set_block(v, q, a, block(post, q, a) + mid * (1.0 - inner * r * (sums[a] + rb[...])))
        for b in range(N):
            for a, w, other, got in ((N - 1, wn[q], high, got_n), (0, ws[q], low, got_s)):
                k = at(q, a, b)
                jump = (tile(it, k) - tile(got, q * N + b)) + (mid - other)
                put(v, k, tile(v, k) - inner * r_at(a, b) * (w * jump))
    stiff(v, kk, st, acc)
    inner_faces(v, coef, acc)

    def add(k, w, other):
        put(acc, k, tile(acc, k) + w * (tile(v, k) - other))

    for q in range(2):
        for a, b0, w, has, got, far, cfar in (
            (N - 1, 0, wn[q], has_n, got_n, high, cn[q]),
            (0, N - 1, ws[q], has_s, got_s, low, cs[q]),
        ):
            back = 2.0 + 2.0 * c[q] / jnp.where(cfar > 0.0, cfar, 1.0)
            for b in range(N):
                k = at(q, a, b)
                jump = (tile(got, q * N + b) - tile(it, k)) + (far - mid)
                other = tile(got, 2 * N + q * N + b) + far * weight(b0, b) - inner * r_at(b0, b) * (back * jump)
                add(k, w, has * other)
    for q, b, far_b, w, got, line, row, cfar in (
        (1, N - 1, 0, we, got_e, 4 * N, 0, ce),
        (0, 0, N - 1, ww, got_w, 4 * N + 1, 1, cw),
    ):
        back = 2.0 + 2.0 * c[q] / cfar
        for a in range(N):
            k = at(q, a, b)
            loss = back * (tile(got, a) - tile(it, k))
            for edge, from_far, other in ((N - 1, got_n, high), (0, got_s, low)):
                if a == edge:
                    wf = 2.0 + 2.0 * from_far[pl.ds((4 * N + 2) * N + row, 1), :] / cfar
                    loss = loss + wf * ((tile(got, a) - tile(from_far, line)) + (mid - other))
            other = tile(got, N + a) + mid * weight(a, far_b) - inner * r_at(a, far_b) * loss
            add(k, w, other)
    for q in range(2):
        for a in range(N):
            r = rt[pl.ds(a * N * N, N * N), :]
            x = block(v, q, a)
            last = x + keep * ((x - block(it, q, a)) - mid) + gain2 * r * (block(g, q, a) - block(acc, q, a))
            for b in range(N):
                out[pl.ds(at(0, a, b) * 2 * N + q, N, stride=2), :] = last[b * N : (b + 1) * N]


def call(kernel, in_kinds, out_shapes, scratch=(), cost=None):
    kinds = {
        "v": pl.BlockSpec(memory_space=pltpu.VMEM),
        "s": pl.BlockSpec(memory_space=pltpu.SMEM),
    }
    return pl.pallas_call(
        kernel,
        out_shape=out_shapes,
        in_specs=[kinds[k] for k in in_kinds],
        out_specs=[kinds["v"]] * len(out_shapes),
        scratch_shapes=list(scratch),
        compiler_params=pltpu.CompilerParams(vmem_limit_bytes=24 << 20),
        cost_estimate=pl.CostEstimate(flops=cost or 10**6, bytes_accessed=10**5, transcendentals=0),
    )


def rows(n, dtype=f32, lanes=128):
    return jax.ShapeDtypeStruct((n, lanes), dtype)


def exchange(block_up, block_down, axis, count, periodic):
    up = [(i, i + 1) for i in range(count - 1)]
    if periodic:
        up.append((count - 1, 0))
    down = [(j, i) for i, j in up]
    return lax.ppermute(block_down, axis, down), lax.ppermute(block_up, axis, up)


def share(block, axis, count):
    return lax.all_to_all(jnp.broadcast_to(block[None], (count, *block.shape)), axis, 0, 0)


def solution(mesh):
    n_sfc, n_sub = mesh.shape["sfc"], mesh.shape["sub"]
    ny = 4 if n_sfc % 16 == 0 else 2
    nz = n_sfc // ny
    mesh4 = Mesh(mesh.devices.reshape(ny, nz, n_sub // 2, 2), ("y", "z", "x", "c"))

    def per_device(right_side, coefficient, stiffness):
        rs = right_side.reshape(ROWS, 128)
        coef = coefficient.reshape(2, 128)
        place = lax.axis_index(SFC).astype(jnp.int32)
        where = place.reshape(1)
        layer, strip = rows((2 * N + 1) * N), rows((N + 1) * N)
        to_n, to_s, to_e, to_w = call(pack_first, "vvs", [layer, layer, strip, strip])(rs, coef, stiffness)
        from_n, from_s = exchange(to_n, to_s, SFC, n_sfc, False)
        from_e, from_w = exchange(to_e, to_w, SUB, n_sub, True)
        field = rows(ROWS)
        g, rt, rb, kk, first, part = call(
            start, "vvsv", [field, rows(N * N * N), rows(N * N), rows(2 * N * N, bf16, N * N), field, field], cost=10**9
        )(rs, coef, stiffness, stiffness)
        it, post, sums, to_e, to_w = call(
            middle,
            "svsvvvvvvvvvv",
            [field, field, rows(2), rows(2 * N * N), rows(2 * N * N)],
        )(where, coef, stiffness, g, rt, rb, kk, first, part, from_n, from_s, from_e, from_w)
        got_e, got_w = exchange(to_e, to_w, SUB, n_sub, True)
        near = share(sums, ("y", "x", "c"), ny * n_sub).sum(0)
        post, to_n, to_s = call(side, "vvvvvvvv", [field, rows((4 * N + 3) * N), rows((4 * N + 3) * N)])(
            coef, rt, it, post, from_e, from_w, got_e, got_w
        )
        got_n, got_s = exchange(to_n, to_s, SFC, n_sfc, False)
        ring = share(near, "z", nz)

        def last(*refs):
            finish(n_sfc, float(2 * n_sub * 128), *refs)

        (out,) = call(
            last, "svs" + "v" * 15, [field], [pltpu.VMEM((ROWS, 128), f32), pltpu.VMEM((ROWS, 128), f32)]
        )(where, coef, stiffness, g, rt, rb, kk, it, post, ring, from_n, from_s, from_e, from_w, got_e, got_w, got_n, got_s)
        return out.reshape(right_side.shape)

    field_spec = P(None, None, None, SFC, SUB, None)
    return jax.shard_map(
        per_device, mesh=mesh4, in_specs=(field_spec, P(SFC, SUB, None), P()), out_specs=field_spec, check_vma=False
    )
```

time: 1120 us -> 86.1 us (0.08)
  blocking collectives: 388 us -> 22.4 us
  local copies, waits for them, and re-layouts: 178 us -> 3.73 us
  loops' own time: 168 us -> 0 us
  starting transfers between devices: 151 us -> 37.5 us
  matrix products: 113 us -> 0 us
  other arithmetic: 93.1 us -> 0.04 us
    unnamed x1 -> x0, blocking collectives: 222 us -> none
    another operation x2 -> x0, loops' own time: 168 us -> none  [entering(): return lax.fori_loop(0, count - 1, lap, running)]
    dynamic_slice x254 -> x0, local copies, waits for them, and re-layouts: 155 us -> none  [lap(): longer = join(running, jax.tree.map(lambda part: part[position], pieces))]
    all_gather x1 -> x0, blocking collectives: 153 us -> none  [entering(): pieces = jax.tree.map(lambda part: lax.all_gather(part, axis), value)]
    ppermute x16 -> x8, starting transfers between devices: 151 us -> 26.5 us  [the longest x4 17.4 us: exchange(): lax.ppermute(block_down, axis, down)]
    dot_general x140 -> x0, matrix products: 113 us -> none  [the longest x128 102 us: combine_maps(): product = jnp.einsum('...ij,...jk->...ik', later, earlier, precision=exact)]
    select_n x127 -> x0, other arithmetic: 86.5 us -> none  [lap(): jnp.where(position < mine, new, old)]
    all_to_all x0 -> x1, blocking collectives: none -> 22.4 us  [share(): lax.all_to_all(jnp.broadcast_to(block[None], (count, *block.shape)), axis...]
  transfers between devices with their start and end apart: 16 -> 9, of which waited for: 10 -> 4; matrix products, arithmetic and copies ran while one was open for 1% -> 0% of each run, Pallas kernels for 0% -> 2%
where the time goes in v1:
time: 86.1 us; the launch traced here: 85.7 us
  starting transfers between devices  37.5 us (44%)
  blocking collectives  22.4 us (26%)
  waiting for transfers between devices  14.9 us (17%)
  Pallas kernels  6.94 us (8%)
  local copies, waits for them, and re-layouts  3.73 us (4%)
    all_to_all x1, blocking collectives, share(): lax.all_to_all(jnp.broadcast_to(block[None], (count, *block.shape)), axis...  22.4 us
    ppermute x4, starting transfers between devices, exchange(): lax.ppermute(block_down, axis, down)  17.4 us
    all_to_all x1, starting transfers between devices, share(): lax.all_to_all(jnp.broadcast_to(block[None], (count, *block.shape)), axis...  11.1 us
    all_to_all x1, waiting for transfers between devices, share(): lax.all_to_all(jnp.broadcast_to(block[None], (count, *block.shape)), axis...  10.5 us
    ppermute x4, starting transfers between devices, exchange(): lax.ppermute(block_up, axis, up)  9.06 us
    ppermute x4, waiting for transfers between devices, exchange(): lax.ppermute(block_down, axis, down)  3.29 us
    pallas_call x1, Pallas kernels, per_device(): call(last, 'svs' + 'v' * 15, [field], [pltpu.VMEM((ROWS, 128), f32), pltp...  3.1 us
    unnamed x8, local copies, waits for them, and re-layouts  3.09 us
  transfers between devices with their start and end apart: 9, of which 4 were waited for; matrix products, arithmetic and copies ran while one was open for 0% of the time, Pallas kernels for 2%

profile of v1, /device:TPU:1, one launch (start us, length us, event | category | flops | bytes accessed | tf_op | source)
XLA Modules:
  0.0 85.7 jit_solution(11237176114428993177)
XLA Ops:
  0.0 0.0 copy-start.3
  0.0 0.7 copy-done.3
  0.7 0.0 copy-start
  0.7 1.0 %copy-done = f32[8,8,8,1,2,128]{5,4,3,2,1,0:T(2,128)S(1)} copy-done((f32[8,8,8,1,2,128]{5,4,3,2,1,0:T(2,128)S(1)}, f32[8,8,8,1,2,128]{5,4,3,2,1,0:T(2,128)}, u32[]{:S(2)}) %copy-start) | copy-done | bytes 524312
  1.7 0.0 copy-start.1
  1.7 0.7 copy-done.1
  2.4 0.6 shard_map.38
  3.0 14.2 %collective-permute-start.2 = (f32[72,128]{1,0:T(8,128)S(1)}, f32[72,128]{1,0:T(8,128)S(1)}, u32[]{:S(2)}, u32[]{:S(2)}) collective-permute-start(f32[72,128]{1,0:T(8,128)S(1)} %get-tuple-element.31), channel_id=1, source_target_pairs={{1,0},{2,1},{3,2},{4,3},{5,4},{6,5},{7,6},{0,7},{9,8},{10,9},{11,1... | collective-permute-start | bytes 110600 | tf_op jit(solution)/shard_map/ppermute | solution.py:401
  17.2 0.0 collective-permute-start.3
  17.2 1.3 %collective-permute-start = (f32[136,128]{1,0:T(8,128)S(1)}, f32[136,128]{1,0:T(8,128)S(1)}, u32[]{:S(2)}, u32[]{:S(2)}) collective-permute-start(f32[136,128]{1,0:T(8,128)S(1)} %get-tuple-element.29), channel_id=1, source_target_pairs={{8,0},{16,8},{24,16},{32,24},{40,32},{48,40},{56,48},{64,56},{72,6... | collective-permute-start | bytes 208904 | tf_op jit(solution)/shard_map/ppermute | solution.py:401
  18.5 4.0 %collective-permute-start.1 = (f32[136,128]{1,0:T(8,128)S(1)}, f32[136,128]{1,0:T(8,128)S(1)}, u32[]{:S(2)}, u32[]{:S(2)}) collective-permute-start(f32[136,128]{1,0:T(8,128)S(1)} %get-tuple-element.30), channel_id=1, source_target_pairs={{0,8},{8,16},{16,24},{24,32},{32,40},{40,48},{48,56},{56,64},{64,7... | collective-permute-start | bytes 208904 | tf_op jit(solution)/shard_map/ppermute | solution.py:401
  22.5 1.8 %shard_map.37 = (f32[1024,128]{1,0:T(8,128)S(1)}, f32[512,128]{1,0:T(8,128)S(1)}, f32[64,128]{1,0:T(8,128)S(1)}, bf16[128,64]{1,0:T(8,128)(2,1)S(1)}, f32[1024,128]{1,0:T(8,128)S(1)}, /*index=5*/f32[1024,128]{1,0:T(8,128)S(1)}) custom-call(f32[1024,128]{1,0:T(8,128)S(1)} %bitcast.7, f32[2,128]{1,0:T(2,128)S(1)} %bitcast.9, f32[8,8]{1,0:T(8,128)S(1)} %copy-done.1, ...), custom_call_target="tpu_custom_call" | custom-call | flops 1000000000 | bytes 100000 | tf_op jit(solution)/shard_map/pallas_call | solution.py:424
  24.3 0.0 collective-permute-done.2.from_e.refs_12_
  24.3 0.0 collective-permute-done.3.from_w.refs_13_
  24.3 0.0 collective-permute-done.from_n.refs_10_
  24.3 0.0 collective-permute-done.1.from_s.refs_11_
  24.3 0.0 copy-start.2
  24.3 0.7 copy-done.2
  25.0 1.4 %shard_map.39 = (f32[1024,128]{1,0:T(8,128)S(1)}, f32[1024,128]{1,0:T(8,128)S(1)}, f32[2,128]{1,0:T(2,128)S(1)}, f32[128,128]{1,0:T(8,128)S(1)}, f32[128,128]{1,0:T(8,128)S(1)}) custom-call(s32[1]{0:T(128)} %bitcast.where.refs_0_, f32[2,128]{1,0:T(2,128)S(1)} %bitcast.10, f32[8,8]{1,0:T(8,128)S(1)} %copy-done.2, ...), custom_call_target="tpu_custom_call" | custom-call | flops 1000000 | bytes 100000 | tf_op jit(solution)/shard_map/pallas_call | solution.py:427
  26.4 22.4 %all_to_all.10 = f32[32,2,128]{2,1,0:T(2,128)S(1)} all-to-all(f32[32,2,128]{2,1,0:T(2,128)S(1)} %broadcast_in_dim.4), channel_id=1, replica_groups=mesh['y'=4,'z'=32,'x'=4,'c'=2] {'y','x','c'}, dimensions={0} | all-to-all | bytes 65536 | tf_op jit(solution)/shard_map/all_to_all | solution.py:405
  48.9 0.6 broadcast_in_dim.5
  49.5 11.1 %all-to-all-start.1 = ((f32[32,2,128]{2,1,0:T(2,128)}), f32[32,2,128]{2,1,0:T(2,128)S(1)}, u32[]{:S(2)}, u32[]{:S(2)}) async-start(f32[32,2,128]{2,1,0:T(2,128)} %broadcast_in_dim.5), calls=%async_computation.1 | async-start | bytes 65536 | tf_op jit(solution)/shard_map/all_to_all | solution.py:405
  60.6 0.7 collective-permute-start.4
  61.3 1.1 %collective-permute-start.5 = (f32[128,128]{1,0:T(8,128)S(1)}, f32[128,128]{1,0:T(8,128)S(1)}, u32[]{:S(2)}, u32[]{:S(2)}) collective-permute-start(f32[128,128]{1,0:T(8,128)S(1)} %get-tuple-element.36), channel_id=1, source_target_pairs={{0,1},{1,2},{2,3},{3,4},{4,5},{5,6},{6,7},{7,0},{8,9},{9,10},{10,1... | collective-permute-start | bytes 196616 | tf_op jit(solution)/shard_map/ppermute | solution.py:401
  62.4 2.1 %collective-permute-done.4.got_e.refs_14_ = f32[128,128]{1,0:T(8,128)S(1)} collective-permute-done((f32[128,128]{1,0:T(8,128)S(1)}, f32[128,128]{1,0:T(8,128)S(1)}, u32[]{:S(2)}, u32[]{:S(2)}) %collective-permute-start.4) | collective-permute-done | bytes 65568 | tf_op jit(solution)/shard_map/ppermute | solution.py:401
  64.5 0.0 collective-permute-done.5.got_w.refs_15_
  64.5 0.1 shard_map.40
  64.5 1.3 %collective-permute-start.6 = (f32[280,128]{1,0:T(8,128)S(1)}, f32[280,128]{1,0:T(8,128)S(1)}, u32[]{:S(2)}, u32[]{:S(2)}) collective-permute-start(f32[280,128]{1,0:T(8,128)S(1)} %get-tuple-element.39), channel_id=1, source_target_pairs={{8,0},{16,8},{24,16},{32,24},{40,32},{48,40},{56,48},{64,56},{72,6... | collective-permute-start | bytes 430088 | tf_op jit(solution)/shard_map/ppermute | solution.py:401
  65.8 4.0 %collective-permute-start.7 = (f32[280,128]{1,0:T(8,128)S(1)}, f32[280,128]{1,0:T(8,128)S(1)}, u32[]{:S(2)}, u32[]{:S(2)}) collective-permute-start(f32[280,128]{1,0:T(8,128)S(1)} %get-tuple-element.40), channel_id=1, source_target_pairs={{0,8},{8,16},{16,24},{24,32},{32,40},{40,48},{48,56},{56,64},{64,7... | collective-permute-start | bytes 430088 | tf_op jit(solution)/shard_map/ppermute | solution.py:401
  69.8 1.2 %collective-permute-done.6.refs_16_ = f32[280,128]{1,0:T(8,128)S(1)} collective-permute-done((f32[280,128]{1,0:T(8,128)S(1)}, f32[280,128]{1,0:T(8,128)S(1)}, u32[]{:S(2)}, u32[]{:S(2)}) %collective-permute-start.6) | collective-permute-done | bytes 143392 | tf_op jit(solution)/shard_map/ppermute | solution.py:401
  71.0 1.1 %collective-permute-done.7.refs_17_ = f32[280,128]{1,0:T(8,128)S(1)} collective-permute-done((f32[280,128]{1,0:T(8,128)S(1)}, f32[280,128]{1,0:T(8,128)S(1)}, u32[]{:S(2)}, u32[]{:S(2)}) %collective-permute-start.7) | collective-permute-done | bytes 143392 | tf_op jit(solution)/shard_map/ppermute | solution.py:401
  72.1 10.5 %all-to-all-done.1.refs_9_ = f32[32,2,128]{2,1,0:T(2,128)S(1)} async-done(((f32[32,2,128]{2,1,0:T(2,128)}), f32[32,2,128]{2,1,0:T(2,128)S(1)}, u32[]{:S(2)}, u32[]{:S(2)}) %all-to-all-start.1) | async-done | bytes 32800 | tf_op jit(solution)/shard_map/all_to_all | solution.py:405
  82.6 3.1 %shard_map.41 = f32[1024,128]{1,0:T(8,128)} custom-call(s32[1]{0:T(128)} %bitcast.where.refs_0_, f32[2,128]{1,0:T(2,128)S(1)} %bitcast.12, f32[8,8]{1,0:T(8,128)S(1)} %copy-done.2, f32[1024,128]{1,0:T(8,128)S(1)} %get-tuple-element.23.g.refs_3_, f32[512,128]{1,0:T(8,128)S(1)} %get-tuple-element.24.rt.refs_4_, f32[64,128]{1,0:T(8,128)S(1)} %get-tuple-element.25.rb.refs_5_, ...), custom_call_target="tpu_custom_call" | custom-call | flops 1000000 | bytes 100000 | tf_op jit(solution)/shard_map/pallas_call | solution.py:443
  (2 shorter events, 0.1 us)
Async XLA Ops:
  0.0 0.7 copy-start.3
  0.7 1.0 %copy-start = (f32[8,8,8,1,2,128]{5,4,3,2,1,0:T(2,128)S(1)}, f32[8,8,8,1,2,128]{5,4,3,2,1,0:T(2,128)}, u32[]{:S(2)}) copy-start(f32[8,8,8,1,2,128]{5,4,3,2,1,0:T(2,128)} %param.3) | copy-start | bytes 1572868
  1.7 0.7 copy-start.1
  3.0 21.2 %collective-permute-start.2 = (f32[72,128]{1,0:T(8,128)S(1)}, f32[72,128]{1,0:T(8,128)S(1)}, u32[]{:S(2)}, u32[]{:S(2)}) collective-permute-start(f32[72,128]{1,0:T(8,128)S(1)} %get-tuple-element.31), channel_id=1, source_target_pairs={{1,0},{2,1},{3,2},{4,3},{5,4},{6,5},{7,6},{0,7},{9,8},{10,9},{11,1... | collective-permute-start | bytes 110600 | tf_op jit(solution)/shard_map/ppermute | solution.py:401
  17.2 7.1 %collective-permute-start.3 = (f32[72,128]{1,0:T(8,128)S(1)}, f32[72,128]{1,0:T(8,128)S(1)}, u32[]{:S(2)}, u32[]{:S(2)}) collective-permute-start(f32[72,128]{1,0:T(8,128)S(1)} %get-tuple-element.32), channel_id=1, source_target_pairs={{0,1},{1,2},{2,3},{3,4},{4,5},{5,6},{6,7},{7,0},{8,9},{9,10},{10,1... | collective-permute-start | bytes 110600 | tf_op jit(solution)/shard_map/ppermute | solution.py:401
  17.2 7.1 %collective-permute-start = (f32[136,128]{1,0:T(8,128)S(1)}, f32[136,128]{1,0:T(8,128)S(1)}, u32[]{:S(2)}, u32[]{:S(2)}) collective-permute-start(f32[136,128]{1,0:T(8,128)S(1)} %get-tuple-element.29), channel_id=1, source_target_pairs={{8,0},{16,8},{24,16},{32,24},{40,32},{48,40},{56,48},{64,56},{72,6... | collective-permute-start | bytes 208904 | tf_op jit(solution)/shard_map/ppermute | solution.py:401
  18.5 5.8 %collective-permute-start.1 = (f32[136,128]{1,0:T(8,128)S(1)}, f32[136,128]{1,0:T(8,128)S(1)}, u32[]{:S(2)}, u32[]{:S(2)}) collective-permute-start(f32[136,128]{1,0:T(8,128)S(1)} %get-tuple-element.30), channel_id=1, source_target_pairs={{0,8},{8,16},{16,24},{24,32},{32,40},{40,48},{48,56},{56,64},{64,7... | collective-permute-start | bytes 208904 | tf_op jit(solution)/shard_map/ppermute | solution.py:401
  24.3 0.7 copy-start.2
  49.5 33.1 %all-to-all-start.1 = ((f32[32,2,128]{2,1,0:T(2,128)}), f32[32,2,128]{2,1,0:T(2,128)S(1)}, u32[]{:S(2)}, u32[]{:S(2)}) async-start(f32[32,2,128]{2,1,0:T(2,128)} %broadcast_in_dim.5), calls=%async_computation.1 | async-start | bytes 65536 | tf_op jit(solution)/shard_map/all_to_all | solution.py:405
  60.6 3.8 %collective-permute-start.4 = (f32[128,128]{1,0:T(8,128)S(1)}, f32[128,128]{1,0:T(8,128)S(1)}, u32[]{:S(2)}, u32[]{:S(2)}) collective-permute-start(f32[128,128]{1,0:T(8,128)S(1)} %get-tuple-element.35), channel_id=1, source_target_pairs={{1,0},{2,1},{3,2},{4,3},{5,4},{6,5},{7,6},{0,7},{9,8},{10,9},{11,1... | collective-permute-start | bytes 196616 | tf_op jit(solution)/shard_map/ppermute | solution.py:401
  61.3 3.2 %collective-permute-start.5 = (f32[128,128]{1,0:T(8,128)S(1)}, f32[128,128]{1,0:T(8,128)S(1)}, u32[]{:S(2)}, u32[]{:S(2)}) collective-permute-start(f32[128,128]{1,0:T(8,128)S(1)} %get-tuple-element.36), channel_id=1, source_target_pairs={{0,1},{1,2},{2,3},{3,4},{4,5},{5,6},{6,7},{7,0},{8,9},{9,10},{10,1... | collective-permute-start | bytes 196616 | tf_op jit(solution)/shard_map/ppermute | solution.py:401
  64.5 6.5 %collective-permute-start.6 = (f32[280,128]{1,0:T(8,128)S(1)}, f32[280,128]{1,0:T(8,128)S(1)}, u32[]{:S(2)}, u32[]{:S(2)}) collective-permute-start(f32[280,128]{1,0:T(8,128)S(1)} %get-tuple-element.39), channel_id=1, source_target_pairs={{8,0},{16,8},{24,16},{32,24},{40,32},{48,40},{56,48},{64,56},{72,6... | collective-permute-start | bytes 430088 | tf_op jit(solution)/shard_map/ppermute | solution.py:401
  65.8 6.3 %collective-permute-start.7 = (f32[280,128]{1,0:T(8,128)S(1)}, f32[280,128]{1,0:T(8,128)S(1)}, u32[]{:S(2)}, u32[]{:S(2)}) collective-permute-start(f32[280,128]{1,0:T(8,128)S(1)} %get-tuple-element.40), channel_id=1, source_target_pairs={{0,8},{8,16},{16,24},{24,32},{32,40},{40,48},{48,56},{56,64},{64,7... | collective-permute-start | bytes 430088 | tf_op jit(solution)/shard_map/ppermute | solution.py:401

commit v2 on v1

--- a/solution.py
+++ b/solution.py
@@ -37,45 +37,48 @@
     return (q * N + a) * N + b
 
 
-def node_scalars(st):
-    diag = [st[i, i] + (2.0 if i in (0, N - 1) else 0.0) for i in range(N)]
-    sums = []
-    for i in range(N):
-        total = st[i, 0]
-        for j in range(1, N):
-            total = total + st[i, j]
-        sums.append(total)
-    return diag, sums
-
-
-def spread(values, index):
-    out = jnp.where(index == 0, values[0], 0.0)
-    for k in range(1, N):
-        out = jnp.where(index == k, values[k], out)
-    return out
-
-
-def pair_index():
-    row = lax.broadcasted_iota(jnp.int32, (N * N, 128), 0)
-    return row // N, row % N
+def node_columns(sv):
+    i = lax.broadcasted_iota(jnp.int32, (N, N), 0)
+    j = lax.broadcasted_iota(jnp.int32, (N, N), 1)
+    s = sv[...]
+    edge = jnp.where((i == j) & ((i == 0) | (i == N - 1)), 2.0, 0.0)
+    diag = jnp.sum(jnp.where(i == j, s, 0.0) + edge, axis=1, keepdims=True)
+    zero = jnp.zeros((N, 128), f32)
+    return diag + zero, jnp.sum(s, axis=1, keepdims=True) + zero
+
+
+def line(x, k, count=N):
+    return jnp.broadcast_to(x[k : k + 1], (count, 128))
+
+
+def pair_sum(x):
+    return jnp.concatenate([line(x, b) + x for b in range(N)], axis=0)
 
 
 def raw(ref, q, a, b):
     return ref[pl.ds(at(0, a, b) * 2 * N + q, N, stride=2), :]
 
 
-def pack_first(rs, coef, st, to_n, to_s, to_e, to_w):
-    diag, _ = node_scalars(st)
+def pack_first(rs_far, coef_far, sv_far, to_n, to_s, to_e, to_w, rs, coef, sv, sems):
+    copies = [
+        pltpu.make_async_copy(src, dst, sems.at[k])
+        for k, (src, dst) in enumerate(((sv_far, sv), (coef_far, coef), (rs_far, rs)))
+    ]
+    for copy in copies:
+        copy.start()
+    copies[0].wait()
+    copies[1].wait()
+    mc, _ = node_columns(sv)
     sub = lax.broadcasted_iota(jnp.int32, (N, 128), 0)
-    mc = spread(diag, sub)
     c = [coef[pl.ds(q, 1), :] for q in range(2)]
     scale = [1.0 / (centre * c[q]) for q in range(2)]
-
-    def value(q, a, b):
-        return raw(rs, q, a, b) * scale[q] / ((diag[a] + diag[b]) + mc)
-
     zero = jnp.zeros((N, 128), f32)
     both = jnp.where(sub == 0, c[0], jnp.where(sub == 1, c[1], zero))
+    copies[2].wait()
+
+    def value(q, a, b):
+        return raw(rs, q, a, b) * scale[q] / ((line(mc, a) + line(mc, b)) + mc)
+
     for q in range(2):
         for b in range(N):
             put(to_n, q * N + b, value(q, N - 1, b))
@@ -107,7 +110,7 @@
             for i in range(N):
                 t = tile(acc, at(q, i, b))
                 for j in range(N):
-                    t = t + st[i, j] * us[j]
+                    t = t + tile(st, i * N + j) * us[j]
                 put(acc, at(q, i, b), t)
 
 
@@ -140,11 +143,15 @@
     ref[pl.ds(at(q, a, 0) * N, N * N), :] = value
 
 
-def start(rs, coef, st, sv, g, rt, rb, kk, first, part):
-    diag, sums = node_scalars(st)
-    bi, ci = pair_index()
-    mbc = spread(diag, bi) + spread(diag, ci)
-    rb[...] = spread(sums, bi) + spread(sums, ci)
+def start(rs, coef, sv, g, rt, rb, kk, st, first, part):
+    diag, sums = node_columns(sv)
+    mbc = pair_sum(diag)
+    pairs = pair_sum(sums)
+    for a in range(N):
+        rb[pl.ds(a * N * N, N * N), :] = pairs + line(sums, a, N * N)
+    for i in range(N):
+        for j in range(N):
+            put(st, i * N + j, jnp.broadcast_to(sv[pl.ds(i, 1), pl.ds(j, 1)], (N, 128)))
     row = lax.broadcasted_iota(jnp.int32, (N * N, N), 0)
     col = lax.broadcasted_iota(jnp.int32, (N * N, N), 1)
     pb = (row // N == col).astype(f32)
@@ -163,7 +170,7 @@
     kk[pl.ds(N * N, N * N), :] = (k - kh.astype(f32)).astype(bf16)
     rc = [1.0 / coef[pl.ds(q, 1), :] for q in range(2)]
     for a in range(N):
-        r = 1.0 / (diag[a] + mbc)
+        r = 1.0 / (line(diag, a, N * N) + mbc)
         rt[pl.ds(a * N * N, N * N), :] = r
         for q in range(2):
             for b in range(N):
@@ -179,7 +186,7 @@
             set_block(part, q, a, v)
 
 
-def middle(where, coef, st, g, rt, rb, kk, first, part, from_n, from_s, from_e, from_w, it, post, sums_out, to_e, to_w):
+def middle(masks, coef, g, rt, rb, first, part, from_n, from_s, from_e, from_w, it, sums_out):
     c = [coef[pl.ds(q, 1), :] for q in range(2)]
     it[...] = part[...]
     wn = [2.0 + 2.0 * from_n[pl.ds(2 * N * N + q, 1), :] / c[q] for q in range(2)]
@@ -201,11 +208,10 @@
     own = jnp.zeros((N, 128), f32)
     above = jnp.zeros((N, 128), f32)
     below = jnp.zeros((N, 128), f32)
-    _, sums = node_scalars(st)
     for q in range(2):
         z = jnp.zeros((N * N, 128), f32)
         for a in range(N):
-            z = z + (block(g, q, a) - (sums[a] + rb[...]) * block(it, q, a))
+            z = z + (block(g, q, a) - rb[pl.ds(a * N * N, N * N), :] * block(it, q, a))
         t = z[:N]
         up = tile(it, at(q, N - 1, 0))
         dn = tile(it, at(q, 0, 0))
@@ -219,7 +225,6 @@
         above = above + up
         below = below + dn
     sub = lax.broadcasted_iota(jnp.int32, (N, 128), 0)
-    lane = lax.broadcasted_iota(jnp.int32, (1, 128), 1)
 
     def total(x):
         return jnp.sum(x, axis=0, keepdims=True)
@@ -229,11 +234,14 @@
     stack = jnp.where(sub == 2, total(below), stack)
     stack = jnp.where(sub == 3, c[0] + c[1], stack)
     s = jnp.sum(stack, axis=1, keepdims=True)
-    p = where[0]
-    means = jnp.where(lane == p, s[0:1], 0.0)
-    means = means + jnp.where(lane == p + 1, s[1:2], 0.0) + jnp.where(lane == p - 1, s[2:3], 0.0)
-    sums_out[pl.ds(0, 1), :] = means
-    sums_out[pl.ds(1, 1), :] = jnp.where(lane == p, s[3:4], 0.0)
+    here = masks[pl.ds(0, 1), :]
+    means = here * s[0:1] + masks[pl.ds(1, 1), :] * s[1:2] + masks[pl.ds(2, 1), :] * s[2:3]
+    sub2 = lax.broadcasted_iota(jnp.int32, (2, 128), 0)
+    pair = jnp.where(sub2 == 0, means, here * s[3:4])
+    sums_out[...] = jnp.broadcast_to(pair[None], sums_out.shape)
+
+
+def smooth(coef, st, g, rt, kk, it, post, to_e, to_w):
     stiff(it, kk, st, post)
     inner_faces(it, coef, post)
     for q in range(2):
@@ -247,7 +255,14 @@
         put(to_w, N + a, tile(post, at(0, a, 0)))
 
 
-def side(coef, rt, it, post_in, from_e, from_w, got_e, got_w, post, to_n, to_s):
+def fold(parts, ready, out):
+    total = parts[0] + ready[pl.ds(0, 2), :]
+    for k in range(1, parts.shape[0]):
+        total = total + parts[k]
+    out[...] = jnp.broadcast_to(total[None], out.shape)
+
+
+def side(coef, rt, it, post_in, from_e, from_w, got_e, got_w, post, to_n, to_s, ready):
     c = [coef[pl.ds(q, 1), :] for q in range(2)]
     ce = from_e[pl.ds(N * N, 1), :]
     cw = from_w[pl.ds(N * N, 1), :]
@@ -269,6 +284,7 @@
         put(to, 4 * N, tile(got_e, a))
         put(to, 4 * N + 1, tile(got_w, a))
         put(to, 4 * N + 2, outer)
+    ready[...] = jnp.zeros((N, 128), f32)
 
 
 def coarse(planes, gains, means):
@@ -292,21 +308,18 @@
     return right / diag
 
 
-def finish(planes, per_plane, where, coef, st, g, rt, rb, kk, it, post, ring, from_n, from_s, from_e, from_w, got_e, got_w, got_n, got_s, out, acc, v):
+def finish(planes, per_plane, masks, coef, st, g, rt, rb, kk, it, post, ring, from_n, from_s, from_e, from_w, got_e, got_w, got_n, got_s, out, acc, v):
     scaled = ring[0]
     for k in range(1, ring.shape[0]):
         scaled = scaled + ring[k]
     corr = coarse(planes, scaled[1:2] * (1.0 / per_plane), scaled[0:1] * (1.0 / (per_plane * N * N * N)))
-    p = where[0]
-    lane = lax.broadcasted_iota(jnp.int32, (1, 128), 1)
 
     def pick(k):
-        return jnp.sum(jnp.where(lane == k, corr, 0.0), axis=1, keepdims=True) + jnp.zeros((1, 128), f32)
-
-    mid, high, low = pick(p), pick(p + 1), pick(p - 1)
-    has_n = (where[0] < planes - 1).astype(f32)
-    has_s = (where[0] > 0).astype(f32)
-    _, sums = node_scalars(st)
+        return jnp.sum(masks[pl.ds(k, 1), :] * corr, axis=1, keepdims=True) + jnp.zeros((1, 128), f32)
+
+    mid, high, low = pick(0), pick(1), pick(2)
+    has_n = masks[pl.ds(3, 1), :]
+    has_s = masks[pl.ds(4, 1), :]
     inner = 1.0 / centre
     c = [coef[pl.ds(q, 1), :] for q in range(2)]
     cn = [from_n[pl.ds(2 * N * N + q, 1), :] for q in range(2)]
@@ -322,12 +335,12 @@
         return tile(rt, a * N + b)
 
     def weight(a, b):
-        return 1.0 - inner * r_at(a, b) * (sums[a] + rb[pl.ds(b * N, N), :])
+        return 1.0 - inner * r_at(a, b) * tile(rb, a * N + b)
 
     for q in range(2):
         for a in range(N):
             r = rt[pl.ds(a * N * N, N * N), :]
-            set_block(v, q, a, block(post, q, a) + mid * (1.0 - inner * r * (sums[a] + rb[...])))
+            set_block(v, q, a, block(post, q, a) + mid * (1.0 - inner * r * rb[pl.ds(a * N * N, N * N), :]))
         for b in range(N):
             for a, w, other, got in ((N - 1, wn[q], high, got_n), (0, ws[q], low, got_s)):
                 k = at(q, a, b)
@@ -373,19 +386,16 @@
                 out[pl.ds(at(0, a, b) * 2 * N + q, N, stride=2), :] = last[b * N : (b + 1) * N]
 
 
-def call(kernel, in_kinds, out_shapes, scratch=(), cost=None):
-    kinds = {
-        "v": pl.BlockSpec(memory_space=pltpu.VMEM),
-        "s": pl.BlockSpec(memory_space=pltpu.SMEM),
-    }
+def call(kernel, in_kinds, out_shapes, scratch=(), cost=10**6, vmem=24):
+    kinds = {"v": pl.BlockSpec(memory_space=pltpu.VMEM), "h": pl.BlockSpec(memory_space=pltpu.HBM)}
     return pl.pallas_call(
         kernel,
         out_shape=out_shapes,
         in_specs=[kinds[k] for k in in_kinds],
         out_specs=[kinds["v"]] * len(out_shapes),
         scratch_shapes=list(scratch),
-        compiler_params=pltpu.CompilerParams(vmem_limit_bytes=24 << 20),
-        cost_estimate=pl.CostEstimate(flops=cost or 10**6, bytes_accessed=10**5, transcendentals=0),
+        compiler_params=pltpu.CompilerParams(vmem_limit_bytes=vmem << 20),
+        cost_estimate=pl.CostEstimate(flops=cost, bytes_accessed=10**5, transcendentals=0),
     )
 
 
@@ -401,8 +411,12 @@
     return lax.ppermute(block_down, axis, down), lax.ppermute(block_up, axis, up)
 
 
-def share(block, axis, count):
-    return lax.all_to_all(jnp.broadcast_to(block[None], (count, *block.shape)), axis, 0, 0)
+def place_masks(place, planes):
+    lane = jnp.arange(128)[None, :]
+    k = jnp.arange(8)[:, None]
+    hot = jnp.where(k == 0, place, jnp.where(k == 1, place + 1, place - 1))
+    has = jnp.where(k == 3, place < planes - 1, place > 0)
+    return jnp.where(k < 3, lane == hot, has).astype(f32)
 
 
 def solution(mesh):
@@ -414,35 +428,50 @@
     def per_device(right_side, coefficient, stiffness):
         rs = right_side.reshape(ROWS, 128)
         coef = coefficient.reshape(2, 128)
-        place = lax.axis_index(SFC).astype(jnp.int32)
-        where = place.reshape(1)
+        masks = place_masks(lax.axis_index(SFC), n_sfc)
+        field = rows(ROWS)
         layer, strip = rows((2 * N + 1) * N), rows((N + 1) * N)
-        to_n, to_s, to_e, to_w = call(pack_first, "vvs", [layer, layer, strip, strip])(rs, coef, stiffness)
+        to_n, to_s, to_e, to_w = call(
+            pack_first,
+            "hhh",
+            [layer, layer, strip, strip],
+            [
+                pltpu.VMEM((ROWS, 128), f32),
+                pltpu.VMEM((2, 128), f32),
+                pltpu.VMEM((N, N), f32),
+                pltpu.SemaphoreType.DMA((3,)),
+            ],
+            vmem=60,
+        )(rs, coef, stiffness)
         from_n, from_s = exchange(to_n, to_s, SFC, n_sfc, False)
         from_e, from_w = exchange(to_e, to_w, SUB, n_sub, True)
-        field = rows(ROWS)
-        g, rt, rb, kk, first, part = call(
-            start, "vvsv", [field, rows(N * N * N), rows(N * N), rows(2 * N * N, bf16, N * N), field, field], cost=10**9
-        )(rs, coef, stiffness, stiffness)
-        it, post, sums, to_e, to_w = call(
-            middle,
-            "svsvvvvvvvvvv",
-            [field, field, rows(2), rows(2 * N * N), rows(2 * N * N)],
-        )(where, coef, stiffness, g, rt, rb, kk, first, part, from_n, from_s, from_e, from_w)
+        table = rows(N * N * N)
+        g, rt, rb, kk, st, first, part = call(
+            start, "vvv", [field, table, table, rows(2 * N * N, bf16, N * N), table, field, field], cost=10**9
+        )(rs, coef, stiffness)
+        it, sums = call(middle, "v" * 11, [field, jax.ShapeDtypeStruct((ny * n_sub, 2, 128), f32)])(
+            masks, coef, g, rt, rb, first, part, from_n, from_s, from_e, from_w
+        )
+        near = lax.all_to_all(sums, ("y", "x", "c"), 0, 0)
+        post, to_e, to_w = call(smooth, "vvvvvv", [field, rows(2 * N * N), rows(2 * N * N)], cost=10**9)(
+            coef, st, g, rt, kk, it
+        )
         got_e, got_w = exchange(to_e, to_w, SUB, n_sub, True)
-        near = share(sums, ("y", "x", "c"), ny * n_sub).sum(0)
-        post, to_n, to_s = call(side, "vvvvvvvv", [field, rows((4 * N + 3) * N), rows((4 * N + 3) * N)])(
+        post, to_n, to_s, ready = call(
+            side, "vvvvvvvv", [field, rows((4 * N + 3) * N), rows((4 * N + 3) * N), rows(N)]
+        )(
             coef, rt, it, post, from_e, from_w, got_e, got_w
         )
+        (near,) = call(fold, "vv", [jax.ShapeDtypeStruct((nz, 2, 128), f32)])(near, ready)
+        ring = lax.all_to_all(near, "z", 0, 0)
         got_n, got_s = exchange(to_n, to_s, SFC, n_sfc, False)
-        ring = share(near, "z", nz)
 
         def last(*refs):
             finish(n_sfc, float(2 * n_sub * 128), *refs)
 
-        (out,) = call(
-            last, "svs" + "v" * 15, [field], [pltpu.VMEM((ROWS, 128), f32), pltpu.VMEM((ROWS, 128), f32)]
-        )(where, coef, stiffness, g, rt, rb, kk, it, post, ring, from_n, from_s, from_e, from_w, got_e, got_w, got_n, got_s)
+        (out,) = call(last, "v" * 18, [field], [pltpu.VMEM((ROWS, 128), f32), pltpu.VMEM((ROWS, 128), f32)])(
+            masks, coef, st, g, rt, rb, kk, it, post, ring, from_n, from_s, from_e, from_w, got_e, got_w, got_n, got_s
+        )
         return out.reshape(right_side.shape)
 
     field_spec = P(None, None, None, SFC, SUB, None)

time: 86.1 us -> 86.6 us (level)
  blocking collectives: 22.4 us -> 0 us
  starting transfers between devices: 37.5 us -> 53.7 us
  waiting for transfers between devices: 14.9 us -> 23.2 us
  local copies, waits for them, and re-layouts: 3.73 us -> 1.26 us
  Pallas kernels: 6.94 us -> 7.89 us
    all_to_all x1 -> x0, blocking collectives: 22.4 us -> none  [share(): lax.all_to_all(jnp.broadcast_to(block[None], (count, *block.shape)), axis...]
    all_to_all x1 -> x2, starting transfers between devices: 11.1 us -> 27.2 us  [the longest x1 16.1 us: per_device(): near = lax.all_to_all(sums, ('y', 'x', 'c'), 0, 0)]
    all_to_all x1 -> x2, waiting for transfers between devices: 10.5 us -> 20.6 us  [the longest x1 14.1 us: per_device(): ring = lax.all_to_all(near, 'z', 0, 0)]
    unnamed x8, local copies, waits for them, and re-layouts: 3.09 us -> 1.26 us
    ppermute x4, waiting for transfers between devices: 3.29 us -> 1.88 us  [exchange(): lax.ppermute(block_down, axis, down)]
    pallas_call x4 -> x6, Pallas kernels: 6.88 us -> 7.83 us  [the longest x1 2.49 us: per_device(): call(last, 'v' * 18, [field], [pltpu.VMEM((ROWS, 128), f32), pltpu.VMEM((...]
  transfers between devices with their start and end apart: 9 -> 10, of which waited for: 4 -> 4; matrix products, arithmetic and copies ran while one was open for 0% -> 0% of each run, Pallas kernels for 2% -> 2%
where the time goes in v2:
time: 86.6 us; the launch traced here: 86.3 us
  starting transfers between devices  53.7 us (62%)
  waiting for transfers between devices  23.2 us (27%)
  Pallas kernels  7.89 us (9%)
  local copies, waits for them, and re-layouts  1.26 us (1%)
    ppermute x4, starting transfers between devices, exchange(): lax.ppermute(block_down, axis, down)  17.9 us
    all_to_all x1, starting transfers between devices, per_device(): near = lax.all_to_all(sums, ('y', 'x', 'c'), 0, 0)  16.1 us
    all_to_all x1, waiting for transfers between devices, per_device(): ring = lax.all_to_all(near, 'z', 0, 0)  14.1 us
    all_to_all x1, starting transfers between devices, per_device(): ring = lax.all_to_all(near, 'z', 0, 0)  11.1 us
    ppermute x4, starting transfers between devices, exchange(): lax.ppermute(block_up, axis, up)  8.57 us
    all_to_all x1, waiting for transfers between devices, per_device(): near = lax.all_to_all(sums, ('y', 'x', 'c'), 0, 0)  6.5 us
    pallas_call x1, Pallas kernels, per_device(): call(last, 'v' * 18, [field], [pltpu.VMEM((ROWS, 128), f32), pltpu.VMEM((...  2.49 us
    ppermute x4, waiting for transfers between devices, exchange(): lax.ppermute(block_down, axis, down)  1.88 us
  transfers between devices with their start and end apart: 10, of which 4 were waited for; matrix products, arithmetic and copies ran while one was open for 0% of the time, Pallas kernels for 2%

profile of v2, /device:TPU:1, one launch (start us, length us, event | category | flops | bytes accessed | tf_op | source)
XLA Modules:
  0.0 86.3 jit_solution(14633001156762706197)
XLA Ops:
  0.0 0.0 copy-start
  0.0 1.8 %shard_map.38 = (f32[136,128]{1,0:T(8,128)}, f32[136,128]{1,0:T(8,128)}, f32[72,128]{1,0:T(8,128)}, f32[72,128]{1,0:T(8,128)}) custom-call(f32[1024,128]{1,0:T(8,128)} %bitcast.5, f32[2,128]{1,0:T(2,128)} %bitcast.7, f32[8,8]{1,0:T(8,128)} %sv_far.1), custom_call_target="tpu_custom_call" | custom-call | flops 1000000 | bytes 100000 | tf_op jit(solution)/shard_map/pallas_call | solution.py:434
  1.9 14.2 %collective-permute-start.2 = (f32[72,128]{1,0:T(8,128)}, f32[72,128]{1,0:T(8,128)S(1)}, u32[]{:S(2)}, u32[]{:S(2)}) collective-permute-start(f32[72,128]{1,0:T(8,128)} %get-tuple-element.34), channel_id=1, source_target_pairs={{1,0},{2,1},{3,2},{4,3},{5,4},{6,5},{7,6},{0,7},{9,8},{10,9},{11,1... | collective-permute-start | bytes 110600 | tf_op jit(solution)/shard_map/ppermute | solution.py:411
  16.0 0.0 collective-permute-start.3
  16.0 1.3 %collective-permute-start = (f32[136,128]{1,0:T(8,128)}, f32[136,128]{1,0:T(8,128)S(1)}, u32[]{:S(2)}, u32[]{:S(2)}) collective-permute-start(f32[136,128]{1,0:T(8,128)} %get-tuple-element.32), channel_id=1, source_target_pairs={{8,0},{16,8},{24,16},{32,24},{40,32},{48,40},{56,48},{64,56},{72,6... | collective-permute-start | bytes 208904 | tf_op jit(solution)/shard_map/ppermute | solution.py:411
  17.3 4.0 %collective-permute-start.1 = (f32[136,128]{1,0:T(8,128)}, f32[136,128]{1,0:T(8,128)S(1)}, u32[]{:S(2)}, u32[]{:S(2)}) collective-permute-start(f32[136,128]{1,0:T(8,128)} %get-tuple-element.33), channel_id=1, source_target_pairs={{0,8},{8,16},{16,24},{24,32},{32,40},{40,48},{48,56},{56,64},{64,7... | collective-permute-start | bytes 208904 | tf_op jit(solution)/shard_map/ppermute | solution.py:411
  21.3 0.0 copy-start.2
  21.4 0.0 copy-start.1
  21.4 0.1 fusion.1.masks.refs_0_
  21.4 0.0 copy-done
  21.4 0.6 copy-done.2
  22.0 0.0 copy-done.1
  22.0 1.4 %shard_map.37 = (f32[1024,128]{1,0:T(8,128)S(1)}, f32[512,128]{1,0:T(8,128)S(1)}, f32[512,128]{1,0:T(8,128)S(1)}, bf16[128,64]{1,0:T(8,128)(2,1)S(1)}, f32[512,1...) custom-call(f32[1024,128]{1,0:T(8,128)S(1)} %bitcast.6, f32[2,128]{1,0:T(2,128)S(1)} %bitcast.8, ...), custom_call_target="tpu_custom_call" | custom-call | flops 1000000000 | bytes 100000 | tf_op jit(solution)/shard_map/pallas_call | solution.py:449
  23.4 0.0 collective-permute-done.2.from_e.refs_12_
  23.4 0.0 collective-permute-done.3.from_w.refs_13_
  23.4 0.0 collective-permute-done.from_n.refs_10_
  23.4 0.0 collective-permute-done.1.from_s.refs_11_
  23.4 0.9 shard_map.39
  24.3 0.6 shard_map.40
  24.9 1.2 %collective-permute-start.4 = (f32[128,128]{1,0:T(8,128)S(1)}, f32[128,128]{1,0:T(8,128)S(1)}, u32[]{:S(2)}, u32[]{:S(2)}) collective-permute-start(f32[128,128]{1,0:T(8,128)S(1)} %get-tuple-element.38), channel_id=1, source_target_pairs={{1,0},{2,1},{3,2},{4,3},{5,4},{6,5},{7,6},{0,7},{9,8},{10,9},{11,1... | collective-permute-start | bytes 196616 | tf_op jit(solution)/shard_map/ppermute | solution.py:411
  26.1 0.6 collective-permute-start.5
  26.7 16.1 %all-to-all-start = ((f32[32,2,128]{2,1,0:T(2,128)}), f32[32,2,128]{2,1,0:T(2,128)S(1)}, u32[]{:S(2)}, u32[]{:S(2)}) async-start(f32[32,2,128]{2,1,0:T(2,128)} %get-tuple-element.41), calls=%async_computation | async-start | bytes 65536 | tf_op jit(solution)/shard_map/all_to_all | solution.py:455
  42.8 0.0 collective-permute-done.4.got_e.refs_14_
  42.8 0.0 collective-permute-done.5.got_w.refs_15_
  42.8 0.1 shard_map.41
  42.9 0.0 copy-start.3
  42.9 0.7 copy-done.3
  43.6 6.5 %all-to-all-done.parts = f32[32,2,128]{2,1,0:T(2,128)S(1)} async-done(((f32[32,2,128]{2,1,0:T(2,128)}), f32[32,2,128]{2,1,0:T(2,128)S(1)}, u32[]{:S(2)}, u32[]{:S(2)}) %all-to-all-start) | async-done | bytes 32800 | tf_op jit(solution)/shard_map/all_to_all | solution.py:455
  50.1 0.6 shard_map.42
  50.7 11.1 %all-to-all-start.1 = ((f32[32,2,128]{2,1,0:T(2,128)}), f32[32,2,128]{2,1,0:T(2,128)S(1)}, u32[]{:S(2)}, u32[]{:S(2)}) async-start(f32[32,2,128]{2,1,0:T(2,128)} %shard_map.42), calls=%async_computation.1 | async-start | bytes 65536 | tf_op jit(solution)/shard_map/all_to_all | solution.py:466
  61.8 1.3 %collective-permute-start.6 = (f32[280,128]{1,0:T(8,128)}, f32[280,128]{1,0:T(8,128)S(1)}, u32[]{:S(2)}, u32[]{:S(2)}) collective-permute-start(f32[280,128]{1,0:T(8,128)} %copy-done.3), channel_id=1, source_target_pairs={{8,0},{16,8},{24,16},{32,24},{40,32},{48,40},{56,48},{64,56},{72,6... | collective-permute-start | bytes 430088 | tf_op jit(solution)/shard_map/ppermute | solution.py:411
  63.1 4.0 %collective-permute-start.7 = (f32[280,128]{1,0:T(8,128)S(1)}, f32[280,128]{1,0:T(8,128)S(1)}, u32[]{:S(2)}, u32[]{:S(2)}) collective-permute-start(f32[280,128]{1,0:T(8,128)S(1)} %get-tuple-element.44), channel_id=1, source_target_pairs={{0,8},{8,16},{16,24},{24,32},{32,40},{40,48},{48,56},{56,64},{64,7... | collective-permute-start | bytes 430088 | tf_op jit(solution)/shard_map/ppermute | solution.py:411
  67.1 1.9 %collective-permute-done.6.refs_16_ = f32[280,128]{1,0:T(8,128)S(1)} collective-permute-done((f32[280,128]{1,0:T(8,128)}, f32[280,128]{1,0:T(8,128)S(1)}, u32[]{:S(2)}, u32[]{:S(2)}) %collective-permute-start.6) | collective-permute-done | bytes 143392 | tf_op jit(solution)/shard_map/ppermute | solution.py:411
  69.0 0.7 collective-permute-done.7.refs_17_
  69.7 14.1 %all-to-all-done.1.refs_9_ = f32[32,2,128]{2,1,0:T(2,128)S(1)} async-done(((f32[32,2,128]{2,1,0:T(2,128)}), f32[32,2,128]{2,1,0:T(2,128)S(1)}, u32[]{:S(2)}, u32[]{:S(2)}) %all-to-all-start.1) | async-done | bytes 32800 | tf_op jit(solution)/shard_map/all_to_all | solution.py:466
  83.8 2.5 %shard_map.43 = f32[1024,128]{1,0:T(8,128)} custom-call(f32[8,128]{1,0:T(8,128)S(1)} %fusion.1.masks.refs_0_, f32[2,128]{1,0:T(2,128)S(1)} %bitcast.12, f32[512,128]{1,0:T(8,128)S(1)} %get-tuple-element.25.st.refs_2_, f32[1024,128]{1,0:T(8,128)S(1)} %get-tuple-element.26.g.refs_3_, f32[512,128]{1,0:T(8,128)S(1)} %get-tuple-element.27.rt.refs_4_, ...), custom_call_target="tpu_custom_call" | custom-call | flops 1000000 | bytes 100000 | tf_op jit(solution)/shard_map/pallas_call | solution.py:472
  (2 shorter events, 0.0 us)
Async XLA Ops:
  0.0 21.4 %copy-start = (f32[8,8,8,1,2,128]{5,4,3,2,1,0:T(2,128)S(1)}, f32[8,8,8,1,2,128]{5,4,3,2,1,0:T(2,128)}, u32[]{:S(2)}) copy-start(f32[8,8,8,1,2,128]{5,4,3,2,1,0:T(2,128)} %param.3) | copy-start | bytes 1572868
  1.9 21.6 %collective-permute-start.2 = (f32[72,128]{1,0:T(8,128)}, f32[72,128]{1,0:T(8,128)S(1)}, u32[]{:S(2)}, u32[]{:S(2)}) collective-permute-start(f32[72,128]{1,0:T(8,128)} %get-tuple-element.34), channel_id=1, source_target_pairs={{1,0},{2,1},{3,2},{4,3},{5,4},{6,5},{7,6},{0,7},{9,8},{10,9},{11,1... | collective-permute-start | bytes 110600 | tf_op jit(solution)/shard_map/ppermute | solution.py:411
  16.0 7.4 %collective-permute-start.3 = (f32[72,128]{1,0:T(8,128)}, f32[72,128]{1,0:T(8,128)S(1)}, u32[]{:S(2)}, u32[]{:S(2)}) collective-permute-start(f32[72,128]{1,0:T(8,128)} %get-tuple-element.35), channel_id=1, source_target_pairs={{0,1},{1,2},{2,3},{3,4},{4,5},{5,6},{6,7},{7,0},{8,9},{9,10},{10,1... | collective-permute-start | bytes 110600 | tf_op jit(solution)/shard_map/ppermute | solution.py:411
  16.0 7.4 %collective-permute-start = (f32[136,128]{1,0:T(8,128)}, f32[136,128]{1,0:T(8,128)S(1)}, u32[]{:S(2)}, u32[]{:S(2)}) collective-permute-start(f32[136,128]{1,0:T(8,128)} %get-tuple-element.32), channel_id=1, source_target_pairs={{8,0},{16,8},{24,16},{32,24},{40,32},{48,40},{56,48},{64,56},{72,6... | collective-permute-start | bytes 208904 | tf_op jit(solution)/shard_map/ppermute | solution.py:411
  17.3 6.1 %collective-permute-start.1 = (f32[136,128]{1,0:T(8,128)}, f32[136,128]{1,0:T(8,128)S(1)}, u32[]{:S(2)}, u32[]{:S(2)}) collective-permute-start(f32[136,128]{1,0:T(8,128)} %get-tuple-element.33), channel_id=1, source_target_pairs={{0,8},{8,16},{16,24},{24,32},{32,40},{40,48},{48,56},{56,64},{64,7... | collective-permute-start | bytes 208904 | tf_op jit(solution)/shard_map/ppermute | solution.py:411
  21.3 0.7 copy-start.2
  21.4 0.7 copy-start.1
  24.9 17.9 %collective-permute-start.4 = (f32[128,128]{1,0:T(8,128)S(1)}, f32[128,128]{1,0:T(8,128)S(1)}, u32[]{:S(2)}, u32[]{:S(2)}) collective-permute-start(f32[128,128]{1,0:T(8,128)S(1)} %get-tuple-element.38), channel_id=1, source_target_pairs={{1,0},{2,1},{3,2},{4,3},{5,4},{6,5},{7,6},{0,7},{9,8},{10,9},{11,1... | collective-permute-start | bytes 196616 | tf_op jit(solution)/shard_map/ppermute | solution.py:411
  26.1 16.7 %collective-permute-start.5 = (f32[128,128]{1,0:T(8,128)S(1)}, f32[128,128]{1,0:T(8,128)S(1)}, u32[]{:S(2)}, u32[]{:S(2)}) collective-permute-start(f32[128,128]{1,0:T(8,128)S(1)} %get-tuple-element.39), channel_id=1, source_target_pairs={{0,1},{1,2},{2,3},{3,4},{4,5},{5,6},{6,7},{7,0},{8,9},{9,10},{10,1... | collective-permute-start | bytes 196616 | tf_op jit(solution)/shard_map/ppermute | solution.py:411
  26.7 23.4 %all-to-all-start = ((f32[32,2,128]{2,1,0:T(2,128)}), f32[32,2,128]{2,1,0:T(2,128)S(1)}, u32[]{:S(2)}, u32[]{:S(2)}) async-start(f32[32,2,128]{2,1,0:T(2,128)} %get-tuple-element.41), calls=%async_computation | async-start | bytes 65536 | tf_op jit(solution)/shard_map/all_to_all | solution.py:455
  42.9 0.7 copy-start.3
  50.7 33.1 %all-to-all-start.1 = ((f32[32,2,128]{2,1,0:T(2,128)}), f32[32,2,128]{2,1,0:T(2,128)S(1)}, u32[]{:S(2)}, u32[]{:S(2)}) async-start(f32[32,2,128]{2,1,0:T(2,128)} %shard_map.42), calls=%async_computation.1 | async-start | bytes 65536 | tf_op jit(solution)/shard_map/all_to_all | solution.py:466
  61.8 7.2 %collective-permute-start.6 = (f32[280,128]{1,0:T(8,128)}, f32[280,128]{1,0:T(8,128)S(1)}, u32[]{:S(2)}, u32[]{:S(2)}) collective-permute-start(f32[280,128]{1,0:T(8,128)} %copy-done.3), channel_id=1, source_target_pairs={{8,0},{16,8},{24,16},{32,24},{40,32},{48,40},{56,48},{64,56},{72,6... | collective-permute-start | bytes 430088 | tf_op jit(solution)/shard_map/ppermute | solution.py:411
  63.1 6.5 %collective-permute-start.7 = (f32[280,128]{1,0:T(8,128)S(1)}, f32[280,128]{1,0:T(8,128)S(1)}, u32[]{:S(2)}, u32[]{:S(2)}) collective-permute-start(f32[280,128]{1,0:T(8,128)S(1)} %get-tuple-element.44), channel_id=1, source_target_pairs={{0,8},{8,16},{16,24},{24,32},{32,40},{40,48},{48,56},{56,64},{64,7... | collective-permute-start | bytes 430088 | tf_op jit(solution)/shard_map/ppermute | solution.py:411

commit v3 on v2

--- a/solution.py
+++ b/solution.py
@@ -25,6 +25,28 @@
 SUB = ("x", "c")
 
 
+class Either:
+    def __init__(self, cond, one, other):
+        self.cond, self.one, self.other = cond, one, other
+
+    def __getitem__(self, key):
+        return jnp.where(self.cond, self.one[key], self.other[key])
+
+
+def both_sides(cond, swap_a, swap_b):
+    return Either(cond, swap_a, swap_b), Either(cond, swap_b, swap_a)
+
+
+def put_both(cond, swap_a, swap_b, t, to_next, to_prev):
+    put(swap_a, t, jnp.where(cond, to_next, to_prev))
+    put(swap_b, t, jnp.where(cond, to_prev, to_next))
+
+
+def position():
+    plane = lax.axis_index("y") * lax.axis_size("z") + lax.axis_index("z")
+    return plane, lax.rem(lax.axis_index("z"), 2) == 0, lax.axis_index("c") == 0
+
+
 def tile(ref, t):
     return ref[pl.ds(t * N, N), :]
 
@@ -59,7 +81,7 @@
     return ref[pl.ds(at(0, a, b) * 2 * N + q, N, stride=2), :]
 
 
-def pack_first(rs_far, coef_far, sv_far, to_n, to_s, to_e, to_w, rs, coef, sv, sems):
+def pack_first(rs_far, coef_far, sv_far, plane_a, plane_b, span_a, span_b, rs, coef, sv, sems):
     copies = [
         pltpu.make_async_copy(src, dst, sems.at[k])
         for k, (src, dst) in enumerate(((sv_far, sv), (coef_far, coef), (rs_far, rs)))
@@ -79,17 +101,15 @@
     def value(q, a, b):
         return raw(rs, q, a, b) * scale[q] / ((line(mc, a) + line(mc, b)) + mc)
 
+    _, even_plane, even_span = position()
     for q in range(2):
         for b in range(N):
-            put(to_n, q * N + b, value(q, N - 1, b))
-            put(to_s, q * N + b, value(q, 0, b))
-    put(to_n, 2 * N, both)
-    put(to_s, 2 * N, both)
-    for a in range(N):
-        put(to_e, a, value(1, a, N - 1))
-        put(to_w, a, value(0, a, 0))
-    put(to_e, N, zero + c[1])
-    put(to_w, N, zero + c[0])
+            put_both(even_plane, plane_a, plane_b, q * N + b, value(q, N - 1, b), value(q, 0, b))
+    put(plane_a, 2 * N, both)
+    put(plane_b, 2 * N, both)
+    for a in range(N):
+        put_both(even_span, span_a, span_b, a, value(1, a, N - 1), value(0, a, 0))
+    put_both(even_span, span_a, span_b, N, zero + c[1], zero + c[0])
 
 
 def stiff(u, kk, st, acc):
@@ -186,7 +206,10 @@
             set_block(part, q, a, v)
 
 
-def middle(masks, coef, g, rt, rb, first, part, from_n, from_s, from_e, from_w, it, sums_out):
+def middle(coef, g, rt, rb, first, part, plane_a, plane_b, span_a, span_b, it, sums_out):
+    plane, even_plane, even_span = position()
+    from_n, from_s = both_sides(even_plane, plane_a, plane_b)
+    from_e, from_w = both_sides(even_span, span_a, span_b)
     c = [coef[pl.ds(q, 1), :] for q in range(2)]
     it[...] = part[...]
     wn = [2.0 + 2.0 * from_n[pl.ds(2 * N * N + q, 1), :] / c[q] for q in range(2)]
@@ -234,25 +257,25 @@
     stack = jnp.where(sub == 2, total(below), stack)
     stack = jnp.where(sub == 3, c[0] + c[1], stack)
     s = jnp.sum(stack, axis=1, keepdims=True)
-    here = masks[pl.ds(0, 1), :]
-    means = here * s[0:1] + masks[pl.ds(1, 1), :] * s[1:2] + masks[pl.ds(2, 1), :] * s[2:3]
+    lane = lax.broadcasted_iota(jnp.int32, (1, 128), 1)
+    means = jnp.where(lane == plane, s[0:1], 0.0)
+    means = means + jnp.where(lane == plane + 1, s[1:2], 0.0) + jnp.where(lane == plane - 1, s[2:3], 0.0)
     sub2 = lax.broadcasted_iota(jnp.int32, (2, 128), 0)
-    pair = jnp.where(sub2 == 0, means, here * s[3:4])
+    pair = jnp.where(sub2 == 0, means, jnp.where(lane == plane, s[3:4], 0.0))
     sums_out[...] = jnp.broadcast_to(pair[None], sums_out.shape)
 
 
-def smooth(coef, st, g, rt, kk, it, post, to_e, to_w):
+def smooth(coef, st, g, rt, kk, it, post, span_a, span_b):
     stiff(it, kk, st, post)
     inner_faces(it, coef, post)
     for q in range(2):
         for a in range(N):
             r = rt[pl.ds(a * N * N, N * N), :] * (1.0 / centre)
             set_block(post, q, a, block(it, q, a) + r * (block(g, q, a) - block(post, q, a)))
-    for a in range(N):
-        put(to_e, a, tile(it, at(1, a, N - 1)))
-        put(to_e, N + a, tile(post, at(1, a, N - 1)))
-        put(to_w, a, tile(it, at(0, a, 0)))
-        put(to_w, N + a, tile(post, at(0, a, 0)))
+    _, _, even_span = position()
+    for a in range(N):
+        for k, field in enumerate((it, post)):
+            put_both(even_span, span_a, span_b, k * N + a, tile(field, at(1, a, N - 1)), tile(field, at(0, a, 0)))
 
 
 def fold(parts, ready, out):
@@ -262,7 +285,10 @@
     out[...] = jnp.broadcast_to(total[None], out.shape)
 
 
-def side(coef, rt, it, post_in, from_e, from_w, got_e, got_w, post, to_n, to_s, ready):
+def side(coef, rt, it, post_in, span_a, span_b, far_a, far_b, post, plane_a, plane_b, ready):
+    _, even_plane, even_span = position()
+    from_e, from_w = both_sides(even_span, span_a, span_b)
+    got_e, got_w = both_sides(even_span, far_a, far_b)
     c = [coef[pl.ds(q, 1), :] for q in range(2)]
     ce = from_e[pl.ds(N * N, 1), :]
     cw = from_w[pl.ds(N * N, 1), :]
@@ -276,14 +302,15 @@
             put(post, k, tile(post, k) - r * (w * (tile(it, k) - tile(got, a))))
     sub = lax.broadcasted_iota(jnp.int32, (N, 128), 0)
     outer = jnp.where(sub == 0, ce, jnp.where(sub == 1, cw, 0.0))
-    for a, to in ((N - 1, to_n), (0, to_s)):
-        for q in range(2):
-            for b in range(N):
-                put(to, q * N + b, tile(it, at(q, a, b)))
-                put(to, 2 * N + q * N + b, tile(post, at(q, a, b)))
-        put(to, 4 * N, tile(got_e, a))
-        put(to, 4 * N + 1, tile(got_w, a))
-        put(to, 4 * N + 2, outer)
+    for q in range(2):
+        for b in range(N):
+            for k, field in enumerate((it, post)):
+                up, down = tile(field, at(q, N - 1, b)), tile(field, at(q, 0, b))
+                put_both(even_plane, plane_a, plane_b, 2 * N * k + q * N + b, up, down)
+    for k, got in enumerate((got_e, got_w)):
+        put_both(even_plane, plane_a, plane_b, 4 * N + k, tile(got, N - 1), tile(got, 0))
+    put(plane_a, 4 * N + 2, outer)
+    put(plane_b, 4 * N + 2, outer)
     ready[...] = jnp.zeros((N, 128), f32)
 
 
@@ -308,18 +335,25 @@
     return right / diag
 
 
-def finish(planes, per_plane, masks, coef, st, g, rt, rb, kk, it, post, ring, from_n, from_s, from_e, from_w, got_e, got_w, got_n, got_s, out, acc, v):
+def finish(planes, per_plane, coef, st, g, rt, rb, kk, it, post, ring, near_a, near_b, span_a, span_b, far_a, far_b, last_a, last_b, out, acc, v):
+    plane, even_plane, even_span = position()
+    from_n, from_s = both_sides(even_plane, near_a, near_b)
+    from_e, from_w = both_sides(even_span, span_a, span_b)
+    got_e, got_w = both_sides(even_span, far_a, far_b)
+    got_n, got_s = both_sides(even_plane, last_a, last_b)
     scaled = ring[0]
     for k in range(1, ring.shape[0]):
         scaled = scaled + ring[k]
     corr = coarse(planes, scaled[1:2] * (1.0 / per_plane), scaled[0:1] * (1.0 / (per_plane * N * N * N)))
 
+    lane = lax.broadcasted_iota(jnp.int32, (1, 128), 1)
+
     def pick(k):
-        return jnp.sum(masks[pl.ds(k, 1), :] * corr, axis=1, keepdims=True) + jnp.zeros((1, 128), f32)
-
-    mid, high, low = pick(0), pick(1), pick(2)
-    has_n = masks[pl.ds(3, 1), :]
-    has_s = masks[pl.ds(4, 1), :]
+        return jnp.sum(jnp.where(lane == k, corr, 0.0), axis=1, keepdims=True) + jnp.zeros((1, 128), f32)
+
+    mid, high, low = pick(plane), pick(plane + 1), pick(plane - 1)
+    has_n = (plane < planes - 1).astype(f32)
+    has_s = (plane > 0).astype(f32)
     inner = 1.0 / centre
     c = [coef[pl.ds(q, 1), :] for q in range(2)]
     cn = [from_n[pl.ds(2 * N * N + q, 1), :] for q in range(2)]
@@ -403,20 +437,13 @@
     return jax.ShapeDtypeStruct((n, lanes), dtype)
 
 
-def exchange(block_up, block_down, axis, count, periodic):
-    up = [(i, i + 1) for i in range(count - 1)]
+def swap(block_a, block_b, axis, count, periodic):
+    first = [(i, i ^ 1) for i in range(count)]
+    second = [(i, i + 1) for i in range(1, count - 1, 2)]
     if periodic:
-        up.append((count - 1, 0))
-    down = [(j, i) for i, j in up]
-    return lax.ppermute(block_down, axis, down), lax.ppermute(block_up, axis, up)
-
-
-def place_masks(place, planes):
-    lane = jnp.arange(128)[None, :]
-    k = jnp.arange(8)[:, None]
-    hot = jnp.where(k == 0, place, jnp.where(k == 1, place + 1, place - 1))
-    has = jnp.where(k == 3, place < planes - 1, place > 0)
-    return jnp.where(k < 3, lane == hot, has).astype(f32)
+        second.append((count - 1, 0))
+    second = second + [(j, i) for i, j in second]
+    return lax.ppermute(block_a, axis, first), lax.ppermute(block_b, axis, second)
 
 
 def solution(mesh):
@@ -428,10 +455,9 @@
     def per_device(right_side, coefficient, stiffness):
         rs = right_side.reshape(ROWS, 128)
         coef = coefficient.reshape(2, 128)
-        masks = place_masks(lax.axis_index(SFC), n_sfc)
         field = rows(ROWS)
         layer, strip = rows((2 * N + 1) * N), rows((N + 1) * N)
-        to_n, to_s, to_e, to_w = call(
+        planes_out = call(
             pack_first,
             "hhh",
             [layer, layer, strip, strip],
@@ -441,36 +467,34 @@
                 pltpu.VMEM((N, N), f32),
                 pltpu.SemaphoreType.DMA((3,)),
             ],
-            vmem=60,
-        )(rs, coef, stiffness)
-        from_n, from_s = exchange(to_n, to_s, SFC, n_sfc, False)
-        from_e, from_w = exchange(to_e, to_w, SUB, n_sub, True)
+        )(*(pltpu.with_memory_space_constraint(x, pltpu.HBM) for x in (rs, coef, stiffness)))
+        near_planes = swap(*planes_out[:2], SFC, n_sfc, False)
+        near_spans = swap(*planes_out[2:], SUB, n_sub, True)
         table = rows(N * N * N)
         g, rt, rb, kk, st, first, part = call(
             start, "vvv", [field, table, table, rows(2 * N * N, bf16, N * N), table, field, field], cost=10**9
         )(rs, coef, stiffness)
-        it, sums = call(middle, "v" * 11, [field, jax.ShapeDtypeStruct((ny * n_sub, 2, 128), f32)])(
-            masks, coef, g, rt, rb, first, part, from_n, from_s, from_e, from_w
+        it, sums = call(middle, "v" * 10, [field, jax.ShapeDtypeStruct((ny * n_sub, 2, 128), f32)])(
+            coef, g, rt, rb, first, part, *near_planes, *near_spans
         )
         near = lax.all_to_all(sums, ("y", "x", "c"), 0, 0)
-        post, to_e, to_w = call(smooth, "vvvvvv", [field, rows(2 * N * N), rows(2 * N * N)], cost=10**9)(
+        post, *spans_out = call(smooth, "vvvvvv", [field, rows(2 * N * N), rows(2 * N * N)], cost=10**9)(
             coef, st, g, rt, kk, it
         )
-        got_e, got_w = exchange(to_e, to_w, SUB, n_sub, True)
-        post, to_n, to_s, ready = call(
-            side, "vvvvvvvv", [field, rows((4 * N + 3) * N), rows((4 * N + 3) * N), rows(N)]
-        )(
-            coef, rt, it, post, from_e, from_w, got_e, got_w
+        far_spans = swap(*spans_out, SUB, n_sub, True)
+        tall = rows((4 * N + 3) * N)
+        post, *planes_out, ready = call(side, "v" * 8, [field, tall, tall, rows(N)])(
+            coef, rt, it, post, *near_spans, *far_spans
         )
         (near,) = call(fold, "vv", [jax.ShapeDtypeStruct((nz, 2, 128), f32)])(near, ready)
         ring = lax.all_to_all(near, "z", 0, 0)
-        got_n, got_s = exchange(to_n, to_s, SFC, n_sfc, False)
+        far_planes = swap(*planes_out, SFC, n_sfc, False)
 
         def last(*refs):
             finish(n_sfc, float(2 * n_sub * 128), *refs)
 
-        (out,) = call(last, "v" * 18, [field], [pltpu.VMEM((ROWS, 128), f32), pltpu.VMEM((ROWS, 128), f32)])(
-            masks, coef, st, g, rt, rb, kk, it, post, ring, from_n, from_s, from_e, from_w, got_e, got_w, got_n, got_s
+        (out,) = call(last, "v" * 17, [field], [pltpu.VMEM((ROWS, 128), f32), pltpu.VMEM((ROWS, 128), f32)])(
+            coef, st, g, rt, rb, kk, it, post, ring, *near_planes, *near_spans, *far_spans, *far_planes
         )
         return out.reshape(right_side.shape)
 

time: 86.6 us -> 93.5 us (1.080)
  starting transfers between devices: 53.7 us -> 58.5 us
  waiting for transfers between devices: 23.2 us -> 26.4 us
    ppermute x8, starting transfers between devices: 26.5 us -> 30.4 us  [the longest x4 23.8 us: swap(): lax.ppermute(block_a, axis, first)]
    all_to_all x1, starting transfers between devices: 11.1 us -> 14.9 us  [per_device(): ring = lax.all_to_all(near, 'z', 0, 0)]
    all_to_all x1, starting transfers between devices: 16.1 us -> 13.2 us  [per_device(): near = lax.all_to_all(sums, ('y', 'x', 'c'), 0, 0)]
    ppermute x8, waiting for transfers between devices: 2.56 us -> 5.05 us  [the longest x4 5.04 us: swap(): lax.ppermute(block_a, axis, first)]
where the time goes in v3:
time: 93.5 us; the launch traced here: 93.1 us
  starting transfers between devices  58.5 us (63%)
  waiting for transfers between devices  26.4 us (28%)
  Pallas kernels  7.26 us (8%)
    ppermute x4, starting transfers between devices, swap(): lax.ppermute(block_a, axis, first)  23.8 us
    all_to_all x1, starting transfers between devices, per_device(): ring = lax.all_to_all(near, 'z', 0, 0)  14.9 us
    all_to_all x1, waiting for transfers between devices, per_device(): ring = lax.all_to_all(near, 'z', 0, 0)  14.9 us
    all_to_all x1, starting transfers between devices, per_device(): near = lax.all_to_all(sums, ('y', 'x', 'c'), 0, 0)  13.2 us
    ppermute x4, starting transfers between devices, swap(): lax.ppermute(block_b, axis, second)  6.62 us
    all_to_all x1, waiting for transfers between devices, per_device(): near = lax.all_to_all(sums, ('y', 'x', 'c'), 0, 0)  6.5 us
    ppermute x4, waiting for transfers between devices, swap(): lax.ppermute(block_a, axis, first)  5.04 us
    pallas_call x1, Pallas kernels, per_device(): call(last, 'v' * 17, [field], [pltpu.VMEM((ROWS, 128), f32), pltpu.VMEM((...  2.51 us
  transfers between devices with their start and end apart: 10, of which 4 were waited for; matrix products, arithmetic and copies ran while one was open for 0% of the time, Pallas kernels for 2%

profile of v3, /device:TPU:1, one launch (start us, length us, event | category | flops | bytes accessed | tf_op | source)
XLA Modules:
  0.0 93.1 jit_solution(806420624897278788)
XLA Ops:
  0.0 0.0 copy-start
  0.0 1.2 %shard_map.38 = (f32[136,128]{1,0:T(8,128)S(1)}, f32[136,128]{1,0:T(8,128)S(1)}, f32[72,128]{1,0:T(8,128)S(1)}, f32[72,128]{1,0:T(8,128)S(1)}) custom-call(f32[1024,128]{1,0:T(8,128)} %bitcast.5, f32[2,128]{1,0:T(2,128)} %bitcast.7, f32[8,8]{1,0:T(8,128)} %sv_far.1), custom_call_target="tpu_custom_call" | custom-call | flops 1000000 | bytes 100000 | tf_op jit(solution)/shard_map/pallas_call | solution.py:460
  1.2 0.0 copy-start.2
  1.2 16.1 %collective-permute-start.2 = (f32[72,128]{1,0:T(8,128)S(1)}, f32[72,128]{1,0:T(8,128)S(1)}, u32[]{:S(2)}, u32[]{:S(2)}) collective-permute-start(f32[72,128]{1,0:T(8,128)S(1)} %get-tuple-element.34), channel_id=1, source_target_pairs={{0,1},{1,0},{2,3},{3,2},{4,5},{5,4},{6,7},{7,6},{8,9},{9,8},{10,11... | collective-permute-start | bytes 110600 | tf_op jit(solution)/shard_map/ppermute | solution.py:446
  17.3 1.9 %collective-permute-start.3 = (f32[72,128]{1,0:T(8,128)S(1)}, f32[72,128]{1,0:T(8,128)S(1)}, u32[]{:S(2)}, u32[]{:S(2)}) collective-permute-start(f32[72,128]{1,0:T(8,128)S(1)} %get-tuple-element.35), channel_id=1, source_target_pairs={{1,2},{3,4},{5,6},{7,0},{2,1},{4,3},{6,5},{0,7},{9,10},{11,12},{13... | collective-permute-start | bytes 110600 | tf_op jit(solution)/shard_map/ppermute | solution.py:446
  19.2 0.0 copy-start.1
  19.2 1.9 %collective-permute-start = (f32[136,128]{1,0:T(8,128)S(1)}, f32[136,128]{1,0:T(8,128)S(1)}, u32[]{:S(2)}, u32[]{:S(2)}) collective-permute-start(f32[136,128]{1,0:T(8,128)S(1)} %get-tuple-element.32), channel_id=1, source_target_pairs={{0,8},{8,0},{16,24},{24,16},{32,40},{40,32},{48,56},{56,48},{64,72... | collective-permute-start | bytes 208904 | tf_op jit(solution)/shard_map/ppermute | solution.py:446
  21.1 0.7 collective-permute-start.1
  21.8 0.0 copy-done
  21.8 0.0 copy-done.2
  21.8 0.0 copy-done.1
  21.9 1.3 %shard_map.37 = (f32[1024,128]{1,0:T(8,128)S(1)}, f32[512,128]{1,0:T(8,128)S(1)}, f32[512,128]{1,0:T(8,128)S(1)}, bf16[128,64]{1,0:T(8,128)(2,1)S(1)}, f32[512,1...) custom-call(f32[1024,128]{1,0:T(8,128)S(1)} %bitcast.6, f32[2,128]{1,0:T(2,128)S(1)} %bitcast.8, ...), custom_call_target="tpu_custom_call" | custom-call | flops 1000000000 | bytes 100000 | tf_op jit(solution)/shard_map/pallas_call | solution.py:474
  23.2 0.0 collective-permute-done.2.span_a.refs_11_
  23.2 0.0 collective-permute-done.3.span_b.refs_12_
  23.2 1.7 %collective-permute-done.plane_a.refs_9_ = f32[136,128]{1,0:T(8,128)S(1)} collective-permute-done((f32[136,128]{1,0:T(8,128)S(1)}, f32[136,128]{1,0:T(8,128)S(1)}, u32[]{:S(2)}, u32[]{:S(2)}) %collective-permute-start) | collective-permute-done | bytes 69664 | tf_op jit(solution)/shard_map/ppermute | solution.py:446
  24.9 0.0 collective-permute-done.1.plane_b.refs_10_
  24.9 0.9 shard_map.39
  25.8 0.6 shard_map.40
  26.4 2.7 %collective-permute-start.4 = (f32[128,128]{1,0:T(8,128)S(1)}, f32[128,128]{1,0:T(8,128)S(1)}, u32[]{:S(2)}, u32[]{:S(2)}) collective-permute-start(f32[128,128]{1,0:T(8,128)S(1)} %get-tuple-element.38), channel_id=1, source_target_pairs={{0,1},{1,0},{2,3},{3,2},{4,5},{5,4},{6,7},{7,6},{8,9},{9,8},{10,11... | collective-permute-start | bytes 196616 | tf_op jit(solution)/shard_map/ppermute | solution.py:446
  29.1 3.4 %collective-permute-start.5 = (f32[128,128]{1,0:T(8,128)S(1)}, f32[128,128]{1,0:T(8,128)S(1)}, u32[]{:S(2)}, u32[]{:S(2)}) collective-permute-start(f32[128,128]{1,0:T(8,128)S(1)} %get-tuple-element.39), channel_id=1, source_target_pairs={{1,2},{3,4},{5,6},{7,0},{2,1},{4,3},{6,5},{0,7},{9,10},{11,12},{13... | collective-permute-start | bytes 196616 | tf_op jit(solution)/shard_map/ppermute | solution.py:446
  32.5 13.2 %all-to-all-start = ((f32[32,2,128]{2,1,0:T(2,128)}), f32[32,2,128]{2,1,0:T(2,128)S(1)}, u32[]{:S(2)}, u32[]{:S(2)}) async-start(f32[32,2,128]{2,1,0:T(2,128)} %get-tuple-element.41), calls=%async_computation | async-start | bytes 65536 | tf_op jit(solution)/shard_map/all_to_all | solution.py:480
  45.7 0.0 collective-permute-done.4.far_a.refs_13_
  45.7 0.0 collective-permute-done.5.far_b.refs_14_
  45.7 0.1 shard_map.41
  45.8 0.0 copy-start.3
  45.8 0.7 copy-done.3
  46.5 6.5 %all-to-all-done.parts = f32[32,2,128]{2,1,0:T(2,128)S(1)} async-done(((f32[32,2,128]{2,1,0:T(2,128)}), f32[32,2,128]{2,1,0:T(2,128)S(1)}, u32[]{:S(2)}, u32[]{:S(2)}) %all-to-all-start) | async-done | bytes 32800 | tf_op jit(solution)/shard_map/all_to_all | solution.py:480
  53.0 0.7 shard_map.42
  53.6 14.9 %all-to-all-start.1 = ((f32[32,2,128]{2,1,0:T(2,128)}), f32[32,2,128]{2,1,0:T(2,128)S(1)}, u32[]{:S(2)}, u32[]{:S(2)}) async-start(f32[32,2,128]{2,1,0:T(2,128)} %shard_map.42), calls=%async_computation.1 | async-start | bytes 65536 | tf_op jit(solution)/shard_map/all_to_all | solution.py:490
  68.5 3.1 %collective-permute-start.6 = (f32[280,128]{1,0:T(8,128)}, f32[280,128]{1,0:T(8,128)S(1)}, u32[]{:S(2)}, u32[]{:S(2)}) collective-permute-start(f32[280,128]{1,0:T(8,128)} %copy-done.3), channel_id=1, source_target_pairs={{0,8},{8,0},{16,24},{24,16},{32,40},{40,32},{48,56},{56,48},{64,72... | collective-permute-start | bytes 430088 | tf_op jit(solution)/shard_map/ppermute | solution.py:446
  71.7 0.7 collective-permute-start.7
  72.4 3.3 %collective-permute-done.6.refs_15_ = f32[280,128]{1,0:T(8,128)S(1)} collective-permute-done((f32[280,128]{1,0:T(8,128)}, f32[280,128]{1,0:T(8,128)S(1)}, u32[]{:S(2)}, u32[]{:S(2)}) %collective-permute-start.6) | collective-permute-done | bytes 143392 | tf_op jit(solution)/shard_map/ppermute | solution.py:446
  75.7 0.0 collective-permute-done.7.refs_16_
  75.7 14.9 %all-to-all-done.1.refs_8_ = f32[32,2,128]{2,1,0:T(2,128)S(1)} async-done(((f32[32,2,128]{2,1,0:T(2,128)}), f32[32,2,128]{2,1,0:T(2,128)S(1)}, u32[]{:S(2)}, u32[]{:S(2)}) %all-to-all-start.1) | async-done | bytes 32800 | tf_op jit(solution)/shard_map/all_to_all | solution.py:490
  90.6 2.5 %shard_map.43 = f32[1024,128]{1,0:T(8,128)} custom-call(f32[2,128]{1,0:T(2,128)S(1)} %bitcast.12, f32[512,128]{1,0:T(8,128)S(1)} %get-tuple-element.25.st.refs_1_, f32[1024,128]{1,0:T(8,128)S(1)} %get-tuple-element.26.g.refs_2_, f32[512,128]{1,0:T(8,128)S(1)} %get-tuple-element.27.rt.refs_3_, f32[512,128]{1,0:T(8,128)S(1)} %get-tuple-element.28.rb.refs_4_, ...), custom_call_target="tpu_custom_call" | custom-call | flops 1000000 | bytes 100000 | tf_op jit(solution)/shard_map/pallas_call | solution.py:496
Async XLA Ops:
  0.0 21.8 %copy-start = (f32[8,8,8,1,2,128]{5,4,3,2,1,0:T(2,128)S(1)}, f32[8,8,8,1,2,128]{5,4,3,2,1,0:T(2,128)}, u32[]{:S(2)}) copy-start(f32[8,8,8,1,2,128]{5,4,3,2,1,0:T(2,128)} %param.3) | copy-start | bytes 1572868
  1.2 20.6 %copy-start.2 = (f32[8,8]{1,0:T(8,128)S(1)}, f32[8,8]{1,0:T(8,128)}, u32[]{:S(2)}) copy-start(f32[8,8]{1,0:T(8,128)} %sv_far.1) | copy-start | bytes 772
  1.2 22.0 %collective-permute-start.2 = (f32[72,128]{1,0:T(8,128)S(1)}, f32[72,128]{1,0:T(8,128)S(1)}, u32[]{:S(2)}, u32[]{:S(2)}) collective-permute-start(f32[72,128]{1,0:T(8,128)S(1)} %get-tuple-element.34), channel_id=1, source_target_pairs={{0,1},{1,0},{2,3},{3,2},{4,5},{5,4},{6,7},{7,6},{8,9},{9,8},{10,11... | collective-permute-start | bytes 110600 | tf_op jit(solution)/shard_map/ppermute | solution.py:446
  17.3 5.9 %collective-permute-start.3 = (f32[72,128]{1,0:T(8,128)S(1)}, f32[72,128]{1,0:T(8,128)S(1)}, u32[]{:S(2)}, u32[]{:S(2)}) collective-permute-start(f32[72,128]{1,0:T(8,128)S(1)} %get-tuple-element.35), channel_id=1, source_target_pairs={{1,2},{3,4},{5,6},{7,0},{2,1},{4,3},{6,5},{0,7},{9,10},{11,12},{13... | collective-permute-start | bytes 110600 | tf_op jit(solution)/shard_map/ppermute | solution.py:446
  19.2 2.6 %copy-start.1 = (f32[1,2,128]{2,1,0:T(2,128)S(1)}, f32[1,2,128]{2,1,0:T(2,128)}, u32[]{:S(2)}) copy-start(f32[1,2,128]{2,1,0:T(2,128)} %param.4) | copy-start | bytes 3076
  19.2 5.7 %collective-permute-start = (f32[136,128]{1,0:T(8,128)S(1)}, f32[136,128]{1,0:T(8,128)S(1)}, u32[]{:S(2)}, u32[]{:S(2)}) collective-permute-start(f32[136,128]{1,0:T(8,128)S(1)} %get-tuple-element.32), channel_id=1, source_target_pairs={{0,8},{8,0},{16,24},{24,16},{32,40},{40,32},{48,56},{56,48},{64,72... | collective-permute-start | bytes 208904 | tf_op jit(solution)/shard_map/ppermute | solution.py:446
  21.1 3.8 %collective-permute-start.1 = (f32[136,128]{1,0:T(8,128)S(1)}, f32[136,128]{1,0:T(8,128)S(1)}, u32[]{:S(2)}, u32[]{:S(2)}) collective-permute-start(f32[136,128]{1,0:T(8,128)S(1)} %get-tuple-element.33), channel_id=1, source_target_pairs={{8,16},{24,32},{40,48},{56,64},{72,80},{88,96},{104,112},{120,128}... | collective-permute-start | bytes 208904 | tf_op jit(solution)/shard_map/ppermute | solution.py:446
  26.4 19.3 %collective-permute-start.4 = (f32[128,128]{1,0:T(8,128)S(1)}, f32[128,128]{1,0:T(8,128)S(1)}, u32[]{:S(2)}, u32[]{:S(2)}) collective-permute-start(f32[128,128]{1,0:T(8,128)S(1)} %get-tuple-element.38), channel_id=1, source_target_pairs={{0,1},{1,0},{2,3},{3,2},{4,5},{5,4},{6,7},{7,6},{8,9},{9,8},{10,11... | collective-permute-start | bytes 196616 | tf_op jit(solution)/shard_map/ppermute | solution.py:446
  29.1 16.6 %collective-permute-start.5 = (f32[128,128]{1,0:T(8,128)S(1)}, f32[128,128]{1,0:T(8,128)S(1)}, u32[]{:S(2)}, u32[]{:S(2)}) collective-permute-start(f32[128,128]{1,0:T(8,128)S(1)} %get-tuple-element.39), channel_id=1, source_target_pairs={{1,2},{3,4},{5,6},{7,0},{2,1},{4,3},{6,5},{0,7},{9,10},{11,12},{13... | collective-permute-start | bytes 196616 | tf_op jit(solution)/shard_map/ppermute | solution.py:446
  32.5 20.4 %all-to-all-start = ((f32[32,2,128]{2,1,0:T(2,128)}), f32[32,2,128]{2,1,0:T(2,128)S(1)}, u32[]{:S(2)}, u32[]{:S(2)}) async-start(f32[32,2,128]{2,1,0:T(2,128)} %get-tuple-element.41), calls=%async_computation | async-start | bytes 65536 | tf_op jit(solution)/shard_map/all_to_all | solution.py:480
  45.8 0.7 copy-start.3
  53.6 37.0 %all-to-all-start.1 = ((f32[32,2,128]{2,1,0:T(2,128)}), f32[32,2,128]{2,1,0:T(2,128)S(1)}, u32[]{:S(2)}, u32[]{:S(2)}) async-start(f32[32,2,128]{2,1,0:T(2,128)} %shard_map.42), calls=%async_computation.1 | async-start | bytes 65536 | tf_op jit(solution)/shard_map/all_to_all | solution.py:490
  68.5 7.2 %collective-permute-start.6 = (f32[280,128]{1,0:T(8,128)}, f32[280,128]{1,0:T(8,128)S(1)}, u32[]{:S(2)}, u32[]{:S(2)}) collective-permute-start(f32[280,128]{1,0:T(8,128)} %copy-done.3), channel_id=1, source_target_pairs={{0,8},{8,0},{16,24},{24,16},{32,40},{40,32},{48,56},{56,48},{64,72... | collective-permute-start | bytes 430088 | tf_op jit(solution)/shard_map/ppermute | solution.py:446
  71.7 4.0 %collective-permute-start.7 = (f32[280,128]{1,0:T(8,128)S(1)}, f32[280,128]{1,0:T(8,128)S(1)}, u32[]{:S(2)}, u32[]{:S(2)}) collective-permute-start(f32[280,128]{1,0:T(8,128)S(1)} %get-tuple-element.44), channel_id=1, source_target_pairs={{8,16},{24,32},{40,48},{56,64},{72,80},{88,96},{104,112},{120,128}... | collective-permute-start | bytes 430088 | tf_op jit(solution)/shard_map/ppermute | solution.py:446

commit v4 on v2

--- a/solution.py
+++ b/solution.py
@@ -25,6 +25,10 @@
 SUB = ("x", "c")
 
 
+def plane_index():
+    return lax.axis_index("y") * lax.axis_size("z") + lax.axis_index("z")
+
+
 def tile(ref, t):
     return ref[pl.ds(t * N, N), :]
 
@@ -186,7 +190,8 @@
             set_block(part, q, a, v)
 
 
-def middle(masks, coef, g, rt, rb, first, part, from_n, from_s, from_e, from_w, it, sums_out):
+def middle(coef, g, rt, rb, first, part, from_n, from_s, from_e, from_w, it, sums_out):
+    plane = plane_index()
     c = [coef[pl.ds(q, 1), :] for q in range(2)]
     it[...] = part[...]
     wn = [2.0 + 2.0 * from_n[pl.ds(2 * N * N + q, 1), :] / c[q] for q in range(2)]
@@ -234,10 +239,11 @@
     stack = jnp.where(sub == 2, total(below), stack)
     stack = jnp.where(sub == 3, c[0] + c[1], stack)
     s = jnp.sum(stack, axis=1, keepdims=True)
-    here = masks[pl.ds(0, 1), :]
-    means = here * s[0:1] + masks[pl.ds(1, 1), :] * s[1:2] + masks[pl.ds(2, 1), :] * s[2:3]
+    lane = lax.broadcasted_iota(jnp.int32, (1, 128), 1)
+    means = jnp.where(lane == plane, s[0:1], 0.0)
+    means = means + jnp.where(lane == plane + 1, s[1:2], 0.0) + jnp.where(lane == plane - 1, s[2:3], 0.0)
     sub2 = lax.broadcasted_iota(jnp.int32, (2, 128), 0)
-    pair = jnp.where(sub2 == 0, means, here * s[3:4])
+    pair = jnp.where(sub2 == 0, means, jnp.where(lane == plane, s[3:4], 0.0))
     sums_out[...] = jnp.broadcast_to(pair[None], sums_out.shape)
 
 
@@ -249,20 +255,19 @@
             r = rt[pl.ds(a * N * N, N * N), :] * (1.0 / centre)
             set_block(post, q, a, block(it, q, a) + r * (block(g, q, a) - block(post, q, a)))
     for a in range(N):
-        put(to_e, a, tile(it, at(1, a, N - 1)))
-        put(to_e, N + a, tile(post, at(1, a, N - 1)))
-        put(to_w, a, tile(it, at(0, a, 0)))
-        put(to_w, N + a, tile(post, at(0, a, 0)))
-
-
-def fold(parts, ready, out):
-    total = parts[0] + ready[pl.ds(0, 2), :]
+        for k, field in enumerate((it, post)):
+            put(to_e, k * N + a, tile(field, at(1, a, N - 1)))
+            put(to_w, k * N + a, tile(field, at(0, a, 0)))
+
+
+def fold(parts, out):
+    total = parts[0]
     for k in range(1, parts.shape[0]):
         total = total + parts[k]
     out[...] = jnp.broadcast_to(total[None], out.shape)
 
 
-def side(coef, rt, it, post_in, from_e, from_w, got_e, got_w, post, to_n, to_s, ready):
+def side(coef, rt, it, post_in, from_e, from_w, got_e, got_w, post, to_n, to_s):
     c = [coef[pl.ds(q, 1), :] for q in range(2)]
     ce = from_e[pl.ds(N * N, 1), :]
     cw = from_w[pl.ds(N * N, 1), :]
@@ -284,7 +289,6 @@
         put(to, 4 * N, tile(got_e, a))
         put(to, 4 * N + 1, tile(got_w, a))
         put(to, 4 * N + 2, outer)
-    ready[...] = jnp.zeros((N, 128), f32)
 
 
 def coarse(planes, gains, means):
@@ -308,18 +312,21 @@
     return right / diag
 
 
-def finish(planes, per_plane, masks, coef, st, g, rt, rb, kk, it, post, ring, from_n, from_s, from_e, from_w, got_e, got_w, got_n, got_s, out, acc, v):
+def finish(planes, per_plane, coef, st, g, rt, rb, kk, it, post, ring, from_n, from_s, from_e, from_w, got_e, got_w, got_n, got_s, out, acc, v):
+    plane = plane_index()
     scaled = ring[0]
     for k in range(1, ring.shape[0]):
         scaled = scaled + ring[k]
     corr = coarse(planes, scaled[1:2] * (1.0 / per_plane), scaled[0:1] * (1.0 / (per_plane * N * N * N)))
 
+    lane = lax.broadcasted_iota(jnp.int32, (1, 128), 1)
+
     def pick(k):
-        return jnp.sum(masks[pl.ds(k, 1), :] * corr, axis=1, keepdims=True) + jnp.zeros((1, 128), f32)
-
-    mid, high, low = pick(0), pick(1), pick(2)
-    has_n = masks[pl.ds(3, 1), :]
-    has_s = masks[pl.ds(4, 1), :]
+        return jnp.sum(jnp.where(lane == k, corr, 0.0), axis=1, keepdims=True) + jnp.zeros((1, 128), f32)
+
+    mid, high, low = pick(plane), pick(plane + 1), pick(plane - 1)
+    has_n = (plane < planes - 1).astype(f32)
+    has_s = (plane > 0).astype(f32)
     inner = 1.0 / centre
     c = [coef[pl.ds(q, 1), :] for q in range(2)]
     cn = [from_n[pl.ds(2 * N * N + q, 1), :] for q in range(2)]
@@ -411,14 +418,6 @@
     return lax.ppermute(block_down, axis, down), lax.ppermute(block_up, axis, up)
 
 
-def place_masks(place, planes):
-    lane = jnp.arange(128)[None, :]
-    k = jnp.arange(8)[:, None]
-    hot = jnp.where(k == 0, place, jnp.where(k == 1, place + 1, place - 1))
-    has = jnp.where(k == 3, place < planes - 1, place > 0)
-    return jnp.where(k < 3, lane == hot, has).astype(f32)
-
-
 def solution(mesh):
     n_sfc, n_sub = mesh.shape["sfc"], mesh.shape["sub"]
     ny = 4 if n_sfc % 16 == 0 else 2
@@ -428,10 +427,9 @@
     def per_device(right_side, coefficient, stiffness):
         rs = right_side.reshape(ROWS, 128)
         coef = coefficient.reshape(2, 128)
-        masks = place_masks(lax.axis_index(SFC), n_sfc)
         field = rows(ROWS)
         layer, strip = rows((2 * N + 1) * N), rows((N + 1) * N)
-        to_n, to_s, to_e, to_w = call(
+        planes_out = call(
             pack_first,
             "hhh",
             [layer, layer, strip, strip],
@@ -441,36 +439,33 @@
                 pltpu.VMEM((N, N), f32),
                 pltpu.SemaphoreType.DMA((3,)),
             ],
-            vmem=60,
-        )(rs, coef, stiffness)
-        from_n, from_s = exchange(to_n, to_s, SFC, n_sfc, False)
-        from_e, from_w = exchange(to_e, to_w, SUB, n_sub, True)
+        )(*(pltpu.with_memory_space_constraint(x, pltpu.HBM) for x in (rs, coef, stiffness)))
+        near_planes = exchange(*planes_out[:2], SFC, n_sfc, False)
+        near_spans = exchange(*planes_out[2:], SUB, n_sub, True)
         table = rows(N * N * N)
         g, rt, rb, kk, st, first, part = call(
             start, "vvv", [field, table, table, rows(2 * N * N, bf16, N * N), table, field, field], cost=10**9
         )(rs, coef, stiffness)
-        it, sums = call(middle, "v" * 11, [field, jax.ShapeDtypeStruct((ny * n_sub, 2, 128), f32)])(
-            masks, coef, g, rt, rb, first, part, from_n, from_s, from_e, from_w
+        it, sums = call(middle, "v" * 10, [field, jax.ShapeDtypeStruct((ny * n_sub, 2, 128), f32)])(
+            coef, g, rt, rb, first, part, *near_planes, *near_spans
         )
         near = lax.all_to_all(sums, ("y", "x", "c"), 0, 0)
-        post, to_e, to_w = call(smooth, "vvvvvv", [field, rows(2 * N * N), rows(2 * N * N)], cost=10**9)(
+        (near,) = call(fold, "v", [jax.ShapeDtypeStruct((nz, 2, 128), f32)])(near)
+        near, it = lax.optimization_barrier((near, it))
+        ring = lax.all_to_all(near, "z", 0, 0)
+        post, *spans_out = call(smooth, "vvvvvv", [field, rows(2 * N * N), rows(2 * N * N)], cost=10**9)(
             coef, st, g, rt, kk, it
         )
-        got_e, got_w = exchange(to_e, to_w, SUB, n_sub, True)
-        post, to_n, to_s, ready = call(
-            side, "vvvvvvvv", [field, rows((4 * N + 3) * N), rows((4 * N + 3) * N), rows(N)]
-        )(
-            coef, rt, it, post, from_e, from_w, got_e, got_w
-        )
-        (near,) = call(fold, "vv", [jax.ShapeDtypeStruct((nz, 2, 128), f32)])(near, ready)
-        ring = lax.all_to_all(near, "z", 0, 0)
-        got_n, got_s = exchange(to_n, to_s, SFC, n_sfc, False)
+        far_spans = exchange(*spans_out, SUB, n_sub, True)
+        tall = rows((4 * N + 3) * N)
+        post, *planes_out = call(side, "v" * 8, [field, tall, tall])(coef, rt, it, post, *near_spans, *far_spans)
+        far_planes = exchange(*planes_out, SFC, n_sfc, False)
 
         def last(*refs):
             finish(n_sfc, float(2 * n_sub * 128), *refs)
 
-        (out,) = call(last, "v" * 18, [field], [pltpu.VMEM((ROWS, 128), f32), pltpu.VMEM((ROWS, 128), f32)])(
-            masks, coef, st, g, rt, rb, kk, it, post, ring, from_n, from_s, from_e, from_w, got_e, got_w, got_n, got_s
+        (out,) = call(last, "v" * 17, [field], [pltpu.VMEM((ROWS, 128), f32), pltpu.VMEM((ROWS, 128), f32)])(
+            coef, st, g, rt, rb, kk, it, post, ring, *near_planes, *near_spans, *far_spans, *far_planes
         )
         return out.reshape(right_side.shape)
 

time: 86.6 us -> 81.8 us (0.945)
  blocking collectives: 0 us -> 22.8 us
  starting transfers between devices: 53.7 us -> 37.7 us
  waiting for transfers between devices: 23.2 us -> 14.2 us
  local copies, waits for them, and re-layouts: 1.26 us -> 0.01 us
  Pallas kernels: 7.89 us -> 6.65 us
    all_to_all x0 -> x1, blocking collectives: none -> 22.8 us  [per_device(): near = lax.all_to_all(sums, ('y', 'x', 'c'), 0, 0)]
    all_to_all x1 -> x0, starting transfers between devices: 16.1 us -> none  [per_device(): near = lax.all_to_all(sums, ('y', 'x', 'c'), 0, 0)]
    all_to_all x1 -> x0, waiting for transfers between devices: 6.5 us -> none  [per_device(): near = lax.all_to_all(sums, ('y', 'x', 'c'), 0, 0)]
    all_to_all x1, waiting for transfers between devices: 14.1 us -> 9.79 us  [per_device(): ring = lax.all_to_all(near, 'z', 0, 0)]
    ppermute x4, waiting for transfers between devices: 1.88 us -> 3.31 us  [exchange(): lax.ppermute(block_down, axis, down)]
    unnamed x8 -> x6, local copies, waits for them, and re-layouts: 1.26 us -> 0.01 us
  transfers between devices with their start and end apart: 10 -> 9, of which waited for: 4 -> 4; matrix products, arithmetic and copies ran while one was open for 0% -> 0% of each run, Pallas kernels for 2% -> 3%
where the time goes in v4:
time: 81.8 us; the launch traced here: 81.5 us
  starting transfers between devices  37.7 us (46%)
  blocking collectives  22.8 us (28%)
  waiting for transfers between devices  14.2 us (17%)
  Pallas kernels  6.65 us (8%)
    all_to_all x1, blocking collectives, per_device(): near = lax.all_to_all(sums, ('y', 'x', 'c'), 0, 0)  22.8 us
    ppermute x4, starting transfers between devices, exchange(): lax.ppermute(block_down, axis, down)  17.6 us
    all_to_all x1, starting transfers between devices, per_device(): ring = lax.all_to_all(near, 'z', 0, 0)  11.1 us
    all_to_all x1, waiting for transfers between devices, per_device(): ring = lax.all_to_all(near, 'z', 0, 0)  9.79 us
    ppermute x4, starting transfers between devices, exchange(): lax.ppermute(block_up, axis, up)  9.06 us
    ppermute x4, waiting for transfers between devices, exchange(): lax.ppermute(block_down, axis, down)  3.31 us
    pallas_call x1, Pallas kernels, per_device(): call(last, 'v' * 17, [field], [pltpu.VMEM((ROWS, 128), f32), pltpu.VMEM((...  2.49 us
  transfers between devices with their start and end apart: 9, of which 4 were waited for; matrix products, arithmetic and copies ran while one was open for 0% of the time, Pallas kernels for 3%

profile of v4, /device:TPU:1, one launch (start us, length us, event | category | flops | bytes accessed | tf_op | source)
XLA Modules:
  0.0 81.5 jit_solution(6694735522000613941)
XLA Ops:
  0.0 0.0 copy-start
  0.0 1.2 %shard_map.38 = (f32[136,128]{1,0:T(8,128)S(1)}, f32[136,128]{1,0:T(8,128)S(1)}, f32[72,128]{1,0:T(8,128)S(1)}, f32[72,128]{1,0:T(8,128)S(1)}) custom-call(f32[1024,128]{1,0:T(8,128)} %bitcast.5, f32[2,128]{1,0:T(2,128)} %bitcast.7, f32[8,8]{1,0:T(8,128)} %sv_far.1), custom_call_target="tpu_custom_call" | custom-call | flops 1000000 | bytes 100000 | tf_op jit(solution)/shard_map/pallas_call | solution.py:432
  1.2 0.0 copy-start.2
  1.2 14.2 %collective-permute-start.2 = (f32[72,128]{1,0:T(8,128)S(1)}, f32[72,128]{1,0:T(8,128)S(1)}, u32[]{:S(2)}, u32[]{:S(2)}) collective-permute-start(f32[72,128]{1,0:T(8,128)S(1)} %get-tuple-element.35), channel_id=1, source_target_pairs={{1,0},{2,1},{3,2},{4,3},{5,4},{6,5},{7,6},{0,7},{9,8},{10,9},{11,1... | collective-permute-start | bytes 110600 | tf_op jit(solution)/shard_map/ppermute | solution.py:418
  15.4 0.0 collective-permute-start.3
  15.4 0.0 copy-start.1
  15.4 1.4 %collective-permute-start = (f32[136,128]{1,0:T(8,128)S(1)}, f32[136,128]{1,0:T(8,128)S(1)}, u32[]{:S(2)}, u32[]{:S(2)}) collective-permute-start(f32[136,128]{1,0:T(8,128)S(1)} %get-tuple-element.33), channel_id=1, source_target_pairs={{8,0},{16,8},{24,16},{32,24},{40,32},{48,40},{56,48},{64,56},{72,6... | collective-permute-start | bytes 208904 | tf_op jit(solution)/shard_map/ppermute | solution.py:418
  16.8 4.0 %collective-permute-start.1 = (f32[136,128]{1,0:T(8,128)S(1)}, f32[136,128]{1,0:T(8,128)S(1)}, u32[]{:S(2)}, u32[]{:S(2)}) collective-permute-start(f32[136,128]{1,0:T(8,128)S(1)} %get-tuple-element.34), channel_id=1, source_target_pairs={{0,8},{8,16},{16,24},{24,32},{32,40},{40,48},{48,56},{56,64},{64,7... | collective-permute-start | bytes 208904 | tf_op jit(solution)/shard_map/ppermute | solution.py:418
  20.8 0.0 copy-done
  20.8 0.0 copy-done.2
  20.8 0.0 copy-done.1
  20.8 1.4 %shard_map.37 = (f32[1024,128]{1,0:T(8,128)S(1)}, f32[512,128]{1,0:T(8,128)S(1)}, f32[512,128]{1,0:T(8,128)S(1)}, bf16[128,64]{1,0:T(8,128)(2,1)S(1)}, f32[512,1...) custom-call(f32[1024,128]{1,0:T(8,128)S(1)} %bitcast.6, f32[2,128]{1,0:T(2,128)S(1)} %bitcast.8, ...), custom_call_target="tpu_custom_call" | custom-call | flops 1000000000 | bytes 100000 | tf_op jit(solution)/shard_map/pallas_call | solution.py:446
  22.2 0.0 collective-permute-done.2.from_e.refs_11_
  22.2 0.0 collective-permute-done.3.from_w.refs_12_
  22.2 0.0 collective-permute-done.from_n.refs_9_
  22.2 0.0 collective-permute-done.1.from_s.refs_10_
  22.2 0.2 shard_map.39
  22.5 22.8 %all_to_all.10.parts = f32[32,2,128]{2,1,0:T(2,128)S(1)} all-to-all(f32[32,2,128]{2,1,0:T(2,128)S(1)} %get-tuple-element.37), channel_id=1, replica_groups=mesh['y'=4,'z'=32,'x'=4,'c'=2] {'y','x','c'}, dimensions={0} | all-to-all | bytes 65536 | tf_op jit(solution)/shard_map/all_to_all | solution.py:452
  45.3 0.7 shard_map.40
  46.0 11.1 %all-to-all-start.1 = ((f32[32,2,128]{2,1,0:T(2,128)}), f32[32,2,128]{2,1,0:T(2,128)S(1)}, u32[]{:S(2)}, u32[]{:S(2)}) async-start(f32[32,2,128]{2,1,0:T(2,128)} %shard_map.40), calls=%async_computation.1 | async-start | bytes 65536 | tf_op jit(solution)/shard_map/all_to_all | solution.py:455
  57.0 0.7 shard_map.41
  57.7 0.7 collective-permute-start.4
  58.4 1.1 %collective-permute-start.5 = (f32[128,128]{1,0:T(8,128)S(1)}, f32[128,128]{1,0:T(8,128)S(1)}, u32[]{:S(2)}, u32[]{:S(2)}) collective-permute-start(f32[128,128]{1,0:T(8,128)S(1)} %get-tuple-element.42), channel_id=1, source_target_pairs={{0,1},{1,2},{2,3},{3,4},{4,5},{5,6},{6,7},{7,0},{8,9},{9,10},{10,1... | collective-permute-start | bytes 196616 | tf_op jit(solution)/shard_map/ppermute | solution.py:418
  59.5 2.2 %collective-permute-done.4.got_e.refs_13_ = f32[128,128]{1,0:T(8,128)S(1)} collective-permute-done((f32[128,128]{1,0:T(8,128)S(1)}, f32[128,128]{1,0:T(8,128)S(1)}, u32[]{:S(2)}, u32[]{:S(2)}) %collective-permute-start.4) | collective-permute-done | bytes 65568 | tf_op jit(solution)/shard_map/ppermute | solution.py:418
  61.7 0.0 collective-permute-done.5.got_w.refs_14_
  61.7 0.1 shard_map.42
  61.8 1.3 %collective-permute-start.6 = (f32[280,128]{1,0:T(8,128)S(1)}, f32[280,128]{1,0:T(8,128)S(1)}, u32[]{:S(2)}, u32[]{:S(2)}) collective-permute-start(f32[280,128]{1,0:T(8,128)S(1)} %get-tuple-element.45), channel_id=1, source_target_pairs={{8,0},{16,8},{24,16},{32,24},{40,32},{48,40},{56,48},{64,56},{72,6... | collective-permute-start | bytes 430088 | tf_op jit(solution)/shard_map/ppermute | solution.py:418
  63.1 4.0 %collective-permute-start.7 = (f32[280,128]{1,0:T(8,128)S(1)}, f32[280,128]{1,0:T(8,128)S(1)}, u32[]{:S(2)}, u32[]{:S(2)}) collective-permute-start(f32[280,128]{1,0:T(8,128)S(1)} %get-tuple-element.46), channel_id=1, source_target_pairs={{0,8},{8,16},{16,24},{24,32},{32,40},{40,48},{48,56},{56,64},{64,7... | collective-permute-start | bytes 430088 | tf_op jit(solution)/shard_map/ppermute | solution.py:418
  67.1 1.1 %collective-permute-done.6.refs_15_ = f32[280,128]{1,0:T(8,128)S(1)} collective-permute-done((f32[280,128]{1,0:T(8,128)S(1)}, f32[280,128]{1,0:T(8,128)S(1)}, u32[]{:S(2)}, u32[]{:S(2)}) %collective-permute-start.6) | collective-permute-done | bytes 143392 | tf_op jit(solution)/shard_map/ppermute | solution.py:418
  68.1 1.1 %collective-permute-done.7.refs_16_ = f32[280,128]{1,0:T(8,128)S(1)} collective-permute-done((f32[280,128]{1,0:T(8,128)S(1)}, f32[280,128]{1,0:T(8,128)S(1)}, u32[]{:S(2)}, u32[]{:S(2)}) %collective-permute-start.7) | collective-permute-done | bytes 143392 | tf_op jit(solution)/shard_map/ppermute | solution.py:418
  69.3 9.8 %all-to-all-done.1.refs_8_ = f32[32,2,128]{2,1,0:T(2,128)S(1)} async-done(((f32[32,2,128]{2,1,0:T(2,128)}), f32[32,2,128]{2,1,0:T(2,128)S(1)}, u32[]{:S(2)}, u32[]{:S(2)}) %all-to-all-start.1) | async-done | bytes 32800 | tf_op jit(solution)/shard_map/all_to_all | solution.py:455
  79.0 2.5 %shard_map.43 = f32[1024,128]{1,0:T(8,128)} custom-call(f32[2,128]{1,0:T(2,128)S(1)} %bitcast.12, f32[512,128]{1,0:T(8,128)S(1)} %get-tuple-element.26.st.refs_1_, f32[1024,128]{1,0:T(8,128)S(1)} %get-tuple-element.27.g.refs_2_, f32[512,128]{1,0:T(8,128)S(1)} %get-tuple-element.28.rt.refs_3_, f32[512,128]{1,0:T(8,128)S(1)} %get-tuple-element.29.rb.refs_4_, ...), custom_call_target="tpu_custom_call" | custom-call | flops 1000000 | bytes 100000 | tf_op jit(solution)/shard_map/pallas_call | solution.py:467
Async XLA Ops:
  0.0 20.8 %copy-start = (f32[8,8,8,1,2,128]{5,4,3,2,1,0:T(2,128)S(1)}, f32[8,8,8,1,2,128]{5,4,3,2,1,0:T(2,128)}, u32[]{:S(2)}) copy-start(f32[8,8,8,1,2,128]{5,4,3,2,1,0:T(2,128)} %param.3) | copy-start | bytes 1572868
  1.2 19.6 %copy-start.2 = (f32[8,8]{1,0:T(8,128)S(1)}, f32[8,8]{1,0:T(8,128)}, u32[]{:S(2)}) copy-start(f32[8,8]{1,0:T(8,128)} %sv_far.1) | copy-start | bytes 772
  1.2 21.0 %collective-permute-start.2 = (f32[72,128]{1,0:T(8,128)S(1)}, f32[72,128]{1,0:T(8,128)S(1)}, u32[]{:S(2)}, u32[]{:S(2)}) collective-permute-start(f32[72,128]{1,0:T(8,128)S(1)} %get-tuple-element.35), channel_id=1, source_target_pairs={{1,0},{2,1},{3,2},{4,3},{5,4},{6,5},{7,6},{0,7},{9,8},{10,9},{11,1... | collective-permute-start | bytes 110600 | tf_op jit(solution)/shard_map/ppermute | solution.py:418
  15.4 6.8 %collective-permute-start.3 = (f32[72,128]{1,0:T(8,128)S(1)}, f32[72,128]{1,0:T(8,128)S(1)}, u32[]{:S(2)}, u32[]{:S(2)}) collective-permute-start(f32[72,128]{1,0:T(8,128)S(1)} %get-tuple-element.36), channel_id=1, source_target_pairs={{0,1},{1,2},{2,3},{3,4},{4,5},{5,6},{6,7},{7,0},{8,9},{9,10},{10,1... | collective-permute-start | bytes 110600 | tf_op jit(solution)/shard_map/ppermute | solution.py:418
  15.4 5.4 %copy-start.1 = (f32[1,2,128]{2,1,0:T(2,128)S(1)}, f32[1,2,128]{2,1,0:T(2,128)}, u32[]{:S(2)}) copy-start(f32[1,2,128]{2,1,0:T(2,128)} %param.4) | copy-start | bytes 3076
  15.4 6.8 %collective-permute-start = (f32[136,128]{1,0:T(8,128)S(1)}, f32[136,128]{1,0:T(8,128)S(1)}, u32[]{:S(2)}, u32[]{:S(2)}) collective-permute-start(f32[136,128]{1,0:T(8,128)S(1)} %get-tuple-element.33), channel_id=1, source_target_pairs={{8,0},{16,8},{24,16},{32,24},{40,32},{48,40},{56,48},{64,56},{72,6... | collective-permute-start | bytes 208904 | tf_op jit(solution)/shard_map/ppermute | solution.py:418
  16.8 5.4 %collective-permute-start.1 = (f32[136,128]{1,0:T(8,128)S(1)}, f32[136,128]{1,0:T(8,128)S(1)}, u32[]{:S(2)}, u32[]{:S(2)}) collective-permute-start(f32[136,128]{1,0:T(8,128)S(1)} %get-tuple-element.34), channel_id=1, source_target_pairs={{0,8},{8,16},{16,24},{24,32},{32,40},{40,48},{48,56},{56,64},{64,7... | collective-permute-start | bytes 208904 | tf_op jit(solution)/shard_map/ppermute | solution.py:418
  46.0 33.1 %all-to-all-start.1 = ((f32[32,2,128]{2,1,0:T(2,128)}), f32[32,2,128]{2,1,0:T(2,128)S(1)}, u32[]{:S(2)}, u32[]{:S(2)}) async-start(f32[32,2,128]{2,1,0:T(2,128)} %shard_map.40), calls=%async_computation.1 | async-start | bytes 65536 | tf_op jit(solution)/shard_map/all_to_all | solution.py:455
  57.7 4.0 %collective-permute-start.4 = (f32[128,128]{1,0:T(8,128)S(1)}, f32[128,128]{1,0:T(8,128)S(1)}, u32[]{:S(2)}, u32[]{:S(2)}) collective-permute-start(f32[128,128]{1,0:T(8,128)S(1)} %get-tuple-element.41), channel_id=1, source_target_pairs={{1,0},{2,1},{3,2},{4,3},{5,4},{6,5},{7,6},{0,7},{9,8},{10,9},{11,1... | collective-permute-start | bytes 196616 | tf_op jit(solution)/shard_map/ppermute | solution.py:418
  58.4 3.3 %collective-permute-start.5 = (f32[128,128]{1,0:T(8,128)S(1)}, f32[128,128]{1,0:T(8,128)S(1)}, u32[]{:S(2)}, u32[]{:S(2)}) collective-permute-start(f32[128,128]{1,0:T(8,128)S(1)} %get-tuple-element.42), channel_id=1, source_target_pairs={{0,1},{1,2},{2,3},{3,4},{4,5},{5,6},{6,7},{7,0},{8,9},{9,10},{10,1... | collective-permute-start | bytes 196616 | tf_op jit(solution)/shard_map/ppermute | solution.py:418
  61.8 6.4 %collective-permute-start.6 = (f32[280,128]{1,0:T(8,128)S(1)}, f32[280,128]{1,0:T(8,128)S(1)}, u32[]{:S(2)}, u32[]{:S(2)}) collective-permute-start(f32[280,128]{1,0:T(8,128)S(1)} %get-tuple-element.45), channel_id=1, source_target_pairs={{8,0},{16,8},{24,16},{32,24},{40,32},{48,40},{56,48},{64,56},{72,6... | collective-permute-start | bytes 430088 | tf_op jit(solution)/shard_map/ppermute | solution.py:418
  63.1 6.2 %collective-permute-start.7 = (f32[280,128]{1,0:T(8,128)S(1)}, f32[280,128]{1,0:T(8,128)S(1)}, u32[]{:S(2)}, u32[]{:S(2)}) collective-permute-start(f32[280,128]{1,0:T(8,128)S(1)} %get-tuple-element.46), channel_id=1, source_target_pairs={{0,8},{8,16},{16,24},{24,32},{32,40},{40,48},{48,56},{56,64},{64,7... | collective-permute-start | bytes 430088 | tf_op jit(solution)/shard_map/ppermute | solution.py:418

commit v5 on v4

--- a/solution.py
+++ b/solution.py
@@ -312,22 +312,27 @@
     return right / diag
 
 
-def finish(planes, per_plane, coef, st, g, rt, rb, kk, it, post, ring, from_n, from_s, from_e, from_w, got_e, got_w, got_n, got_s, out, acc, v):
-    plane = plane_index()
-    scaled = ring[0]
-    for k in range(1, ring.shape[0]):
-        scaled = scaled + ring[k]
-    corr = coarse(planes, scaled[1:2] * (1.0 / per_plane), scaled[0:1] * (1.0 / (per_plane * N * N * N)))
-
-    lane = lax.broadcasted_iota(jnp.int32, (1, 128), 1)
-
-    def pick(k):
-        return jnp.sum(jnp.where(lane == k, corr, 0.0), axis=1, keepdims=True) + jnp.zeros((1, 128), f32)
-
-    mid, high, low = pick(plane), pick(plane + 1), pick(plane - 1)
-    has_n = (plane < planes - 1).astype(f32)
-    has_s = (plane > 0).astype(f32)
-    inner = 1.0 / centre
+def tables(rt, rb, kk, st, wt, t1, t7, t0, u, acc):
+    lane = lax.broadcasted_iota(jnp.int32, (N * N, 128), 1)
+    for a in range(N):
+        r = rt[pl.ds(a * N * N, N * N), :] * (1.0 / centre)
+        w = 1.0 - r * rb[pl.ds(a * N * N, N * N), :]
+        wt[pl.ds(a * N * N, N * N), :] = w
+        x = jnp.where(lane == 0, w, 0.0)
+        if a == N - 1:
+            x = jnp.where(lane == 1, -r, x)
+        if a == 0:
+            x = jnp.where(lane == 2, -r, x)
+        set_block(u, 0, a, x)
+        set_block(u, 1, a, jnp.zeros((N * N, 128), f32))
+    stiff(u, kk, st, acc)
+    for a in range(N):
+        x = block(acc, 0, a)
+        for k, out in enumerate((t1, t7, t0)):
+            out[pl.ds(a * N * N, N * N), :] = jnp.broadcast_to(x[:, k : k + 1], (N * N, 128))
+
+
+def face_weights(coef, from_n, from_s, from_e, from_w):
     c = [coef[pl.ds(q, 1), :] for q in range(2)]
     cn = [from_n[pl.ds(2 * N * N + q, 1), :] for q in range(2)]
     cs = [from_s[pl.ds(2 * N * N + q, 1), :] for q in range(2)]
@@ -337,22 +342,29 @@
     ws = [2.0 + 2.0 * cs[q] / c[q] for q in range(2)]
     we = 2.0 + 2.0 * ce / c[1]
     ww = 2.0 + 2.0 * cw / c[0]
+    return c, cn, cs, ce, cw, wn, ws, we, ww
+
+
+def back_weight(own, far):
+    return 2.0 + 2.0 * own / jnp.where(far > 0.0, far, 1.0)
+
+
+def ahead(planes, coef, st, g, rt, kk, it, post, from_n, from_s, from_e, from_w, got_e, got_w, got_n, got_s, base, faces, acc, v):
+    plane = plane_index()
+    has_n = (plane < planes - 1).astype(f32)
+    has_s = (plane > 0).astype(f32)
+    inner = 1.0 / centre
+    c, cn, cs, ce, cw, wn, ws, we, ww = face_weights(coef, from_n, from_s, from_e, from_w)
 
     def r_at(a, b):
         return tile(rt, a * N + b)
 
-    def weight(a, b):
-        return 1.0 - inner * r_at(a, b) * tile(rb, a * N + b)
-
-    for q in range(2):
-        for a in range(N):
-            r = rt[pl.ds(a * N * N, N * N), :]
-            set_block(v, q, a, block(post, q, a) + mid * (1.0 - inner * r * rb[pl.ds(a * N * N, N * N), :]))
+    v[...] = post[...]
+    for q in range(2):
         for b in range(N):
-            for a, w, other, got in ((N - 1, wn[q], high, got_n), (0, ws[q], low, got_s)):
+            for a, w, got in ((N - 1, wn[q], got_n), (0, ws[q], got_s)):
                 k = at(q, a, b)
-                jump = (tile(it, k) - tile(got, q * N + b)) + (mid - other)
-                put(v, k, tile(v, k) - inner * r_at(a, b) * (w * jump))
+                put(v, k, tile(v, k) - inner * r_at(a, b) * (w * (tile(it, k) - tile(got, q * N + b))))
     stiff(v, kk, st, acc)
     inner_faces(v, coef, acc)
 
@@ -360,35 +372,97 @@
         put(acc, k, tile(acc, k) + w * (tile(v, k) - other))
 
     for q in range(2):
-        for a, b0, w, has, got, far, cfar in (
-            (N - 1, 0, wn[q], has_n, got_n, high, cn[q]),
-            (0, N - 1, ws[q], has_s, got_s, low, cs[q]),
+        for a, b0, w, has, got, cfar in (
+            (N - 1, 0, wn[q], has_n, got_n, cn[q]),
+            (0, N - 1, ws[q], has_s, got_s, cs[q]),
         ):
-            back = 2.0 + 2.0 * c[q] / jnp.where(cfar > 0.0, cfar, 1.0)
+            back = back_weight(c[q], cfar)
+            faces[pl.ds((2 if a else 4) + q, 1), :] = w
+            faces[pl.ds((6 if a else 8) + q, 1), :] = back
             for b in range(N):
                 k = at(q, a, b)
-                jump = (tile(got, q * N + b) - tile(it, k)) + (far - mid)
-                other = tile(got, 2 * N + q * N + b) + far * weight(b0, b) - inner * r_at(b0, b) * (back * jump)
-                add(k, w, has * other)
+                jump = tile(got, q * N + b) - tile(it, k)
+                add(k, w, has * (tile(got, 2 * N + q * N + b) - inner * r_at(b0, b) * (back * jump)))
     for q, b, far_b, w, got, line, row, cfar in (
         (1, N - 1, 0, we, got_e, 4 * N, 0, ce),
         (0, 0, N - 1, ww, got_w, 4 * N + 1, 1, cw),
     ):
-        back = 2.0 + 2.0 * c[q] / cfar
+        back = back_weight(c[q], cfar)
+        faces[pl.ds(row, 1), :] = w
         for a in range(N):
             k = at(q, a, b)
             loss = back * (tile(got, a) - tile(it, k))
-            for edge, from_far, other in ((N - 1, got_n, high), (0, got_s, low)):
+            for edge, from_far in ((N - 1, got_n), (0, got_s)):
                 if a == edge:
                     wf = 2.0 + 2.0 * from_far[pl.ds((4 * N + 2) * N + row, 1), :] / cfar
-                    loss = loss + wf * ((tile(got, a) - tile(from_far, line)) + (mid - other))
-            other = tile(got, N + a) + mid * weight(a, far_b) - inner * r_at(a, far_b) * loss
-            add(k, w, other)
+                    faces[pl.ds((10 if a else 12) + row, 1), :] = wf
+                    loss = loss + wf * (tile(got, a) - tile(from_far, line))
+            add(k, w, tile(got, N + a) - inner * r_at(a, far_b) * loss)
     for q in range(2):
         for a in range(N):
             r = rt[pl.ds(a * N * N, N * N), :]
-            x = block(v, q, a)
-            last = x + keep * ((x - block(it, q, a)) - mid) + gain2 * r * (block(g, q, a) - block(acc, q, a))
+            x = (1.0 + keep) * block(v, q, a) - keep * block(it, q, a)
+            set_block(base, q, a, x + gain2 * r * (block(g, q, a) - block(acc, q, a)))
+
+
+def finish(planes, per_plane, coef, rt, wt, t1, t7, t0, base, faces, ring, out, acc, v):
+    scaled = ring[0]
+    for k in range(1, ring.shape[0]):
+        scaled = scaled + ring[k]
+    corr = coarse(planes, scaled[1:2] * (1.0 / per_plane), scaled[0:1] * (1.0 / (per_plane * N * N * N)))
+    plane = plane_index()
+    lane = lax.broadcasted_iota(jnp.int32, (1, 128), 1)
+
+    def pick(k):
+        return jnp.sum(jnp.where(lane == k, corr, 0.0), axis=1, keepdims=True) + jnp.zeros((1, 128), f32)
+
+    mid, high, low = pick(plane), pick(plane + 1), pick(plane - 1)
+    has_n = (plane < planes - 1).astype(f32)
+    has_s = (plane > 0).astype(f32)
+    inner = 1.0 / centre
+
+    def face(k):
+        return faces[pl.ds(k, 1), :]
+
+    we, ww = face(0), face(1)
+    wn, ws = [face(2), face(3)], [face(4), face(5)]
+
+    def r_at(a, b):
+        return tile(rt, a * N + b)
+
+    for q in range(2):
+        up, down = wn[q] * (mid - high), ws[q] * (mid - low)
+        for a in range(N):
+            rows_a = pl.ds(a * N * N, N * N)
+            x = mid * wt[rows_a, :]
+            if a == N - 1:
+                x = x - inner * rt[rows_a, :] * up
+            if a == 0:
+                x = x - inner * rt[rows_a, :] * down
+            set_block(v, q, a, x)
+            set_block(acc, q, a, mid * t1[rows_a, :] + up * t7[rows_a, :] + down * t0[rows_a, :])
+    inner_faces(v, coef, acc)
+
+    def add(k, w, other):
+        put(acc, k, tile(acc, k) + w * (tile(v, k) - other))
+
+    for q in range(2):
+        for a, b0, w, has, far in ((N - 1, 0, wn[q], has_n, high), (0, N - 1, ws[q], has_s, low)):
+            step = face((6 if a else 8) + q) * (far - mid)
+            for b in range(N):
+                add(at(q, a, b), w, has * (far * tile(wt, b0 * N + b) - inner * r_at(b0, b) * step))
+    for q, b, far_b, w, row in ((1, N - 1, 0, we, 0), (0, 0, N - 1, ww, 1)):
+        for a in range(N):
+            other = mid * tile(wt, a * N + far_b)
+            for edge, far in ((N - 1, high), (0, low)):
+                if a == edge:
+                    other = other - inner * r_at(a, far_b) * (face((10 if a else 12) + row) * (mid - far))
+            add(at(q, a, b), w, other)
+    for q in range(2):
+        for a in range(N):
+            r = rt[pl.ds(a * N * N, N * N), :]
+            x = block(base, q, a) + ((1.0 + keep) * block(v, q, a) - keep * mid)
+            last = x - gain2 * r * block(acc, q, a)
             for b in range(N):
                 out[pl.ds(at(0, a, b) * 2 * N + q, N, stride=2), :] = last[b * N : (b + 1) * N]
 
@@ -461,12 +535,19 @@
         post, *planes_out = call(side, "v" * 8, [field, tall, tall])(coef, rt, it, post, *near_spans, *far_spans)
         far_planes = exchange(*planes_out, SFC, n_sfc, False)
 
+        scratch = [pltpu.VMEM((ROWS, 128), f32), pltpu.VMEM((ROWS, 128), f32)]
+        parts = call(tables, "vvvv", [table] * 4, scratch)(rt, rb, kk, st)
+
+        def early(*refs):
+            ahead(n_sfc, *refs)
+
         def last(*refs):
             finish(n_sfc, float(2 * n_sub * 128), *refs)
 
-        (out,) = call(last, "v" * 17, [field], [pltpu.VMEM((ROWS, 128), f32), pltpu.VMEM((ROWS, 128), f32)])(
-            coef, st, g, rt, rb, kk, it, post, ring, *near_planes, *near_spans, *far_spans, *far_planes
+        base, faces = call(early, "v" * 15, [field, rows(2 * N)], scratch)(
+            coef, st, g, rt, kk, it, post, *near_planes, *near_spans, *far_spans, *far_planes
         )
+        (out,) = call(last, "v" * 9, [field], scratch)(coef, rt, *parts, base, faces, ring)
         return out.reshape(right_side.shape)
 
     field_spec = P(None, None, None, SFC, SUB, None)

time: 81.8 us -> 81.3 us (level)
  waiting for transfers between devices: 14.2 us -> 12.9 us
  Pallas kernels: 6.65 us -> 7.51 us
    pallas_call x1 -> x3, Pallas kernels: 2.49 us -> 3.36 us  [the longest x1 1.99 us: per_device(): call(last, 'v' * 9, [field], scratch)(coef, rt, *parts, base, faces, ring)]
    all_to_all x1, waiting for transfers between devices: 9.79 us -> 8.93 us  [per_device(): ring = lax.all_to_all(near, 'z', 0, 0)]
  transfers between devices with their start and end apart: 9 -> 9, of which waited for: 4 -> 4; matrix products, arithmetic and copies ran while one was open for 0% -> 0% of each run, Pallas kernels for 3% -> 4%
where the time goes in v5:
time: 81.3 us; the launch traced here: 81 us
  starting transfers between devices  37.7 us (46%)
  blocking collectives  22.8 us (28%)
  waiting for transfers between devices  12.9 us (16%)
  Pallas kernels  7.51 us (9%)
    all_to_all x1, blocking collectives, per_device(): near = lax.all_to_all(sums, ('y', 'x', 'c'), 0, 0)  22.8 us
    ppermute x4, starting transfers between devices, exchange(): lax.ppermute(block_down, axis, down)  17.6 us
    all_to_all x1, starting transfers between devices, per_device(): ring = lax.all_to_all(near, 'z', 0, 0)  11.1 us
    ppermute x4, starting transfers between devices, exchange(): lax.ppermute(block_up, axis, up)  9.06 us
    all_to_all x1, waiting for transfers between devices, per_device(): ring = lax.all_to_all(near, 'z', 0, 0)  8.93 us
    ppermute x4, waiting for transfers between devices, exchange(): lax.ppermute(block_down, axis, down)  2.8 us
    pallas_call x1, Pallas kernels, per_device(): call(last, 'v' * 9, [field], scratch)(coef, rt, *parts, base, faces, ring)  1.99 us
  transfers between devices with their start and end apart: 9, of which 4 were waited for; matrix products, arithmetic and copies ran while one was open for 0% of the time, Pallas kernels for 4%

profile of v5, /device:TPU:1, one launch (start us, length us, event | category | flops | bytes accessed | tf_op | source)
XLA Modules:
  0.0 81.0 jit_solution(13132931063201234944)
XLA Ops:
  0.0 0.0 copy-start
  0.0 1.2 %shard_map.39 = (f32[136,128]{1,0:T(8,128)S(1)}, f32[136,128]{1,0:T(8,128)S(1)}, f32[72,128]{1,0:T(8,128)S(1)}, f32[72,128]{1,0:T(8,128)S(1)}) custom-call(f32[1024,128]{1,0:T(8,128)} %bitcast.5, f32[2,128]{1,0:T(2,128)} %bitcast.7, f32[8,8]{1,0:T(8,128)} %sv_far.1), custom_call_target="tpu_custom_call" | custom-call | flops 1000000 | bytes 100000 | tf_op jit(solution)/shard_map/pallas_call | solution.py:506
  1.2 0.0 copy-start.2
  1.2 14.2 %collective-permute-start.2 = (f32[72,128]{1,0:T(8,128)S(1)}, f32[72,128]{1,0:T(8,128)S(1)}, u32[]{:S(2)}, u32[]{:S(2)}) collective-permute-start(f32[72,128]{1,0:T(8,128)S(1)} %get-tuple-element.45), channel_id=1, source_target_pairs={{1,0},{2,1},{3,2},{4,3},{5,4},{6,5},{7,6},{0,7},{9,8},{10,9},{11,1... | collective-permute-start | bytes 110600 | tf_op jit(solution)/shard_map/ppermute | solution.py:492
  15.4 0.0 collective-permute-start.3
  15.4 0.0 copy-start.1
  15.4 1.4 %collective-permute-start = (f32[136,128]{1,0:T(8,128)S(1)}, f32[136,128]{1,0:T(8,128)S(1)}, u32[]{:S(2)}, u32[]{:S(2)}) collective-permute-start(f32[136,128]{1,0:T(8,128)S(1)} %get-tuple-element.43), channel_id=1, source_target_pairs={{8,0},{16,8},{24,16},{32,24},{40,32},{48,40},{56,48},{64,56},{72,6... | collective-permute-start | bytes 208904 | tf_op jit(solution)/shard_map/ppermute | solution.py:492
  16.8 4.0 %collective-permute-start.1 = (f32[136,128]{1,0:T(8,128)S(1)}, f32[136,128]{1,0:T(8,128)S(1)}, u32[]{:S(2)}, u32[]{:S(2)}) collective-permute-start(f32[136,128]{1,0:T(8,128)S(1)} %get-tuple-element.44), channel_id=1, source_target_pairs={{0,8},{8,16},{16,24},{24,32},{32,40},{40,48},{48,56},{56,64},{64,7... | collective-permute-start | bytes 208904 | tf_op jit(solution)/shard_map/ppermute | solution.py:492
  20.8 0.0 copy-done
  20.8 0.0 copy-done.2
  20.8 0.0 copy-done.1
  20.8 1.3 %shard_map.37 = (f32[1024,128]{1,0:T(8,128)S(1)}, f32[512,128]{1,0:T(8,128)S(1)}, f32[512,128]{1,0:T(8,128)S(1)}, bf16[128,64]{1,0:T(8,128)(2,1)S(1)}, f32[512,1...) custom-call(f32[1024,128]{1,0:T(8,128)S(1)} %bitcast.6, f32[2,128]{1,0:T(2,128)S(1)} %bitcast.8, ...), custom_call_target="tpu_custom_call" | custom-call | flops 1000000000 | bytes 100000 | tf_op jit(solution)/shard_map/pallas_call | solution.py:520
  22.2 0.0 collective-permute-done.2.from_e.refs_9_
  22.2 0.0 collective-permute-done.3.from_w.refs_10_
  22.2 0.0 collective-permute-done.from_n.refs_7_
  22.2 0.0 collective-permute-done.1.from_s.refs_8_
  22.2 0.2 shard_map.40
  22.5 22.8 %all_to_all.10.parts = f32[32,2,128]{2,1,0:T(2,128)S(1)} all-to-all(f32[32,2,128]{2,1,0:T(2,128)S(1)} %get-tuple-element.47), channel_id=1, replica_groups=mesh['y'=4,'z'=32,'x'=4,'c'=2] {'y','x','c'}, dimensions={0} | all-to-all | bytes 65536 | tf_op jit(solution)/shard_map/all_to_all | solution.py:526
  45.3 0.7 shard_map.41
  46.0 11.1 %all-to-all-start.1 = ((f32[32,2,128]{2,1,0:T(2,128)}), f32[32,2,128]{2,1,0:T(2,128)S(1)}, u32[]{:S(2)}, u32[]{:S(2)}) async-start(f32[32,2,128]{2,1,0:T(2,128)} %shard_map.41), calls=%async_computation.1 | async-start | bytes 65536 | tf_op jit(solution)/shard_map/all_to_all | solution.py:529
  57.0 0.7 shard_map.42
  57.7 0.7 collective-permute-start.4
  58.4 1.1 %collective-permute-start.5 = (f32[128,128]{1,0:T(8,128)S(1)}, f32[128,128]{1,0:T(8,128)S(1)}, u32[]{:S(2)}, u32[]{:S(2)}) collective-permute-start(f32[128,128]{1,0:T(8,128)S(1)} %get-tuple-element.52), channel_id=1, source_target_pairs={{0,1},{1,2},{2,3},{3,4},{4,5},{5,6},{6,7},{7,0},{8,9},{9,10},{10,1... | collective-permute-start | bytes 196616 | tf_op jit(solution)/shard_map/ppermute | solution.py:492
  59.4 2.2 %collective-permute-done.4.got_e.refs_11_ = f32[128,128]{1,0:T(8,128)S(1)} collective-permute-done((f32[128,128]{1,0:T(8,128)S(1)}, f32[128,128]{1,0:T(8,128)S(1)}, u32[]{:S(2)}, u32[]{:S(2)}) %collective-permute-start.4) | collective-permute-done | bytes 65568 | tf_op jit(solution)/shard_map/ppermute | solution.py:492
  61.7 0.0 collective-permute-done.5.got_w.refs_12_
  61.7 0.1 shard_map.43
  61.8 1.3 %collective-permute-start.6 = (f32[280,128]{1,0:T(8,128)S(1)}, f32[280,128]{1,0:T(8,128)S(1)}, u32[]{:S(2)}, u32[]{:S(2)}) collective-permute-start(f32[280,128]{1,0:T(8,128)S(1)} %get-tuple-element.54), channel_id=1, source_target_pairs={{8,0},{16,8},{24,16},{32,24},{40,32},{48,40},{56,48},{64,56},{72,6... | collective-permute-start | bytes 430088 | tf_op jit(solution)/shard_map/ppermute | solution.py:492
  63.1 4.0 %collective-permute-start.7 = (f32[280,128]{1,0:T(8,128)S(1)}, f32[280,128]{1,0:T(8,128)S(1)}, u32[]{:S(2)}, u32[]{:S(2)}) collective-permute-start(f32[280,128]{1,0:T(8,128)S(1)} %get-tuple-element.55), channel_id=1, source_target_pairs={{0,8},{8,16},{16,24},{24,32},{32,40},{40,48},{48,56},{56,64},{64,7... | collective-permute-start | bytes 430088 | tf_op jit(solution)/shard_map/ppermute | solution.py:492
  67.1 0.5 shard_map.38
  67.6 0.6 collective-permute-done.6.refs_13_
  68.1 1.1 %collective-permute-done.7.refs_14_ = f32[280,128]{1,0:T(8,128)S(1)} collective-permute-done((f32[280,128]{1,0:T(8,128)S(1)}, f32[280,128]{1,0:T(8,128)S(1)}, u32[]{:S(2)}, u32[]{:S(2)}) %collective-permute-start.7) | collective-permute-done | bytes 143392 | tf_op jit(solution)/shard_map/ppermute | solution.py:492
  69.3 0.9 %shard_map.44 = (f32[1024,128]{1,0:T(8,128)S(1)}, f32[16,128]{1,0:T(8,128)S(1)}) custom-call(f32[2,128]{1,0:T(2,128)S(1)} %bitcast.12, f32[512,128]{1,0:T(8,128)S(1)} %get-tuple-element.35.st.refs_1_, f32[1024,128]{1,0:T(8,128)S(1)} %get-tuple-element.40.g.refs_2_, f32[512,128]{1,0:T(8,128)S(1)} %get-tuple-element.32.rt.refs_3_.refs_1_, ...), custom_call_target="tpu_custom_call" | custom-call | flops 1000000 | bytes 100000 | tf_op jit(solution)/shard_map/pallas_call | solution.py:547
  70.1 8.9 %all-to-all-done.1.refs_8_ = f32[32,2,128]{2,1,0:T(2,128)S(1)} async-done(((f32[32,2,128]{2,1,0:T(2,128)}), f32[32,2,128]{2,1,0:T(2,128)S(1)}, u32[]{:S(2)}, u32[]{:S(2)}) %all-to-all-start.1) | async-done | bytes 32800 | tf_op jit(solution)/shard_map/all_to_all | solution.py:529
  79.0 2.0 %shard_map.45 = f32[1024,128]{1,0:T(8,128)} custom-call(f32[2,128]{1,0:T(2,128)S(1)} %bitcast.13, f32[512,128]{1,0:T(8,128)S(1)} %get-tuple-element.32.rt.refs_3_.refs_1_, f32[512,128]{1,0:T(8,128)S(1)} %get-tuple-element.36.refs_2_, f32[512,128]{1,0:T(8,128)S(1)} %get-tuple-element.37.refs_3_, f32[512,128]{1,0:T(8,128)S(1)} %get-tuple-element.38.refs_4_, ...), custom_call_target="tpu_custom_call" | custom-call | flops 1000000 | bytes 100000 | tf_op jit(solution)/shard_map/pallas_call | solution.py:550
Async XLA Ops:
  0.0 20.8 %copy-start = (f32[8,8,8,1,2,128]{5,4,3,2,1,0:T(2,128)S(1)}, f32[8,8,8,1,2,128]{5,4,3,2,1,0:T(2,128)}, u32[]{:S(2)}) copy-start(f32[8,8,8,1,2,128]{5,4,3,2,1,0:T(2,128)} %param.3) | copy-start | bytes 1572868
  1.2 19.6 %copy-start.2 = (f32[8,8]{1,0:T(8,128)S(1)}, f32[8,8]{1,0:T(8,128)}, u32[]{:S(2)}) copy-start(f32[8,8]{1,0:T(8,128)} %sv_far.1) | copy-start | bytes 772
  1.2 21.0 %collective-permute-start.2 = (f32[72,128]{1,0:T(8,128)S(1)}, f32[72,128]{1,0:T(8,128)S(1)}, u32[]{:S(2)}, u32[]{:S(2)}) collective-permute-start(f32[72,128]{1,0:T(8,128)S(1)} %get-tuple-element.45), channel_id=1, source_target_pairs={{1,0},{2,1},{3,2},{4,3},{5,4},{6,5},{7,6},{0,7},{9,8},{10,9},{11,1... | collective-permute-start | bytes 110600 | tf_op jit(solution)/shard_map/ppermute | solution.py:492
  15.4 6.8 %collective-permute-start.3 = (f32[72,128]{1,0:T(8,128)S(1)}, f32[72,128]{1,0:T(8,128)S(1)}, u32[]{:S(2)}, u32[]{:S(2)}) collective-permute-start(f32[72,128]{1,0:T(8,128)S(1)} %get-tuple-element.46), channel_id=1, source_target_pairs={{0,1},{1,2},{2,3},{3,4},{4,5},{5,6},{6,7},{7,0},{8,9},{9,10},{10,1... | collective-permute-start | bytes 110600 | tf_op jit(solution)/shard_map/ppermute | solution.py:492
  15.4 5.4 %copy-start.1 = (f32[1,2,128]{2,1,0:T(2,128)S(1)}, f32[1,2,128]{2,1,0:T(2,128)}, u32[]{:S(2)}) copy-start(f32[1,2,128]{2,1,0:T(2,128)} %param.4) | copy-start | bytes 3076
  15.4 6.8 %collective-permute-start = (f32[136,128]{1,0:T(8,128)S(1)}, f32[136,128]{1,0:T(8,128)S(1)}, u32[]{:S(2)}, u32[]{:S(2)}) collective-permute-start(f32[136,128]{1,0:T(8,128)S(1)} %get-tuple-element.43), channel_id=1, source_target_pairs={{8,0},{16,8},{24,16},{32,24},{40,32},{48,40},{56,48},{64,56},{72,6... | collective-permute-start | bytes 208904 | tf_op jit(solution)/shard_map/ppermute | solution.py:492
  16.8 5.4 %collective-permute-start.1 = (f32[136,128]{1,0:T(8,128)S(1)}, f32[136,128]{1,0:T(8,128)S(1)}, u32[]{:S(2)}, u32[]{:S(2)}) collective-permute-start(f32[136,128]{1,0:T(8,128)S(1)} %get-tuple-element.44), channel_id=1, source_target_pairs={{0,8},{8,16},{16,24},{24,32},{32,40},{40,48},{48,56},{56,64},{64,7... | collective-permute-start | bytes 208904 | tf_op jit(solution)/shard_map/ppermute | solution.py:492
  46.0 33.1 %all-to-all-start.1 = ((f32[32,2,128]{2,1,0:T(2,128)}), f32[32,2,128]{2,1,0:T(2,128)S(1)}, u32[]{:S(2)}, u32[]{:S(2)}) async-start(f32[32,2,128]{2,1,0:T(2,128)} %shard_map.41), calls=%async_computation.1 | async-start | bytes 65536 | tf_op jit(solution)/shard_map/all_to_all | solution.py:529
  57.7 4.0 %collective-permute-start.4 = (f32[128,128]{1,0:T(8,128)S(1)}, f32[128,128]{1,0:T(8,128)S(1)}, u32[]{:S(2)}, u32[]{:S(2)}) collective-permute-start(f32[128,128]{1,0:T(8,128)S(1)} %get-tuple-element.51), channel_id=1, source_target_pairs={{1,0},{2,1},{3,2},{4,3},{5,4},{6,5},{7,6},{0,7},{9,8},{10,9},{11,1... | collective-permute-start | bytes 196616 | tf_op jit(solution)/shard_map/ppermute | solution.py:492
  58.4 3.3 %collective-permute-start.5 = (f32[128,128]{1,0:T(8,128)S(1)}, f32[128,128]{1,0:T(8,128)S(1)}, u32[]{:S(2)}, u32[]{:S(2)}) collective-permute-start(f32[128,128]{1,0:T(8,128)S(1)} %get-tuple-element.52), channel_id=1, source_target_pairs={{0,1},{1,2},{2,3},{3,4},{4,5},{5,6},{6,7},{7,0},{8,9},{9,10},{10,1... | collective-permute-start | bytes 196616 | tf_op jit(solution)/shard_map/ppermute | solution.py:492
  61.8 6.4 %collective-permute-start.6 = (f32[280,128]{1,0:T(8,128)S(1)}, f32[280,128]{1,0:T(8,128)S(1)}, u32[]{:S(2)}, u32[]{:S(2)}) collective-permute-start(f32[280,128]{1,0:T(8,128)S(1)} %get-tuple-element.54), channel_id=1, source_target_pairs={{8,0},{16,8},{24,16},{32,24},{40,32},{48,40},{56,48},{64,56},{72,6... | collective-permute-start | bytes 430088 | tf_op jit(solution)/shard_map/ppermute | solution.py:492
  63.1 6.2 %collective-permute-start.7 = (f32[280,128]{1,0:T(8,128)S(1)}, f32[280,128]{1,0:T(8,128)S(1)}, u32[]{:S(2)}, u32[]{:S(2)}) collective-permute-start(f32[280,128]{1,0:T(8,128)S(1)} %get-tuple-element.55), channel_id=1, source_target_pairs={{0,8},{8,16},{16,24},{24,32},{32,40},{40,48},{48,56},{56,64},{64,7... | collective-permute-start | bytes 430088 | tf_op jit(solution)/shard_map/ppermute | solution.py:492

commit v6 on v5

--- a/solution.py
+++ b/solution.py
@@ -526,7 +526,8 @@
         near = lax.all_to_all(sums, ("y", "x", "c"), 0, 0)
         (near,) = call(fold, "v", [jax.ShapeDtypeStruct((nz, 2, 128), f32)])(near)
         near, it = lax.optimization_barrier((near, it))
-        ring = lax.all_to_all(near, "z", 0, 0)
+        turned = [(k + nz // 2) % nz for k in range(nz)]
+        ring = lax.all_to_all(near, "z", 0, 0, axis_index_groups=[turned])
         post, *spans_out = call(smooth, "vvvvvv", [field, rows(2 * N * N), rows(2 * N * N)], cost=10**9)(
             coef, st, g, rt, kk, it
         )

time: 81.3 us -> 87.3 us (1.074)
  the two profiles are of different devices: /device:TPU:1 before, /device:TPU:8 now
where the time goes in v6:
time: 87.3 us; the launch traced here: 87 us
  starting transfers between devices  51 us (58%)
  waiting for transfers between devices  15.8 us (18%)
  blocking collectives  12.6 us (14%)
  Pallas kernels  7.51 us (9%)
    ppermute x4, starting transfers between devices, exchange(): lax.ppermute(block_down, axis, down)  24.6 us
    all_to_all x1, starting transfers between devices, per_device(): ring = lax.all_to_all(near, 'z', 0, 0, axis_index_groups=[turned])  21.8 us
    ppermute x4, waiting for transfers between devices, exchange(): lax.ppermute(block_up, axis, up)  13.4 us
    all_to_all x1, blocking collectives, per_device(): near = lax.all_to_all(sums, ('y', 'x', 'c'), 0, 0)  12.6 us
    ppermute x4, starting transfers between devices, exchange(): lax.ppermute(block_up, axis, up)  4.61 us
    ppermute x4, waiting for transfers between devices, exchange(): lax.ppermute(block_down, axis, down)  2.37 us
    pallas_call x1, Pallas kernels, per_device(): call(last, 'v' * 9, [field], scratch)(coef, rt, *parts, base, faces, ring)  1.99 us
  transfers between devices with their start and end apart: 9, of which 5 were waited for; matrix products, arithmetic and copies ran while one was open for 0% of the time, Pallas kernels for 4%

profile of v6, /device:TPU:8, one launch (start us, length us, event | category | flops | bytes accessed | tf_op | source)
XLA Modules:
  0.0 87.0 jit_solution(1277644275564099323)
XLA Ops:
  0.0 0.0 copy-start
  0.0 1.2 %shard_map.39 = (f32[136,128]{1,0:T(8,128)S(1)}, f32[136,128]{1,0:T(8,128)S(1)}, f32[72,128]{1,0:T(8,128)S(1)}, f32[72,128]{1,0:T(8,128)S(1)}) custom-call(f32[1024,128]{1,0:T(8,128)} %bitcast.5, f32[2,128]{1,0:T(2,128)} %bitcast.7, f32[8,8]{1,0:T(8,128)} %sv_far.1), custom_call_target="tpu_custom_call" | custom-call | flops 1000000 | bytes 100000 | tf_op jit(solution)/shard_map/pallas_call | solution.py:506
  1.2 0.0 copy-start.2
  1.2 2.2 %collective-permute-start.2 = (f32[72,128]{1,0:T(8,128)S(1)}, f32[72,128]{1,0:T(8,128)S(1)}, u32[]{:S(2)}, u32[]{:S(2)}) collective-permute-start(f32[72,128]{1,0:T(8,128)S(1)} %get-tuple-element.45), channel_id=1, source_target_pairs={{1,0},{2,1},{3,2},{4,3},{5,4},{6,5},{7,6},{0,7},{9,8},{10,9},{11,1... | collective-permute-start | bytes 110600 | tf_op jit(solution)/shard_map/ppermute | solution.py:492
  3.4 0.0 collective-permute-start.3
  3.4 0.0 copy-start.1
  3.4 18.7 %collective-permute-start = (f32[136,128]{1,0:T(8,128)S(1)}, f32[136,128]{1,0:T(8,128)S(1)}, u32[]{:S(2)}, u32[]{:S(2)}) collective-permute-start(f32[136,128]{1,0:T(8,128)S(1)} %get-tuple-element.43), channel_id=1, source_target_pairs={{8,0},{16,8},{24,16},{32,24},{40,32},{48,40},{56,48},{64,56},{72,6... | collective-permute-start | bytes 208904 | tf_op jit(solution)/shard_map/ppermute | solution.py:492
  22.1 1.9 %collective-permute-start.1 = (f32[136,128]{1,0:T(8,128)S(1)}, f32[136,128]{1,0:T(8,128)S(1)}, u32[]{:S(2)}, u32[]{:S(2)}) collective-permute-start(f32[136,128]{1,0:T(8,128)S(1)} %get-tuple-element.44), channel_id=1, source_target_pairs={{0,8},{8,16},{16,24},{24,32},{32,40},{40,48},{48,56},{56,64},{64,7... | collective-permute-start | bytes 208904 | tf_op jit(solution)/shard_map/ppermute | solution.py:492
  24.0 0.0 copy-done
  24.0 0.0 copy-done.2
  24.1 0.0 copy-done.1
  24.1 1.3 %shard_map.37 = (f32[1024,128]{1,0:T(8,128)S(1)}, f32[512,128]{1,0:T(8,128)S(1)}, f32[512,128]{1,0:T(8,128)S(1)}, bf16[128,64]{1,0:T(8,128)(2,1)S(1)}, f32[512,1...) custom-call(f32[1024,128]{1,0:T(8,128)S(1)} %bitcast.6, f32[2,128]{1,0:T(2,128)S(1)} %bitcast.8, ...), custom_call_target="tpu_custom_call" | custom-call | flops 1000000000 | bytes 100000 | tf_op jit(solution)/shard_map/pallas_call | solution.py:520
  25.4 0.0 collective-permute-done.2.from_e.refs_9_
  25.4 0.0 collective-permute-done.3.from_w.refs_10_
  25.4 0.0 collective-permute-done.from_n.refs_7_
  25.5 5.0 %collective-permute-done.1.from_s.refs_8_ = f32[136,128]{1,0:T(8,128)S(1)} collective-permute-done((f32[136,128]{1,0:T(8,128)S(1)}, f32[136,128]{1,0:T(8,128)S(1)}, u32[]{:S(2)}, u32[]{:S(2)}) %collective-permute-start.1) | collective-permute-done | bytes 69664 | tf_op jit(solution)/shard_map/ppermute | solution.py:492
  30.4 0.2 shard_map.40
  30.7 12.6 %all_to_all.10.parts = f32[32,2,128]{2,1,0:T(2,128)S(1)} all-to-all(f32[32,2,128]{2,1,0:T(2,128)S(1)} %get-tuple-element.47), channel_id=1, replica_groups=mesh['y'=4,'z'=32,'x'=4,'c'=2] {'y','x','c'}, dimensions={0} | all-to-all | bytes 65536 | tf_op jit(solution)/shard_map/all_to_all | solution.py:526
  43.2 0.7 shard_map.41
  43.9 21.8 %all-to-all-start.1 = ((f32[32,2,128]{2,1,0:T(2,128)}), f32[32,2,128]{2,1,0:T(2,128)S(1)}, u32[]{:S(2)}, u32[]{:S(2)}) async-start(f32[32,2,128]{2,1,0:T(2,128)} %shard_map.41), calls=%async_computation.1 | async-start | bytes 65536 | tf_op jit(solution)/shard_map/all_to_all | solution.py:530
  65.7 0.7 shard_map.42
  66.3 0.4 collective-permute-start.4
  66.7 0.2 collective-permute-start.5
  66.9 1.7 %collective-permute-done.4.got_e.refs_11_ = f32[128,128]{1,0:T(8,128)S(1)} collective-permute-done((f32[128,128]{1,0:T(8,128)S(1)}, f32[128,128]{1,0:T(8,128)S(1)}, u32[]{:S(2)}, u32[]{:S(2)}) %collective-permute-start.4) | collective-permute-done | bytes 65568 | tf_op jit(solution)/shard_map/ppermute | solution.py:492
  68.6 3.0 %collective-permute-done.5.got_w.refs_12_ = f32[128,128]{1,0:T(8,128)S(1)} collective-permute-done((f32[128,128]{1,0:T(8,128)S(1)}, f32[128,128]{1,0:T(8,128)S(1)}, u32[]{:S(2)}, u32[]{:S(2)}) %collective-permute-start.5) | collective-permute-done | bytes 65568 | tf_op jit(solution)/shard_map/ppermute | solution.py:492
  71.6 0.1 shard_map.43
  71.7 3.3 %collective-permute-start.6 = (f32[280,128]{1,0:T(8,128)S(1)}, f32[280,128]{1,0:T(8,128)S(1)}, u32[]{:S(2)}, u32[]{:S(2)}) collective-permute-start(f32[280,128]{1,0:T(8,128)S(1)} %get-tuple-element.54), channel_id=1, source_target_pairs={{8,0},{16,8},{24,16},{32,24},{40,32},{48,40},{56,48},{64,56},{72,6... | collective-permute-start | bytes 430088 | tf_op jit(solution)/shard_map/ppermute | solution.py:492
  75.0 2.5 %collective-permute-start.7 = (f32[280,128]{1,0:T(8,128)S(1)}, f32[280,128]{1,0:T(8,128)S(1)}, u32[]{:S(2)}, u32[]{:S(2)}) collective-permute-start(f32[280,128]{1,0:T(8,128)S(1)} %get-tuple-element.55), channel_id=1, source_target_pairs={{0,8},{8,16},{16,24},{24,32},{32,40},{40,48},{48,56},{56,64},{64,7... | collective-permute-start | bytes 430088 | tf_op jit(solution)/shard_map/ppermute | solution.py:492
  77.5 0.5 shard_map.38
  78.1 0.6 collective-permute-done.6.refs_13_
  78.7 5.4 %collective-permute-done.7.refs_14_ = f32[280,128]{1,0:T(8,128)S(1)} collective-permute-done((f32[280,128]{1,0:T(8,128)S(1)}, f32[280,128]{1,0:T(8,128)S(1)}, u32[]{:S(2)}, u32[]{:S(2)}) %collective-permute-start.7) | collective-permute-done | bytes 143392 | tf_op jit(solution)/shard_map/ppermute | solution.py:492
  84.1 0.9 shard_map.44
  85.0 0.0 all-to-all-done.1.refs_8_
  85.0 2.0 %shard_map.45 = f32[1024,128]{1,0:T(8,128)} custom-call(f32[2,128]{1,0:T(2,128)S(1)} %bitcast.13, f32[512,128]{1,0:T(8,128)S(1)} %get-tuple-element.32.rt.refs_3_.refs_1_, f32[512,128]{1,0:T(8,128)S(1)} %get-tuple-element.36.refs_2_, f32[512,128]{1,0:T(8,128)S(1)} %get-tuple-element.37.refs_3_, f32[512,128]{1,0:T(8,128)S(1)} %get-tuple-element.38.refs_4_, ...), custom_call_target="tpu_custom_call" | custom-call | flops 1000000 | bytes 100000 | tf_op jit(solution)/shard_map/pallas_call | solution.py:551
Async XLA Ops:
  0.0 24.0 %copy-start = (f32[8,8,8,1,2,128]{5,4,3,2,1,0:T(2,128)S(1)}, f32[8,8,8,1,2,128]{5,4,3,2,1,0:T(2,128)}, u32[]{:S(2)}) copy-start(f32[8,8,8,1,2,128]{5,4,3,2,1,0:T(2,128)} %param.3) | copy-start | bytes 1572868
  1.2 22.9 %copy-start.2 = (f32[8,8]{1,0:T(8,128)S(1)}, f32[8,8]{1,0:T(8,128)}, u32[]{:S(2)}) copy-start(f32[8,8]{1,0:T(8,128)} %sv_far.1) | copy-start | bytes 772
  1.2 24.2 %collective-permute-start.2 = (f32[72,128]{1,0:T(8,128)S(1)}, f32[72,128]{1,0:T(8,128)S(1)}, u32[]{:S(2)}, u32[]{:S(2)}) collective-permute-start(f32[72,128]{1,0:T(8,128)S(1)} %get-tuple-element.45), channel_id=1, source_target_pairs={{1,0},{2,1},{3,2},{4,3},{5,4},{6,5},{7,6},{0,7},{9,8},{10,9},{11,1... | collective-permute-start | bytes 110600 | tf_op jit(solution)/shard_map/ppermute | solution.py:492
  3.4 22.0 %collective-permute-start.3 = (f32[72,128]{1,0:T(8,128)S(1)}, f32[72,128]{1,0:T(8,128)S(1)}, u32[]{:S(2)}, u32[]{:S(2)}) collective-permute-start(f32[72,128]{1,0:T(8,128)S(1)} %get-tuple-element.46), channel_id=1, source_target_pairs={{0,1},{1,2},{2,3},{3,4},{4,5},{5,6},{6,7},{7,0},{8,9},{9,10},{10,1... | collective-permute-start | bytes 110600 | tf_op jit(solution)/shard_map/ppermute | solution.py:492
  3.4 20.6 %copy-start.1 = (f32[1,2,128]{2,1,0:T(2,128)S(1)}, f32[1,2,128]{2,1,0:T(2,128)}, u32[]{:S(2)}) copy-start(f32[1,2,128]{2,1,0:T(2,128)} %param.4) | copy-start | bytes 3076
  3.4 22.0 %collective-permute-start = (f32[136,128]{1,0:T(8,128)S(1)}, f32[136,128]{1,0:T(8,128)S(1)}, u32[]{:S(2)}, u32[]{:S(2)}) collective-permute-start(f32[136,128]{1,0:T(8,128)S(1)} %get-tuple-element.43), channel_id=1, source_target_pairs={{8,0},{16,8},{24,16},{32,24},{40,32},{48,40},{56,48},{64,56},{72,6... | collective-permute-start | bytes 208904 | tf_op jit(solution)/shard_map/ppermute | solution.py:492
  22.1 8.3 %collective-permute-start.1 = (f32[136,128]{1,0:T(8,128)S(1)}, f32[136,128]{1,0:T(8,128)S(1)}, u32[]{:S(2)}, u32[]{:S(2)}) collective-permute-start(f32[136,128]{1,0:T(8,128)S(1)} %get-tuple-element.44), channel_id=1, source_target_pairs={{0,8},{8,16},{16,24},{24,32},{32,40},{40,48},{48,56},{56,64},{64,7... | collective-permute-start | bytes 208904 | tf_op jit(solution)/shard_map/ppermute | solution.py:492
  43.9 41.1 %all-to-all-start.1 = ((f32[32,2,128]{2,1,0:T(2,128)}), f32[32,2,128]{2,1,0:T(2,128)S(1)}, u32[]{:S(2)}, u32[]{:S(2)}) async-start(f32[32,2,128]{2,1,0:T(2,128)} %shard_map.41), calls=%async_computation.1 | async-start | bytes 65536 | tf_op jit(solution)/shard_map/all_to_all | solution.py:530
  66.3 2.3 %collective-permute-start.4 = (f32[128,128]{1,0:T(8,128)S(1)}, f32[128,128]{1,0:T(8,128)S(1)}, u32[]{:S(2)}, u32[]{:S(2)}) collective-permute-start(f32[128,128]{1,0:T(8,128)S(1)} %get-tuple-element.51), channel_id=1, source_target_pairs={{1,0},{2,1},{3,2},{4,3},{5,4},{6,5},{7,6},{0,7},{9,8},{10,9},{11,1... | collective-permute-start | bytes 196616 | tf_op jit(solution)/shard_map/ppermute | solution.py:492
  66.7 4.9 %collective-permute-start.5 = (f32[128,128]{1,0:T(8,128)S(1)}, f32[128,128]{1,0:T(8,128)S(1)}, u32[]{:S(2)}, u32[]{:S(2)}) collective-permute-start(f32[128,128]{1,0:T(8,128)S(1)} %get-tuple-element.52), channel_id=1, source_target_pairs={{0,1},{1,2},{2,3},{3,4},{4,5},{5,6},{6,7},{7,0},{8,9},{9,10},{10,1... | collective-permute-start | bytes 196616 | tf_op jit(solution)/shard_map/ppermute | solution.py:492
  71.7 7.0 %collective-permute-start.6 = (f32[280,128]{1,0:T(8,128)S(1)}, f32[280,128]{1,0:T(8,128)S(1)}, u32[]{:S(2)}, u32[]{:S(2)}) collective-permute-start(f32[280,128]{1,0:T(8,128)S(1)} %get-tuple-element.54), channel_id=1, source_target_pairs={{8,0},{16,8},{24,16},{32,24},{40,32},{48,40},{56,48},{64,56},{72,6... | collective-permute-start | bytes 430088 | tf_op jit(solution)/shard_map/ppermute | solution.py:492
  75.0 9.1 %collective-permute-start.7 = (f32[280,128]{1,0:T(8,128)S(1)}, f32[280,128]{1,0:T(8,128)S(1)}, u32[]{:S(2)}, u32[]{:S(2)}) collective-permute-start(f32[280,128]{1,0:T(8,128)S(1)} %get-tuple-element.55), channel_id=1, source_target_pairs={{0,8},{8,16},{16,24},{24,32},{32,40},{40,48},{48,56},{56,64},{64,7... | collective-permute-start | bytes 430088 | tf_op jit(solution)/shard_map/ppermute | solution.py:492

commit v7 on v6

--- a/solution.py
+++ b/solution.py
@@ -526,7 +526,7 @@
         near = lax.all_to_all(sums, ("y", "x", "c"), 0, 0)
         (near,) = call(fold, "v", [jax.ShapeDtypeStruct((nz, 2, 128), f32)])(near)
         near, it = lax.optimization_barrier((near, it))
-        turned = [(k + nz // 2) % nz for k in range(nz)]
+        turned = [(k + nz // 6) % nz for k in range(nz)]
         ring = lax.all_to_all(near, "z", 0, 0, axis_index_groups=[turned])
         post, *spans_out = call(smooth, "vvvvvv", [field, rows(2 * N * N), rows(2 * N * N)], cost=10**9)(
             coef, st, g, rt, kk, it

time: 87.3 us -> 83.1 us (0.952)
  starting transfers between devices: 51 us -> 46.2 us
    all_to_all x1, starting transfers between devices: 21.8 us -> 15.5 us  [per_device(): ring = lax.all_to_all(near, 'z', 0, 0, axis_index_groups=[turned])]
    ppermute x4, starting transfers between devices: 24.6 us -> 26.7 us  [exchange(): lax.ppermute(block_down, axis, down)]
    ppermute x4, waiting for transfers between devices: 13.4 us -> 14.4 us  [exchange(): lax.ppermute(block_up, axis, up)]
where the time goes in v7:
time: 83.1 us; the launch traced here: 82.8 us
  starting transfers between devices  46.2 us (56%)
  waiting for transfers between devices  16.4 us (20%)
  blocking collectives  12.6 us (15%)
  Pallas kernels  7.51 us (9%)
    ppermute x4, starting transfers between devices, exchange(): lax.ppermute(block_down, axis, down)  26.7 us
    all_to_all x1, starting transfers between devices, per_device(): ring = lax.all_to_all(near, 'z', 0, 0, axis_index_groups=[turned])  15.5 us
    ppermute x4, waiting for transfers between devices, exchange(): lax.ppermute(block_up, axis, up)  14.4 us
    all_to_all x1, blocking collectives, per_device(): near = lax.all_to_all(sums, ('y', 'x', 'c'), 0, 0)  12.6 us
    ppermute x4, starting transfers between devices, exchange(): lax.ppermute(block_up, axis, up)  4.01 us
    pallas_call x1, Pallas kernels, per_device(): call(last, 'v' * 9, [field], scratch)(coef, rt, *parts, base, faces, ring)  1.99 us
    ppermute x4, waiting for transfers between devices, exchange(): lax.ppermute(block_down, axis, down)  1.94 us
  transfers between devices with their start and end apart: 9, of which 5 were waited for; matrix products, arithmetic and copies ran while one was open for 0% of the time, Pallas kernels for 4%

profile of v7, /device:TPU:8, one launch (start us, length us, event | category | flops | bytes accessed | tf_op | source)
XLA Modules:
  0.0 82.8 jit_solution(16344983818046104617)
XLA Ops:
  0.0 0.0 copy-start
  0.0 1.2 %shard_map.39 = (f32[136,128]{1,0:T(8,128)S(1)}, f32[136,128]{1,0:T(8,128)S(1)}, f32[72,128]{1,0:T(8,128)S(1)}, f32[72,128]{1,0:T(8,128)S(1)}) custom-call(f32[1024,128]{1,0:T(8,128)} %bitcast.5, f32[2,128]{1,0:T(2,128)} %bitcast.7, f32[8,8]{1,0:T(8,128)} %sv_far.1), custom_call_target="tpu_custom_call" | custom-call | flops 1000000 | bytes 100000 | tf_op jit(solution)/shard_map/pallas_call | solution.py:506
  1.2 0.0 copy-start.2
  1.2 2.2 %collective-permute-start.2 = (f32[72,128]{1,0:T(8,128)S(1)}, f32[72,128]{1,0:T(8,128)S(1)}, u32[]{:S(2)}, u32[]{:S(2)}) collective-permute-start(f32[72,128]{1,0:T(8,128)S(1)} %get-tuple-element.45), channel_id=1, source_target_pairs={{1,0},{2,1},{3,2},{4,3},{5,4},{6,5},{7,6},{0,7},{9,8},{10,9},{11,1... | collective-permute-start | bytes 110600 | tf_op jit(solution)/shard_map/ppermute | solution.py:492
  3.4 0.0 collective-permute-start.3
  3.4 0.0 copy-start.1
  3.4 18.7 %collective-permute-start = (f32[136,128]{1,0:T(8,128)S(1)}, f32[136,128]{1,0:T(8,128)S(1)}, u32[]{:S(2)}, u32[]{:S(2)}) collective-permute-start(f32[136,128]{1,0:T(8,128)S(1)} %get-tuple-element.43), channel_id=1, source_target_pairs={{8,0},{16,8},{24,16},{32,24},{40,32},{48,40},{56,48},{64,56},{72,6... | collective-permute-start | bytes 208904 | tf_op jit(solution)/shard_map/ppermute | solution.py:492
  22.1 1.9 %collective-permute-start.1 = (f32[136,128]{1,0:T(8,128)S(1)}, f32[136,128]{1,0:T(8,128)S(1)}, u32[]{:S(2)}, u32[]{:S(2)}) collective-permute-start(f32[136,128]{1,0:T(8,128)S(1)} %get-tuple-element.44), channel_id=1, source_target_pairs={{0,8},{8,16},{16,24},{24,32},{32,40},{40,48},{48,56},{56,64},{64,7... | collective-permute-start | bytes 208904 | tf_op jit(solution)/shard_map/ppermute | solution.py:492
  24.0 0.0 copy-done
  24.0 0.0 copy-done.2
  24.1 0.0 copy-done.1
  24.1 1.3 %shard_map.37 = (f32[1024,128]{1,0:T(8,128)S(1)}, f32[512,128]{1,0:T(8,128)S(1)}, f32[512,128]{1,0:T(8,128)S(1)}, bf16[128,64]{1,0:T(8,128)(2,1)S(1)}, f32[512,1...) custom-call(f32[1024,128]{1,0:T(8,128)S(1)} %bitcast.6, f32[2,128]{1,0:T(2,128)S(1)} %bitcast.8, ...), custom_call_target="tpu_custom_call" | custom-call | flops 1000000000 | bytes 100000 | tf_op jit(solution)/shard_map/pallas_call | solution.py:520
  25.4 0.0 collective-permute-done.2.from_e.refs_9_
  25.4 0.0 collective-permute-done.3.from_w.refs_10_
  25.4 0.0 collective-permute-done.from_n.refs_7_
  25.5 5.0 %collective-permute-done.1.from_s.refs_8_ = f32[136,128]{1,0:T(8,128)S(1)} collective-permute-done((f32[136,128]{1,0:T(8,128)S(1)}, f32[136,128]{1,0:T(8,128)S(1)}, u32[]{:S(2)}, u32[]{:S(2)}) %collective-permute-start.1) | collective-permute-done | bytes 69664 | tf_op jit(solution)/shard_map/ppermute | solution.py:492
  30.4 0.2 shard_map.40
  30.7 12.6 %all_to_all.10.parts = f32[32,2,128]{2,1,0:T(2,128)S(1)} all-to-all(f32[32,2,128]{2,1,0:T(2,128)S(1)} %get-tuple-element.47), channel_id=1, replica_groups=mesh['y'=4,'z'=32,'x'=4,'c'=2] {'y','x','c'}, dimensions={0} | all-to-all | bytes 65536 | tf_op jit(solution)/shard_map/all_to_all | solution.py:526
  43.2 0.7 shard_map.41
  43.9 15.5 %all-to-all-start.1 = ((f32[32,2,128]{2,1,0:T(2,128)}), f32[32,2,128]{2,1,0:T(2,128)S(1)}, u32[]{:S(2)}, u32[]{:S(2)}) async-start(f32[32,2,128]{2,1,0:T(2,128)} %shard_map.41), calls=%async_computation.1 | async-start | bytes 65536 | tf_op jit(solution)/shard_map/all_to_all | solution.py:530
  59.4 0.7 shard_map.42
  60.1 0.4 collective-permute-start.4
  60.4 0.2 collective-permute-start.5
  60.6 1.7 %collective-permute-done.4.got_e.refs_11_ = f32[128,128]{1,0:T(8,128)S(1)} collective-permute-done((f32[128,128]{1,0:T(8,128)S(1)}, f32[128,128]{1,0:T(8,128)S(1)}, u32[]{:S(2)}, u32[]{:S(2)}) %collective-permute-start.4) | collective-permute-done | bytes 65568 | tf_op jit(solution)/shard_map/ppermute | solution.py:492
  62.3 3.0 %collective-permute-done.5.got_w.refs_12_ = f32[128,128]{1,0:T(8,128)S(1)} collective-permute-done((f32[128,128]{1,0:T(8,128)S(1)}, f32[128,128]{1,0:T(8,128)S(1)}, u32[]{:S(2)}, u32[]{:S(2)}) %collective-permute-start.5) | collective-permute-done | bytes 65568 | tf_op jit(solution)/shard_map/ppermute | solution.py:492
  65.3 0.1 shard_map.43
  65.4 5.4 %collective-permute-start.6 = (f32[280,128]{1,0:T(8,128)S(1)}, f32[280,128]{1,0:T(8,128)S(1)}, u32[]{:S(2)}, u32[]{:S(2)}) collective-permute-start(f32[280,128]{1,0:T(8,128)S(1)} %get-tuple-element.54), channel_id=1, source_target_pairs={{8,0},{16,8},{24,16},{32,24},{40,32},{48,40},{56,48},{64,56},{72,6... | collective-permute-start | bytes 430088 | tf_op jit(solution)/shard_map/ppermute | solution.py:492
  70.8 1.9 %collective-permute-start.7 = (f32[280,128]{1,0:T(8,128)S(1)}, f32[280,128]{1,0:T(8,128)S(1)}, u32[]{:S(2)}, u32[]{:S(2)}) collective-permute-start(f32[280,128]{1,0:T(8,128)S(1)} %get-tuple-element.55), channel_id=1, source_target_pairs={{0,8},{8,16},{16,24},{24,32},{32,40},{40,48},{48,56},{56,64},{64,7... | collective-permute-start | bytes 430088 | tf_op jit(solution)/shard_map/ppermute | solution.py:492
  72.7 0.5 shard_map.38
  73.3 0.2 collective-permute-done.6.refs_13_
  73.4 6.5 %collective-permute-done.7.refs_14_ = f32[280,128]{1,0:T(8,128)S(1)} collective-permute-done((f32[280,128]{1,0:T(8,128)S(1)}, f32[280,128]{1,0:T(8,128)S(1)}, u32[]{:S(2)}, u32[]{:S(2)}) %collective-permute-start.7) | collective-permute-done | bytes 143392 | tf_op jit(solution)/shard_map/ppermute | solution.py:492
  79.9 0.9 %shard_map.44 = (f32[1024,128]{1,0:T(8,128)S(1)}, f32[16,128]{1,0:T(8,128)S(1)}) custom-call(f32[2,128]{1,0:T(2,128)S(1)} %bitcast.12, f32[512,128]{1,0:T(8,128)S(1)} %get-tuple-element.35.st.refs_1_, f32[1024,128]{1,0:T(8,128)S(1)} %get-tuple-element.40.g.refs_2_, f32[512,128]{1,0:T(8,128)S(1)} %get-tuple-element.32.rt.refs_3_.refs_1_, ...), custom_call_target="tpu_custom_call" | custom-call | flops 1000000 | bytes 100000 | tf_op jit(solution)/shard_map/pallas_call | solution.py:548
  80.8 0.0 all-to-all-done.1.refs_8_
  80.8 2.0 %shard_map.45 = f32[1024,128]{1,0:T(8,128)} custom-call(f32[2,128]{1,0:T(2,128)S(1)} %bitcast.13, f32[512,128]{1,0:T(8,128)S(1)} %get-tuple-element.32.rt.refs_3_.refs_1_, f32[512,128]{1,0:T(8,128)S(1)} %get-tuple-element.36.refs_2_, f32[512,128]{1,0:T(8,128)S(1)} %get-tuple-element.37.refs_3_, f32[512,128]{1,0:T(8,128)S(1)} %get-tuple-element.38.refs_4_, ...), custom_call_target="tpu_custom_call" | custom-call | flops 1000000 | bytes 100000 | tf_op jit(solution)/shard_map/pallas_call | solution.py:551
Async XLA Ops:
  0.0 24.0 %copy-start = (f32[8,8,8,1,2,128]{5,4,3,2,1,0:T(2,128)S(1)}, f32[8,8,8,1,2,128]{5,4,3,2,1,0:T(2,128)}, u32[]{:S(2)}) copy-start(f32[8,8,8,1,2,128]{5,4,3,2,1,0:T(2,128)} %param.3) | copy-start | bytes 1572868
  1.2 22.9 %copy-start.2 = (f32[8,8]{1,0:T(8,128)S(1)}, f32[8,8]{1,0:T(8,128)}, u32[]{:S(2)}) copy-start(f32[8,8]{1,0:T(8,128)} %sv_far.1) | copy-start | bytes 772
  1.2 24.2 %collective-permute-start.2 = (f32[72,128]{1,0:T(8,128)S(1)}, f32[72,128]{1,0:T(8,128)S(1)}, u32[]{:S(2)}, u32[]{:S(2)}) collective-permute-start(f32[72,128]{1,0:T(8,128)S(1)} %get-tuple-element.45), channel_id=1, source_target_pairs={{1,0},{2,1},{3,2},{4,3},{5,4},{6,5},{7,6},{0,7},{9,8},{10,9},{11,1... | collective-permute-start | bytes 110600 | tf_op jit(solution)/shard_map/ppermute | solution.py:492
  3.4 22.0 %collective-permute-start.3 = (f32[72,128]{1,0:T(8,128)S(1)}, f32[72,128]{1,0:T(8,128)S(1)}, u32[]{:S(2)}, u32[]{:S(2)}) collective-permute-start(f32[72,128]{1,0:T(8,128)S(1)} %get-tuple-element.46), channel_id=1, source_target_pairs={{0,1},{1,2},{2,3},{3,4},{4,5},{5,6},{6,7},{7,0},{8,9},{9,10},{10,1... | collective-permute-start | bytes 110600 | tf_op jit(solution)/shard_map/ppermute | solution.py:492
  3.4 20.6 %copy-start.1 = (f32[1,2,128]{2,1,0:T(2,128)S(1)}, f32[1,2,128]{2,1,0:T(2,128)}, u32[]{:S(2)}) copy-start(f32[1,2,128]{2,1,0:T(2,128)} %param.4) | copy-start | bytes 3076
  3.4 22.0 %collective-permute-start = (f32[136,128]{1,0:T(8,128)S(1)}, f32[136,128]{1,0:T(8,128)S(1)}, u32[]{:S(2)}, u32[]{:S(2)}) collective-permute-start(f32[136,128]{1,0:T(8,128)S(1)} %get-tuple-element.43), channel_id=1, source_target_pairs={{8,0},{16,8},{24,16},{32,24},{40,32},{48,40},{56,48},{64,56},{72,6... | collective-permute-start | bytes 208904 | tf_op jit(solution)/shard_map/ppermute | solution.py:492
  22.1 8.3 %collective-permute-start.1 = (f32[136,128]{1,0:T(8,128)S(1)}, f32[136,128]{1,0:T(8,128)S(1)}, u32[]{:S(2)}, u32[]{:S(2)}) collective-permute-start(f32[136,128]{1,0:T(8,128)S(1)} %get-tuple-element.44), channel_id=1, source_target_pairs={{0,8},{8,16},{16,24},{24,32},{32,40},{40,48},{48,56},{56,64},{64,7... | collective-permute-start | bytes 208904 | tf_op jit(solution)/shard_map/ppermute | solution.py:492
  43.9 36.9 %all-to-all-start.1 = ((f32[32,2,128]{2,1,0:T(2,128)}), f32[32,2,128]{2,1,0:T(2,128)S(1)}, u32[]{:S(2)}, u32[]{:S(2)}) async-start(f32[32,2,128]{2,1,0:T(2,128)} %shard_map.41), calls=%async_computation.1 | async-start | bytes 65536 | tf_op jit(solution)/shard_map/all_to_all | solution.py:530
  60.1 2.3 %collective-permute-start.4 = (f32[128,128]{1,0:T(8,128)S(1)}, f32[128,128]{1,0:T(8,128)S(1)}, u32[]{:S(2)}, u32[]{:S(2)}) collective-permute-start(f32[128,128]{1,0:T(8,128)S(1)} %get-tuple-element.51), channel_id=1, source_target_pairs={{1,0},{2,1},{3,2},{4,3},{5,4},{6,5},{7,6},{0,7},{9,8},{10,9},{11,1... | collective-permute-start | bytes 196616 | tf_op jit(solution)/shard_map/ppermute | solution.py:492
  60.4 4.9 %collective-permute-start.5 = (f32[128,128]{1,0:T(8,128)S(1)}, f32[128,128]{1,0:T(8,128)S(1)}, u32[]{:S(2)}, u32[]{:S(2)}) collective-permute-start(f32[128,128]{1,0:T(8,128)S(1)} %get-tuple-element.52), channel_id=1, source_target_pairs={{0,1},{1,2},{2,3},{3,4},{4,5},{5,6},{6,7},{7,0},{8,9},{9,10},{10,1... | collective-permute-start | bytes 196616 | tf_op jit(solution)/shard_map/ppermute | solution.py:492
  65.4 8.1 %collective-permute-start.6 = (f32[280,128]{1,0:T(8,128)S(1)}, f32[280,128]{1,0:T(8,128)S(1)}, u32[]{:S(2)}, u32[]{:S(2)}) collective-permute-start(f32[280,128]{1,0:T(8,128)S(1)} %get-tuple-element.54), channel_id=1, source_target_pairs={{8,0},{16,8},{24,16},{32,24},{40,32},{48,40},{56,48},{64,56},{72,6... | collective-permute-start | bytes 430088 | tf_op jit(solution)/shard_map/ppermute | solution.py:492
  70.8 9.1 %collective-permute-start.7 = (f32[280,128]{1,0:T(8,128)S(1)}, f32[280,128]{1,0:T(8,128)S(1)}, u32[]{:S(2)}, u32[]{:S(2)}) collective-permute-start(f32[280,128]{1,0:T(8,128)S(1)} %get-tuple-element.55), channel_id=1, source_target_pairs={{0,8},{8,16},{16,24},{24,32},{32,40},{40,48},{48,56},{56,64},{64,7... | collective-permute-start | bytes 430088 | tf_op jit(solution)/shard_map/ppermute | solution.py:492

commit v8 on v7

--- a/solution.py
+++ b/solution.py
@@ -526,7 +526,7 @@
         near = lax.all_to_all(sums, ("y", "x", "c"), 0, 0)
         (near,) = call(fold, "v", [jax.ShapeDtypeStruct((nz, 2, 128), f32)])(near)
         near, it = lax.optimization_barrier((near, it))
-        turned = [(k + nz // 6) % nz for k in range(nz)]
+        turned = [(k + nz // 16) % nz for k in range(nz)]
         ring = lax.all_to_all(near, "z", 0, 0, axis_index_groups=[turned])
         post, *spans_out = call(smooth, "vvvvvv", [field, rows(2 * N * N), rows(2 * N * N)], cost=10**9)(
             coef, st, g, rt, kk, it

time: 83.1 us -> 80.6 us (0.970)
  the two profiles are of different devices: /device:TPU:8 before, /device:TPU:1 now
where the time goes in v8:
time: 80.6 us; the launch traced here: 80.3 us
  starting transfers between devices  38.6 us (48%)
  blocking collectives  22.8 us (28%)
  waiting for transfers between devices  11.2 us (14%)
  Pallas kernels  7.51 us (9%)
    all_to_all x1, blocking collectives, per_device(): near = lax.all_to_all(sums, ('y', 'x', 'c'), 0, 0)  22.8 us
    ppermute x4, starting transfers between devices, exchange(): lax.ppermute(block_down, axis, down)  17.8 us
    all_to_all x1, starting transfers between devices, per_device(): ring = lax.all_to_all(near, 'z', 0, 0, axis_index_groups=[turned])  11.9 us
    ppermute x4, starting transfers between devices, exchange(): lax.ppermute(block_up, axis, up)  8.78 us
    all_to_all x1, waiting for transfers between devices, per_device(): ring = lax.all_to_all(near, 'z', 0, 0, axis_index_groups=[turned])  7.35 us
    ppermute x4, waiting for transfers between devices, exchange(): lax.ppermute(block_down, axis, down)  2.82 us
    pallas_call x1, Pallas kernels, per_device(): call(last, 'v' * 9, [field], scratch)(coef, rt, *parts, base, faces, ring)  1.99 us
  transfers between devices with their start and end apart: 9, of which 4 were waited for; matrix products, arithmetic and copies ran while one was open for 0% of the time, Pallas kernels for 4%

profile of v8, /device:TPU:1, one launch (start us, length us, event | category | flops | bytes accessed | tf_op | source)
XLA Modules:
  0.0 80.3 jit_solution(13024664510807254761)
XLA Ops:
  0.0 0.0 copy-start
  0.0 1.2 %shard_map.39 = (f32[136,128]{1,0:T(8,128)S(1)}, f32[136,128]{1,0:T(8,128)S(1)}, f32[72,128]{1,0:T(8,128)S(1)}, f32[72,128]{1,0:T(8,128)S(1)}) custom-call(f32[1024,128]{1,0:T(8,128)} %bitcast.5, f32[2,128]{1,0:T(2,128)} %bitcast.7, f32[8,8]{1,0:T(8,128)} %sv_far.1), custom_call_target="tpu_custom_call" | custom-call | flops 1000000 | bytes 100000 | tf_op jit(solution)/shard_map/pallas_call | solution.py:506
  1.2 0.0 copy-start.2
  1.2 14.2 %collective-permute-start.2 = (f32[72,128]{1,0:T(8,128)S(1)}, f32[72,128]{1,0:T(8,128)S(1)}, u32[]{:S(2)}, u32[]{:S(2)}) collective-permute-start(f32[72,128]{1,0:T(8,128)S(1)} %get-tuple-element.45), channel_id=1, source_target_pairs={{1,0},{2,1},{3,2},{4,3},{5,4},{6,5},{7,6},{0,7},{9,8},{10,9},{11,1... | collective-permute-start | bytes 110600 | tf_op jit(solution)/shard_map/ppermute | solution.py:492
  15.4 0.0 collective-permute-start.3
  15.4 0.0 copy-start.1
  15.4 1.4 %collective-permute-start = (f32[136,128]{1,0:T(8,128)S(1)}, f32[136,128]{1,0:T(8,128)S(1)}, u32[]{:S(2)}, u32[]{:S(2)}) collective-permute-start(f32[136,128]{1,0:T(8,128)S(1)} %get-tuple-element.43), channel_id=1, source_target_pairs={{8,0},{16,8},{24,16},{32,24},{40,32},{48,40},{56,48},{64,56},{72,6... | collective-permute-start | bytes 208904 | tf_op jit(solution)/shard_map/ppermute | solution.py:492
  16.8 4.0 %collective-permute-start.1 = (f32[136,128]{1,0:T(8,128)S(1)}, f32[136,128]{1,0:T(8,128)S(1)}, u32[]{:S(2)}, u32[]{:S(2)}) collective-permute-start(f32[136,128]{1,0:T(8,128)S(1)} %get-tuple-element.44), channel_id=1, source_target_pairs={{0,8},{8,16},{16,24},{24,32},{32,40},{40,48},{48,56},{56,64},{64,7... | collective-permute-start | bytes 208904 | tf_op jit(solution)/shard_map/ppermute | solution.py:492
  20.8 0.0 copy-done
  20.8 0.0 copy-done.2
  20.8 0.0 copy-done.1
  20.8 1.3 %shard_map.37 = (f32[1024,128]{1,0:T(8,128)S(1)}, f32[512,128]{1,0:T(8,128)S(1)}, f32[512,128]{1,0:T(8,128)S(1)}, bf16[128,64]{1,0:T(8,128)(2,1)S(1)}, f32[512,1...) custom-call(f32[1024,128]{1,0:T(8,128)S(1)} %bitcast.6, f32[2,128]{1,0:T(2,128)S(1)} %bitcast.8, ...), custom_call_target="tpu_custom_call" | custom-call | flops 1000000000 | bytes 100000 | tf_op jit(solution)/shard_map/pallas_call | solution.py:520
  22.2 0.0 collective-permute-done.2.from_e.refs_9_
  22.2 0.0 collective-permute-done.3.from_w.refs_10_
  22.2 0.0 collective-permute-done.from_n.refs_7_
  22.2 0.0 collective-permute-done.1.from_s.refs_8_
  22.2 0.2 shard_map.40
  22.5 22.8 %all_to_all.10.parts = f32[32,2,128]{2,1,0:T(2,128)S(1)} all-to-all(f32[32,2,128]{2,1,0:T(2,128)S(1)} %get-tuple-element.47), channel_id=1, replica_groups=mesh['y'=4,'z'=32,'x'=4,'c'=2] {'y','x','c'}, dimensions={0} | all-to-all | bytes 65536 | tf_op jit(solution)/shard_map/all_to_all | solution.py:526
  45.3 0.7 shard_map.41
  46.0 11.9 %all-to-all-start.1 = ((f32[32,2,128]{2,1,0:T(2,128)}), f32[32,2,128]{2,1,0:T(2,128)S(1)}, u32[]{:S(2)}, u32[]{:S(2)}) async-start(f32[32,2,128]{2,1,0:T(2,128)} %shard_map.41), calls=%async_computation.1 | async-start | bytes 65536 | tf_op jit(solution)/shard_map/all_to_all | solution.py:530
  57.9 0.7 shard_map.42
  58.6 1.0 %collective-permute-start.4 = (f32[128,128]{1,0:T(8,128)S(1)}, f32[128,128]{1,0:T(8,128)S(1)}, u32[]{:S(2)}, u32[]{:S(2)}) collective-permute-start(f32[128,128]{1,0:T(8,128)S(1)} %get-tuple-element.51), channel_id=1, source_target_pairs={{1,0},{2,1},{3,2},{4,3},{5,4},{6,5},{7,6},{0,7},{9,8},{10,9},{11,1... | collective-permute-start | bytes 196616 | tf_op jit(solution)/shard_map/ppermute | solution.py:492
  59.5 0.8 collective-permute-start.5
  60.3 2.2 %collective-permute-done.4.got_e.refs_11_ = f32[128,128]{1,0:T(8,128)S(1)} collective-permute-done((f32[128,128]{1,0:T(8,128)S(1)}, f32[128,128]{1,0:T(8,128)S(1)}, u32[]{:S(2)}, u32[]{:S(2)}) %collective-permute-start.4) | collective-permute-done | bytes 65568 | tf_op jit(solution)/shard_map/ppermute | solution.py:492
  62.6 0.0 collective-permute-done.5.got_w.refs_12_
  62.6 0.1 shard_map.43
  62.6 1.3 %collective-permute-start.6 = (f32[280,128]{1,0:T(8,128)S(1)}, f32[280,128]{1,0:T(8,128)S(1)}, u32[]{:S(2)}, u32[]{:S(2)}) collective-permute-start(f32[280,128]{1,0:T(8,128)S(1)} %get-tuple-element.54), channel_id=1, source_target_pairs={{8,0},{16,8},{24,16},{32,24},{40,32},{48,40},{56,48},{64,56},{72,6... | collective-permute-start | bytes 430088 | tf_op jit(solution)/shard_map/ppermute | solution.py:492
  63.9 4.0 %collective-permute-start.7 = (f32[280,128]{1,0:T(8,128)S(1)}, f32[280,128]{1,0:T(8,128)S(1)}, u32[]{:S(2)}, u32[]{:S(2)}) collective-permute-start(f32[280,128]{1,0:T(8,128)S(1)} %get-tuple-element.55), channel_id=1, source_target_pairs={{0,8},{8,16},{16,24},{24,32},{32,40},{40,48},{48,56},{56,64},{64,7... | collective-permute-start | bytes 430088 | tf_op jit(solution)/shard_map/ppermute | solution.py:492
  67.9 0.5 shard_map.38
  68.5 0.6 collective-permute-done.6.refs_13_
  69.0 1.0 %collective-permute-done.7.refs_14_ = f32[280,128]{1,0:T(8,128)S(1)} collective-permute-done((f32[280,128]{1,0:T(8,128)S(1)}, f32[280,128]{1,0:T(8,128)S(1)}, u32[]{:S(2)}, u32[]{:S(2)}) %collective-permute-start.7) | collective-permute-done | bytes 143392 | tf_op jit(solution)/shard_map/ppermute | solution.py:492
  70.1 0.9 %shard_map.44 = (f32[1024,128]{1,0:T(8,128)S(1)}, f32[16,128]{1,0:T(8,128)S(1)}) custom-call(f32[2,128]{1,0:T(2,128)S(1)} %bitcast.12, f32[512,128]{1,0:T(8,128)S(1)} %get-tuple-element.35.st.refs_1_, f32[1024,128]{1,0:T(8,128)S(1)} %get-tuple-element.40.g.refs_2_, f32[512,128]{1,0:T(8,128)S(1)} %get-tuple-element.32.rt.refs_3_.refs_1_, ...), custom_call_target="tpu_custom_call" | custom-call | flops 1000000 | bytes 100000 | tf_op jit(solution)/shard_map/pallas_call | solution.py:548
  70.9 7.3 %all-to-all-done.1.refs_8_ = f32[32,2,128]{2,1,0:T(2,128)S(1)} async-done(((f32[32,2,128]{2,1,0:T(2,128)}), f32[32,2,128]{2,1,0:T(2,128)S(1)}, u32[]{:S(2)}, u32[]{:S(2)}) %all-to-all-start.1) | async-done | bytes 32800 | tf_op jit(solution)/shard_map/all_to_all | solution.py:530
  78.3 2.0 %shard_map.45 = f32[1024,128]{1,0:T(8,128)} custom-call(f32[2,128]{1,0:T(2,128)S(1)} %bitcast.13, f32[512,128]{1,0:T(8,128)S(1)} %get-tuple-element.32.rt.refs_3_.refs_1_, f32[512,128]{1,0:T(8,128)S(1)} %get-tuple-element.36.refs_2_, f32[512,128]{1,0:T(8,128)S(1)} %get-tuple-element.37.refs_3_, f32[512,128]{1,0:T(8,128)S(1)} %get-tuple-element.38.refs_4_, ...), custom_call_target="tpu_custom_call" | custom-call | flops 1000000 | bytes 100000 | tf_op jit(solution)/shard_map/pallas_call | solution.py:551
Async XLA Ops:
  0.0 20.8 %copy-start = (f32[8,8,8,1,2,128]{5,4,3,2,1,0:T(2,128)S(1)}, f32[8,8,8,1,2,128]{5,4,3,2,1,0:T(2,128)}, u32[]{:S(2)}) copy-start(f32[8,8,8,1,2,128]{5,4,3,2,1,0:T(2,128)} %param.3) | copy-start | bytes 1572868
  1.2 19.6 %copy-start.2 = (f32[8,8]{1,0:T(8,128)S(1)}, f32[8,8]{1,0:T(8,128)}, u32[]{:S(2)}) copy-start(f32[8,8]{1,0:T(8,128)} %sv_far.1) | copy-start | bytes 772
  1.2 21.0 %collective-permute-start.2 = (f32[72,128]{1,0:T(8,128)S(1)}, f32[72,128]{1,0:T(8,128)S(1)}, u32[]{:S(2)}, u32[]{:S(2)}) collective-permute-start(f32[72,128]{1,0:T(8,128)S(1)} %get-tuple-element.45), channel_id=1, source_target_pairs={{1,0},{2,1},{3,2},{4,3},{5,4},{6,5},{7,6},{0,7},{9,8},{10,9},{11,1... | collective-permute-start | bytes 110600 | tf_op jit(solution)/shard_map/ppermute | solution.py:492
  15.4 6.8 %collective-permute-start.3 = (f32[72,128]{1,0:T(8,128)S(1)}, f32[72,128]{1,0:T(8,128)S(1)}, u32[]{:S(2)}, u32[]{:S(2)}) collective-permute-start(f32[72,128]{1,0:T(8,128)S(1)} %get-tuple-element.46), channel_id=1, source_target_pairs={{0,1},{1,2},{2,3},{3,4},{4,5},{5,6},{6,7},{7,0},{8,9},{9,10},{10,1... | collective-permute-start | bytes 110600 | tf_op jit(solution)/shard_map/ppermute | solution.py:492
  15.4 5.4 %copy-start.1 = (f32[1,2,128]{2,1,0:T(2,128)S(1)}, f32[1,2,128]{2,1,0:T(2,128)}, u32[]{:S(2)}) copy-start(f32[1,2,128]{2,1,0:T(2,128)} %param.4) | copy-start | bytes 3076
  15.4 6.8 %collective-permute-start = (f32[136,128]{1,0:T(8,128)S(1)}, f32[136,128]{1,0:T(8,128)S(1)}, u32[]{:S(2)}, u32[]{:S(2)}) collective-permute-start(f32[136,128]{1,0:T(8,128)S(1)} %get-tuple-element.43), channel_id=1, source_target_pairs={{8,0},{16,8},{24,16},{32,24},{40,32},{48,40},{56,48},{64,56},{72,6... | collective-permute-start | bytes 208904 | tf_op jit(solution)/shard_map/ppermute | solution.py:492
  16.8 5.4 %collective-permute-start.1 = (f32[136,128]{1,0:T(8,128)S(1)}, f32[136,128]{1,0:T(8,128)S(1)}, u32[]{:S(2)}, u32[]{:S(2)}) collective-permute-start(f32[136,128]{1,0:T(8,128)S(1)} %get-tuple-element.44), channel_id=1, source_target_pairs={{0,8},{8,16},{16,24},{24,32},{32,40},{40,48},{48,56},{56,64},{64,7... | collective-permute-start | bytes 208904 | tf_op jit(solution)/shard_map/ppermute | solution.py:492
  46.0 32.3 %all-to-all-start.1 = ((f32[32,2,128]{2,1,0:T(2,128)}), f32[32,2,128]{2,1,0:T(2,128)S(1)}, u32[]{:S(2)}, u32[]{:S(2)}) async-start(f32[32,2,128]{2,1,0:T(2,128)} %shard_map.41), calls=%async_computation.1 | async-start | bytes 65536 | tf_op jit(solution)/shard_map/all_to_all | solution.py:530
  58.6 4.0 %collective-permute-start.4 = (f32[128,128]{1,0:T(8,128)S(1)}, f32[128,128]{1,0:T(8,128)S(1)}, u32[]{:S(2)}, u32[]{:S(2)}) collective-permute-start(f32[128,128]{1,0:T(8,128)S(1)} %get-tuple-element.51), channel_id=1, source_target_pairs={{1,0},{2,1},{3,2},{4,3},{5,4},{6,5},{7,6},{0,7},{9,8},{10,9},{11,1... | collective-permute-start | bytes 196616 | tf_op jit(solution)/shard_map/ppermute | solution.py:492
  59.5 3.0 %collective-permute-start.5 = (f32[128,128]{1,0:T(8,128)S(1)}, f32[128,128]{1,0:T(8,128)S(1)}, u32[]{:S(2)}, u32[]{:S(2)}) collective-permute-start(f32[128,128]{1,0:T(8,128)S(1)} %get-tuple-element.52), channel_id=1, source_target_pairs={{0,1},{1,2},{2,3},{3,4},{4,5},{5,6},{6,7},{7,0},{8,9},{9,10},{10,1... | collective-permute-start | bytes 196616 | tf_op jit(solution)/shard_map/ppermute | solution.py:492
  62.6 6.4 %collective-permute-start.6 = (f32[280,128]{1,0:T(8,128)S(1)}, f32[280,128]{1,0:T(8,128)S(1)}, u32[]{:S(2)}, u32[]{:S(2)}) collective-permute-start(f32[280,128]{1,0:T(8,128)S(1)} %get-tuple-element.54), channel_id=1, source_target_pairs={{8,0},{16,8},{24,16},{32,24},{40,32},{48,40},{56,48},{64,56},{72,6... | collective-permute-start | bytes 430088 | tf_op jit(solution)/shard_map/ppermute | solution.py:492
  63.9 6.1 %collective-permute-start.7 = (f32[280,128]{1,0:T(8,128)S(1)}, f32[280,128]{1,0:T(8,128)S(1)}, u32[]{:S(2)}, u32[]{:S(2)}) collective-permute-start(f32[280,128]{1,0:T(8,128)S(1)} %get-tuple-element.55), channel_id=1, source_target_pairs={{0,8},{8,16},{16,24},{24,32},{32,40},{40,48},{48,56},{56,64},{64,7... | collective-permute-start | bytes 430088 | tf_op jit(solution)/shard_map/ppermute | solution.py:492
